TPU v7x, 32 devices: a whole 2x2x4 slice. The times are simulated.
32 devices in a mesh: dp: 8 (over y, x, core), tensor: 4 (over z).
Axes of the slice: x: 2, y: 2, z: 4, core: 2. Of those that a mesh axis runs over, the one named last changes fastest.
Arguments:
- tokens: bfloat16 [8, 1024, 2048], P('dp', 'tensor'), may hold values from -6 to 6
- segments: int32 [8, 1024], P('dp'), may hold values from 0 to 7, never falling along the last dimension, each value on 1 to 512 neighbouring positions
- valid: int32 [8, 1024], P('dp'), may hold values 0 or 1
- routes: int32 [8, 1024, 8], P('dp'), may hold values from 0 to 15, all different within a row; in each aligned block of 1024 rows (0 to 1023, 1024 to 2047, ..., all dimensions but the last counted through in order) at most 544 rows name the same one
- cotangent: bfloat16 [8, 1024, 2048], P('dp', 'tensor'), may hold values from -6 to 6
- query_weight: bfloat16 [2048, 2048], P('dp', 'tensor'), may hold values from -0.125 to 0.125
- key_weight: bfloat16 [2048, 2048], P('dp', 'tensor'), may hold values from -0.125 to 0.125
- value_weight: bfloat16 [2048, 2048], P('dp', 'tensor'), may hold values from -0.125 to 0.125
- output_weight: bfloat16 [2048, 2048], P('dp', 'tensor'), may hold values from -0.75 to 0.75
- attn_norm_gain: bfloat16 [2048], replicated, may hold values from 0.25 to 1.75
- expert_norm_gain: bfloat16 [2048], replicated, may hold values from 0.25 to 1.75
- query_norm_gain: bfloat16 [2048], replicated, may hold values from 0.25 to 1.75
- key_norm_gain: bfloat16 [2048], replicated, may hold values from 0.25 to 1.75
- router_weight: bfloat16 [2048, 16], replicated, may hold values from -0.0625 to 0.0625
- gate_weight: bfloat16 [16, 2048, 1024], P(None, 'dp', 'tensor'), may hold values from -0.125 to 0.125
- up_weight: bfloat16 [16, 2048, 1024], P(None, 'dp', 'tensor'), may hold values from -0.125 to 0.125
- down_weight: bfloat16 [16, 2048, 1024], P(None, 'dp', 'tensor'), may hold values from -1.5 to 1.5
Outputs:
- layer_out: bfloat16 [8, 1024, 2048], P('dp', 'tensor')
- grad_tokens: float32 [8, 1024, 2048], P('dp', 'tensor')
- grad_query: float32 [2048, 2048], P('dp', 'tensor')
- grad_key: float32 [2048, 2048], P('dp', 'tensor')
- grad_value: float32 [2048, 2048], P('dp', 'tensor')
- grad_output: float32 [2048, 2048], P('dp', 'tensor')
- grad_gate: float32 [16, 2048, 1024], P(None, 'dp', 'tensor')
- grad_up: float32 [16, 2048, 1024], P(None, 'dp', 'tensor')
- grad_down: float32 [16, 2048, 1024], P(None, 'dp', 'tensor')
- grad_router: float32 [2048, 16], replicated
- grad_attn_norm: float32 [2048], replicated
- grad_expert_norm: float32 [2048], replicated
- grad_query_norm: float32 [2048], replicated
- grad_key_norm: float32 [2048], replicated
Inputs may be any that keep to these rules, and one draw needn't show every extreme that they name: `routes`: each row names 8 different experts; within one sequence no expert is named by more than 544 rows, and in every draw some expert of some sequence is named by exactly 544 rows. `segments`: document numbers never fall along a sequence; each document has 1 to 512 tokens and one has exactly 512.
All inputs are finite; a program needn't handle non-finite values. No bound on the sum of `valid` on one device may be relied on, other than what follows from the above.
Results may differ from a plain program's by a relative error of at most 0.015.
Values may be sent and summed in bfloat16 or wider, within the bound.
No kernel may reach another device: no remote copies, remote signals or barrier semaphores. Data moves between devices by JAX's collectives and lax.ppermute only.
A program may use at most 640 MiB of HBM per device.

v0:
```python
import jax
import jax.numpy as jnp
from jax import lax
from jax.sharding import PartitionSpec as P

HEAD = 128
TOP = 8
EXPERTS = 16
CAP = 544


EPS = 1e-05
THETA = 10000.0
MASKED = -1e30
PRECISE = lax.Precision.HIGHEST


def rows_norm(values, gain):
    scale = lax.rsqrt(jnp.mean(values * values, axis=-1, keepdims=True) + EPS)
    normed = values * scale
    return (normed * gain, normed, scale)


def norm_back(grad_out, gain, normed, scale):
    grad_normed = grad_out * gain
    inner_mean = jnp.mean(grad_normed * normed, axis=-1, keepdims=True)
    return (scale * (grad_normed - normed * inner_mean), jnp.sum(grad_out * normed, axis=0))


def rotary_tables(length, width):
    half = width // 2
    freq = THETA ** (-(jnp.arange(half, dtype=jnp.float32) * 2.0) / width)
    angle = jnp.arange(length, dtype=jnp.float32)[:, None] * freq[None, :]
    return (jnp.cos(angle)[:, None, :], jnp.sin(angle)[:, None, :])


def rotate(values, cosine, sine_table):
    half = values.shape[-1] // 2
    first = values[..., :half]
    second = values[..., half:]
    return jnp.concatenate(
        [first * cosine - second * sine_table, second * cosine + first * sine_table], axis=-1
    )


def rotate_back(grads, cosine, sine_table):
    half = grads.shape[-1] // 2
    first = grads[..., :half]
    second = grads[..., half:]
    return jnp.concatenate(
        [first * cosine + second * sine_table, second * cosine - first * sine_table], axis=-1
    )


def allowed_rows(segment, usable, first_row, block_rows):
    query_pos = first_row + jnp.arange(block_rows, dtype=jnp.int32)
    key_pos = jnp.arange(segment.shape[0], dtype=jnp.int32)
    segment_rows = lax.dynamic_slice_in_dim(segment, first_row, block_rows)
    same = segment_rows[:, None] == segment[None, :]
    causal = key_pos[None, :] <= query_pos[:, None]
    live = (usable[None, :] == 1) | (key_pos[None, :] == query_pos[:, None])
    return same & causal & live


def dispatch(route):
    length = route.shape[0]
    flat = route.reshape(-1)
    onehot = (flat[:, None] == jnp.arange(EXPERTS, dtype=jnp.int32)[None, :]).astype(jnp.int32)
    before = jnp.cumsum(onehot, axis=0) - onehot
    rank = jnp.sum(before * onehot, axis=1)
    slot = flat * CAP + rank
    owner = jnp.arange(length * TOP, dtype=jnp.int32) // TOP
    slot_token = jnp.zeros((EXPERTS * CAP,), jnp.int32).at[slot].set(owner)
    slot_used = jnp.zeros((EXPERTS * CAP,), jnp.int32).at[slot].set(1)
    return (
        slot_token.reshape(EXPERTS, CAP),
        slot_used.reshape(EXPERTS, CAP),
        slot.reshape(length, TOP),
    )


def combine_slots(stacked, slot_of):
    flat_rows = stacked.reshape(-1, stacked.shape[-1])
    total = flat_rows[slot_of[:, 0]]
    for column in range(1, slot_of.shape[1]):
        total = total + flat_rows[slot_of[:, column]]
    return total


def on_device(
    tokens,
    segments,
    valid,
    routes,
    cotangent,
    query_weight,
    key_weight,
    value_weight,
    output_weight,
    attn_norm_gain,
    expert_norm_gain,
    query_norm_gain,
    key_norm_gain,
    router_weight,
    gate_weight,
    up_weight,
    down_weight,
):
    f32 = jnp.float32
    bf16 = jnp.bfloat16
    local_x = tokens[0].astype(f32)
    rows_here = local_x.shape[0]
    model_width = local_x.shape[1]
    seg_all = segments[0]
    valid_all = valid[0]
    route_all = routes[0]
    length = seg_all.shape[0]
    row_offset = lax.axis_index("tensor") * rows_here
    scale = HEAD ** (-0.5)
    gathered = (
        lax.all_gather(query_weight, "dp", axis=0, tiled=True),
        lax.all_gather(key_weight, "dp", axis=0, tiled=True),
        lax.all_gather(value_weight, "dp", axis=0, tiled=True),
        lax.all_gather(output_weight, "dp", axis=0, tiled=True),
        lax.all_gather(gate_weight, "dp", axis=1, tiled=True),
        lax.all_gather(up_weight, "dp", axis=1, tiled=True),
        lax.all_gather(down_weight, "dp", axis=1, tiled=True),
    )
    query_w, key_w, value_w, output_w, gate_all, up_all, down_all = gathered
    local_cols = query_w.shape[1]
    heads_here = local_cols // HEAD
    head_offset = lax.axis_index("tensor") * local_cols
    gain_attn = attn_norm_gain.astype(f32)
    gain_expert = expert_norm_gain.astype(f32)
    gain_query = lax.dynamic_slice_in_dim(query_norm_gain.astype(f32), head_offset, local_cols)
    gain_key = lax.dynamic_slice_in_dim(key_norm_gain.astype(f32), head_offset, local_cols)
    normed1, unit1, scale1 = rows_norm(local_x, gain_attn)
    normed1_low = normed1.astype(bf16)
    normed1_full = lax.all_gather(normed1_low, "tensor", axis=0, tiled=True)
    query_raw = jnp.dot(normed1_full, query_w, preferred_element_type=f32)
    key_raw = jnp.dot(normed1_full, key_w, preferred_element_type=f32)
    value_heads = (
        jnp.dot(normed1_full, value_w, preferred_element_type=f32)
        .astype(bf16)
        .reshape(length, heads_here, HEAD)
    )
    squares = lax.psum(
        (jnp.sum(query_raw * query_raw, axis=1), jnp.sum(key_raw * key_raw, axis=1)), "tensor"
    )
    query_scale = lax.rsqrt(squares[0] / model_width + EPS)[:, None]
    key_scale = lax.rsqrt(squares[1] / model_width + EPS)[:, None]
    query_unit = query_raw * query_scale
    key_unit = key_raw * key_scale
    cosine, sine_table = rotary_tables(length, HEAD)
    query_rot = rotate(
        (query_unit * gain_query).reshape(length, heads_here, HEAD), cosine, sine_table
    ).astype(bf16)
    key_rot = rotate(
        (key_unit * gain_key).reshape(length, heads_here, HEAD), cosine, sine_table
    ).astype(bf16)
    block_rows = min(512, length)
    starts = jnp.arange(length // block_rows, dtype=jnp.int32) * block_rows

    def attend(first_row):
        query_rows = lax.dynamic_slice_in_dim(query_rot, first_row, block_rows, 0)
        allowed = allowed_rows(seg_all, valid_all, first_row, block_rows)
        scores = jnp.einsum("qhd,khd->hqk", query_rows, key_rot, preferred_element_type=f32) * scale
        scores = jnp.where(allowed[None], scores, MASKED)
        row_max = jnp.max(scores, axis=-1, keepdims=True)
        row_exp = jnp.exp(scores - row_max)
        row_sum = jnp.sum(row_exp, axis=-1, keepdims=True)
        weights_low = (row_exp / row_sum).astype(bf16)
        mixed_rows = jnp.einsum(
            "hqk,khd->qhd", weights_low, value_heads, preferred_element_type=f32
        ).astype(bf16)
        return (mixed_rows, (row_max + jnp.log(row_sum))[..., 0])

    mixed_blocks, lse_blocks = lax.map(attend, starts)
    mixed_heads = mixed_blocks.reshape(length, local_cols)
    attn_local = lax.psum_scatter(
        lax.dot_general(
            mixed_heads, output_w, (((1,), (1,)), ((), ())), preferred_element_type=f32
        ),
        "tensor",
        scatter_dimension=0,
        tiled=True,
    )
    resid = local_x + attn_local
    normed2, unit2, scale2 = rows_norm(resid, gain_expert)
    normed2_low = normed2.astype(bf16)
    normed2_full = lax.all_gather(normed2_low, "tensor", axis=0, tiled=True)
    router_f = router_weight.astype(f32)
    logits = jnp.dot(normed2_full, router_weight, preferred_element_type=f32)
    route_probs = jax.nn.softmax(logits, axis=-1)
    slot_token, slot_used, slot_of = dispatch(route_all)
    expert_ids = jnp.arange(EXPERTS, dtype=jnp.int32)[:, None]
    used_float = slot_used.astype(f32)
    gate_slot = route_probs[slot_token, expert_ids] * used_float

    def expert_step(carried, pieces):
        gate_e, up_e, down_e, tokens_e, weight_e = pieces
        rows_in = normed2_full[tokens_e]
        gate_pre = jnp.dot(rows_in, gate_e, preferred_element_type=f32)
        up_pre = jnp.dot(rows_in, up_e, preferred_element_type=f32)
        hidden_low = (jax.nn.silu(gate_pre) * up_pre).astype(bf16)
        expert_out = lax.dot_general(
            hidden_low, down_e, (((1,), (1,)), ((), ())), preferred_element_type=f32
        )
        return (carried, (expert_out * weight_e[:, None], gate_pre, up_pre))

    _, (weighted_outs, gate_kept, up_kept) = lax.scan(
        expert_step, jnp.zeros((), f32), (gate_all, up_all, down_all, slot_token, gate_slot)
    )
    moe_partial = combine_slots(weighted_outs, slot_of)
    moe_local = lax.psum_scatter(
        moe_partial.astype(jnp.bfloat16), "tensor", scatter_dimension=0, tiled=True
    ).astype(jnp.float32)
    layer_local = (resid + moe_local).astype(bf16)
    valid_here = lax.dynamic_slice_in_dim(valid_all, row_offset, rows_here).astype(f32)
    grad_final = cotangent[0].astype(f32) * valid_here[:, None]
    final_full = lax.all_gather(grad_final.astype(bf16), "tensor", axis=0, tiled=True)

    def expert_back(carried, pieces):
        gate_e, up_e, down_e, tokens_e, weight_e, gate_pre, up_pre = pieces
        rows_in = normed2_full[tokens_e]
        upstream = final_full[tokens_e]
        sig_gate = jax.nn.sigmoid(gate_pre)
        activated = gate_pre * sig_gate
        hidden_low = (activated * up_pre).astype(bf16)
        projected = jnp.dot(upstream, down_e, preferred_element_type=f32)
        grad_weight = jnp.sum(hidden_low.astype(f32) * projected, axis=1)
        grad_eo = (upstream.astype(f32) * weight_e[:, None]).astype(bf16)
        grad_hidden = jnp.dot(grad_eo, down_e, preferred_element_type=f32)
        grad_down_e = lax.dot_general(
            grad_eo, hidden_low, (((0,), (0,)), ((), ())), preferred_element_type=f32
        )
        grad_gpre = (grad_hidden * up_pre * sig_gate * (1.0 + gate_pre * (1.0 - sig_gate))).astype(
            bf16
        )
        grad_upre = (grad_hidden * activated).astype(bf16)
        grad_gate_e = lax.dot_general(
            rows_in, grad_gpre, (((0,), (0,)), ((), ())), preferred_element_type=f32
        )
        grad_up_e = lax.dot_general(
            rows_in, grad_upre, (((0,), (0,)), ((), ())), preferred_element_type=f32
        )
        grad_rows = lax.dot_general(
            grad_gpre, gate_e, (((1,), (1,)), ((), ())), preferred_element_type=f32
        )
        grad_rows = grad_rows + lax.dot_general(
            grad_upre, up_e, (((1,), (1,)), ((), ())), preferred_element_type=f32
        )
        return (carried, (grad_gate_e, grad_up_e, grad_down_e, grad_weight, grad_rows))

    _, (grad_gate_all, grad_up_all, grad_down_all, grad_weight_slot, grad_rows_all) = lax.scan(
        expert_back,
        jnp.zeros((), f32),
        (gate_all, up_all, down_all, slot_token, gate_slot, gate_kept, up_kept),
    )
    normed2_grad_part = combine_slots(grad_rows_all, slot_of)
    picked = grad_weight_slot.reshape(-1)[slot_of]
    route_match = (
        route_all[:, :, None] == jnp.arange(EXPERTS, dtype=jnp.int32)[None, None, :]
    ).astype(f32)
    prob_grad_part = jnp.sum(route_match * picked[:, :, None], axis=1)
    normed2_grad, prob_grad = (
        lax.psum_scatter(normed2_grad_part, "tensor", scatter_dimension=0, tiled=True),
        lax.psum_scatter(prob_grad_part, "tensor", scatter_dimension=0, tiled=True),
    )
    probs_here = lax.dynamic_slice_in_dim(route_probs, row_offset, rows_here, 0)
    grad_logits = probs_here * (prob_grad - jnp.sum(probs_here * prob_grad, axis=1, keepdims=True))
    normed2_grad = normed2_grad + jnp.dot(
        grad_logits, router_f.T, precision=PRECISE, preferred_element_type=f32
    )
    grad_router_part = lax.dot_general(
        normed2_low.astype(f32),
        grad_logits,
        (((0,), (0,)), ((), ())),
        precision=PRECISE,
        preferred_element_type=f32,
    )
    resid_norm_grad, grad_expert_part = norm_back(normed2_grad, gain_expert, unit2, scale2)
    grad_resid = grad_final + resid_norm_grad
    resid_full = lax.all_gather(grad_resid.astype(bf16), "tensor", axis=0, tiled=True)
    grad_output_part = lax.dot_general(
        resid_full, mixed_heads, (((0,), (0,)), ((), ())), preferred_element_type=f32
    )
    grad_mixed = (
        jnp.dot(resid_full, output_w, preferred_element_type=f32)
        .astype(bf16)
        .reshape(length, heads_here, HEAD)
    )

    def attend_back(carried, pieces):
        key_grad, value_grad = carried
        first_row, lse_rows = pieces
        query_rows = lax.dynamic_slice_in_dim(query_rot, first_row, block_rows, 0)
        mixed_grad_rows = lax.dynamic_slice_in_dim(grad_mixed, first_row, block_rows, 0)
        allowed = allowed_rows(seg_all, valid_all, first_row, block_rows)
        scores = jnp.einsum("qhd,khd->hqk", query_rows, key_rot, preferred_element_type=f32) * scale
        scores = jnp.where(allowed[None], scores, MASKED)
        weights_full = jnp.exp(scores - lse_rows[:, :, None])
        weights_low = weights_full.astype(bf16)
        value_grad = value_grad + jnp.einsum(
            "hqk,qhd->khd", weights_low, mixed_grad_rows, preferred_element_type=f32
        )
        weight_grad = jnp.einsum(
            "qhd,khd->hqk", mixed_grad_rows, value_heads, preferred_element_type=f32
        )
        row_dot = jnp.sum(weights_full * weight_grad, axis=-1, keepdims=True)
        score_grad = (weights_full * (weight_grad - row_dot)).astype(bf16)
        query_grad = (
            jnp.einsum("hqk,khd->qhd", score_grad, key_rot, preferred_element_type=f32) * scale
        )
        key_grad = (
            key_grad
            + jnp.einsum("hqk,qhd->khd", score_grad, query_rows, preferred_element_type=f32) * scale
        )
        return ((key_grad, value_grad), query_grad)

    zero_heads = jnp.zeros((length, heads_here, HEAD), f32)
    (key_rot_grad, value_grad), query_blocks = lax.scan(
        attend_back, (zero_heads, zero_heads), (starts, lse_blocks)
    )
    query_rot_grad = query_blocks.reshape(length, heads_here, HEAD)
    query_unit_grad = rotate_back(query_rot_grad, cosine, sine_table).reshape(length, local_cols)
    key_unit_grad = rotate_back(key_rot_grad, cosine, sine_table).reshape(length, local_cols)
    query_gained = query_unit_grad * gain_query
    key_gained = key_unit_grad * gain_key
    inner_sums = lax.psum(
        (jnp.sum(query_unit * query_gained, axis=1), jnp.sum(key_unit * key_gained, axis=1)),
        "tensor",
    )
    query_raw_low = (
        query_scale * (query_gained - query_unit * (inner_sums[0] / model_width)[:, None])
    ).astype(bf16)
    key_raw_low = (
        key_scale * (key_gained - key_unit * (inner_sums[1] / model_width)[:, None])
    ).astype(bf16)
    value_low = value_grad.reshape(length, local_cols).astype(bf16)
    grad_qgain_here = jnp.sum(query_unit_grad * query_unit, axis=0)
    grad_kgain_here = jnp.sum(key_unit_grad * key_unit, axis=0)
    grad_query_part = lax.dot_general(
        normed1_full, query_raw_low, (((0,), (0,)), ((), ())), preferred_element_type=f32
    )
    grad_key_part = lax.dot_general(
        normed1_full, key_raw_low, (((0,), (0,)), ((), ())), preferred_element_type=f32
    )
    grad_value_part = lax.dot_general(
        normed1_full, value_low, (((0,), (0,)), ((), ())), preferred_element_type=f32
    )
    total_rows = lax.dot_general(
        query_raw_low, query_w, (((1,), (1,)), ((), ())), preferred_element_type=f32
    )
    total_rows = total_rows + lax.dot_general(
        key_raw_low, key_w, (((1,), (1,)), ((), ())), preferred_element_type=f32
    )
    total_rows = total_rows + lax.dot_general(
        value_low, value_w, (((1,), (1,)), ((), ())), preferred_element_type=f32
    )
    normed1_grad = lax.psum_scatter(total_rows, "tensor", scatter_dimension=0, tiled=True)
    input_norm_grad, grad_attn_part = norm_back(normed1_grad, gain_attn, unit1, scale1)
    grad_input = grad_resid + input_norm_grad
    reduced = (
        lax.psum_scatter(grad_query_part, "dp", scatter_dimension=0, tiled=True),
        lax.psum_scatter(grad_key_part, "dp", scatter_dimension=0, tiled=True),
        lax.psum_scatter(grad_value_part, "dp", scatter_dimension=0, tiled=True),
        lax.psum_scatter(grad_output_part, "dp", scatter_dimension=0, tiled=True),
        lax.psum_scatter(grad_gate_all, "dp", scatter_dimension=1, tiled=True),
        lax.psum_scatter(grad_up_all, "dp", scatter_dimension=1, tiled=True),
        lax.psum_scatter(grad_down_all, "dp", scatter_dimension=1, tiled=True),
    )
    zeros_width = jnp.zeros((model_width,), f32)
    qgain_full = lax.dynamic_update_slice(zeros_width, grad_qgain_here, (head_offset,))
    kgain_full = lax.dynamic_update_slice(zeros_width, grad_kgain_here, (head_offset,))
    summed = lax.psum(
        (grad_attn_part, grad_expert_part, qgain_full, kgain_full, grad_router_part),
        ("dp", "tensor"),
    )
    return (
        layer_local[None],
        grad_input[None],
        reduced[0],
        reduced[1],
        reduced[2],
        reduced[3],
        reduced[4],
        reduced[5],
        reduced[6],
        summed[4],
        summed[0],
        summed[1],
        summed[2],
        summed[3],
    )


def solution(mesh):
    in_specs = (
        P("dp", "tensor", None),
        P("dp", None),
        P("dp", None),
        P("dp", None, None),
        P("dp", "tensor", None),
        P("dp", "tensor"),
        P("dp", "tensor"),
        P("dp", "tensor"),
        P("dp", "tensor"),
        P(),
        P(),
        P(),
        P(),
        P(),
        P(None, "dp", "tensor"),
        P(None, "dp", "tensor"),
        P(None, "dp", "tensor"),
    )
    out_specs = (
        P("dp", "tensor", None),
        P("dp", "tensor", None),
        P("dp", "tensor"),
        P("dp", "tensor"),
        P("dp", "tensor"),
        P("dp", "tensor"),
        P(None, "dp", "tensor"),
        P(None, "dp", "tensor"),
        P(None, "dp", "tensor"),
        P(),
        P(),
        P(),
        P(),
        P(),
    )
    return jax.shard_map(
        on_device, mesh=mesh, in_specs=in_specs, out_specs=out_specs, check_vma=False
    )
```

profile of v0, /device:TPU:0, one launch (start us, length us, event | category | flops | bytes accessed | tf_op | source)
XLA Modules:
  0.0 3603.2 jit_solution(5977385934253071369)
XLA Ops:
  40.6 82.9 %all-gather.12.cloned.1.call-done = bf16[1024,2048]{1,0:T(8,128)(2,1)} async-done(((bf16[256,2048]{1,0:T(8,128)(2,1)}), bf16[1024,2048]{1,0:T(8,128)(2,1)}) %all-gather.12.cloned.1.call-update) | async-done | bytes 4194320 | tf_op jit(solution)/shard_map/all_gather | solution.py:139
  230.4 143.8 %reduce-scatter.13.cloned.1.call-done = f32[256,2048]{1,0:T(8,128)} async-done(((f32[1024,2048]{1,0:T(8,128)}), f32[256,2048]{1,0:T(8,128)}) %reduce-scatter.13.cloned.1.call-update) | async-done | bytes 2097168 | tf_op jit(solution)/shard_map/reduce_scatter | solution.py:180
  389.9 30.5 scatter_custom_fusion
  421.4 30.5 scatter_custom_fusion.1
  463.9 69.6 %gather_fusion.3 = f32[8704]{0:T(1024)S(1)} fusion(f32[1024,16]{0,1:T(8,128)S(1)} %fusion.120, s32[8704]{0:T(1024)S(1)} %reshape.582), kind=kCustom, calls=%fused_computation.3 | custom fusion | bytes 139264 | tf_op jit(solution)/shard_map/gather | solution.py:198
  550.7 91.8 %all-gather.26.cloned.1.call-done = bf16[16,2048,256]{2,1,0:T(8,128)(2,1)} async-done(((bf16[16,256,256]{2,1,0:T(8,128)(2,1)}), bf16[16,2048,256]{2,1,0:T(8,128)(2,1)}) %all-gather.26.cloned.1.call-update) | async-done | bytes 16777232 | tf_op jit(solution)/shard_map/all_gather | solution.py:126
  642.5 91.6 %all-gather.28.cloned.1.call-done = bf16[16,2048,256]{2,1,0:T(8,128)(2,1)} async-done(((bf16[16,256,256]{2,1,0:T(8,128)(2,1)}), bf16[16,2048,256]{2,1,0:T(8,128)(2,1)}) %all-gather.28.cloned.1.call-update) | async-done | bytes 16777232 | tf_op jit(solution)/shard_map/all_gather | solution.py:127
  757.4 300.9 %while.60 = (s32[]{:T(128)}, f32[16,544,2048]{2,1,0:T(8,128)}, f32[16,544,256]{2,1,0:T(8,128)}, f32[16,544,256]{2,1,0:T(8,128)}, s32[16,544]{1,0:T(8,128)S(1)}, ...) while((s32[]{:T(128)}, f32[16,544,2048]{2,1,0:T(8,128)}, ...), condition=%wide.region_19.20_spmd, body=%wide.region_18.19_spmd.sunk | while | flops 1713228416 | bytes 19879924 | solution.py:211
  1081.0 617.3 %while.61 = (s32[]{:T(128)}, f32[16,2048,256]{2,1,0:T(8,128)}, f32[16,2048,256]{2,1,0:T(8,128)}, f32[16,2048,256]{2,1,0:T(8,128)}, f32[16,544]{1,0:T(8,128)S(1)}...) while((s32[]{:T(128)}, f32[16,2048,256]{2,1,0:T(8,128)}, ...), condition=%wide.region_23.24_spmd, body=%wide.region_21.23_spmd.sunk | while | flops 4003284992 | bytes 56482244 | solution.py:255
  1698.4 45.8 %gather_fusion.20 = f32[8192]{0:T(1024)S(1)} fusion(f32[8704]{0:T(1024)S(1)} %reshape.551, s32[8192]{0:T(1024)S(1)} %copy-done.23), kind=kCustom, calls=%fused_computation.20 | custom fusion | bytes 98304 | tf_op jit(solution)/shard_map/gather | solution.py:261
  1947.5 27.3 add_add_fusion.1
  2209.0 70.7 %reduce-scatter.15.cloned.1.call-done = bf16[256,2048]{1,0:T(8,128)(2,1)} async-done(((bf16[1024,2048]{1,0:T(8,128)(2,1)}), bf16[256,2048]{1,0:T(8,128)(2,1)}) %reduce-scatter.15.cloned.1.call-update) | async-done | bytes 1048592 | tf_op jit(solution)/shard_map/reduce_scatter | solution.py:215
  2284.6 81.3 %all-gather.32.cloned.1.call-done = bf16[1024,2048]{1,0:T(8,128)(2,1)} async-done(((bf16[256,2048]{1,0:T(8,128)(2,1)}), bf16[1024,2048]{1,0:T(8,128)(2,1)}) %all-gather.32.cloned.1.call-update) | async-done | bytes 4194320 | tf_op jit(solution)/shard_map/all_gather | solution.py:284
  2372.2 51.5 %while.62 = (s32[]{:T(128)}, f32[1024,4,128]{0,2,1:T(8,128)S(1)}, f32[1024,4,128]{0,2,1:T(8,128)}, f32[2,512,4,128]{3,1,0,2:T(8,128)}, s32[2]{0:T(128)S(1)}, /*i...) while((s32[]{:T(128)}, f32[1024,4,128]{0,2,1:T(8,128)S(1)}, ...), condition=%wide.region_31.32_spmd.clone, body=%wide.region_29.31_spmd.clone.sunk | while | flops 2721840640 | bytes 180433904 | solution.py:322
  2506.3 109.9 %reduce-scatter.21.cloned.1.call-done = f32[256,2048]{1,0:T(8,128)} async-done(((f32[1024,2048]{1,0:T(8,128)}), f32[256,2048]{1,0:T(8,128)}) %reduce-scatter.21.cloned.1.call-update) | async-done | bytes 2097168 | tf_op jit(solution)/shard_map/reduce_scatter | solution.py:361
  2618.6 42.1 %all-reduce = (f32[2048]{0:T(1024)}, f32[2048]{0:T(1024)}, f32[2048]{0:T(1024)}, f32[2048]{0:T(1024)}) all-reduce(f32[2048]{0:T(1024)S(1)} %get-tuple-element.424, f32[2048]{0:T(1024)S(1)} %copy-done.72, f32[2048]{0:T(1024)S(1)} %dynamic_update_slice.46, ...), channel_id=1, replica_groups=mesh['dp'=8,'tensor'=4] {'dp','tensor'}, use_global_device_ids=true, to_apply=%region_47.48 | all-reduce | flops 8192 | bytes 65536 | tf_op jit(solution)/shard_map/psum | solution.py:376
  2664.1 81.3 %all-reduce.5.cloned.1.call-done = f32[2048,16]{0,1:T(8,128)} async-done(((f32[2048,16]{0,1:T(8,128)}), f32[2048,16]{0,1:T(8,128)}) %all-reduce.5.cloned.1.call-update) | async-done | bytes 131088 | tf_op jit(solution)/shard_map/psum | solution.py:376
  2745.4 54.2 %reduce-scatter.25.cloned.1.call-done = f32[256,512]{1,0:T(8,128)} async-done(((f32[2048,512]{1,0:T(8,128)}), f32[256,512]{1,0:T(8,128)}) %reduce-scatter.25.cloned.1.call-update) | async-done | bytes 524304 | tf_op jit(solution)/shard_map/reduce_scatter | solution.py:366
  2799.6 55.7 %reduce-scatter.23.cloned.1.call-done = f32[256,512]{1,0:T(8,128)} async-done(((f32[2048,512]{1,0:T(8,128)}), f32[256,512]{1,0:T(8,128)}) %reduce-scatter.23.cloned.1.call-update) | async-done | bytes 524304 | tf_op jit(solution)/shard_map/reduce_scatter | solution.py:365
  2855.3 55.1 %reduce-scatter.29.cloned.1.call-done = f32[256,512]{1,0:T(8,128)} async-done(((f32[2048,512]{1,0:T(8,128)}), f32[256,512]{1,0:T(8,128)}) %reduce-scatter.29.cloned.1.call-update) | async-done | bytes 524304 | tf_op jit(solution)/shard_map/reduce_scatter | solution.py:368
  2910.4 55.7 %reduce-scatter.27.cloned.1.call-done = f32[256,512]{1,0:T(8,128)} async-done(((f32[2048,512]{1,0:T(8,128)}), f32[256,512]{1,0:T(8,128)}) %reduce-scatter.27.cloned.1.call-update) | async-done | bytes 524304 | tf_op jit(solution)/shard_map/reduce_scatter | solution.py:367
  2966.0 209.4 %reduce-scatter.31.cloned.1.call-done = f32[16,256,256]{2,1,0:T(8,128)} async-done(((f32[16,2048,256]{2,1,0:T(8,128)}), f32[16,256,256]{2,1,0:T(8,128)}) %reduce-scatter.31.cloned.1.call-update) | async-done | bytes 4194320 | tf_op jit(solution)/shard_map/reduce_scatter | solution.py:369
  3175.4 209.8 %reduce-scatter.33.cloned.1.call-done = f32[16,256,256]{2,1,0:T(8,128)} async-done(((f32[16,2048,256]{2,1,0:T(8,128)}), f32[16,256,256]{2,1,0:T(8,128)}) %reduce-scatter.33.cloned.1.call-update) | async-done | bytes 4194320 | tf_op jit(solution)/shard_map/reduce_scatter | solution.py:370
  3385.3 209.3 %reduce-scatter.35.cloned.1.call-done = f32[16,256,256]{2,1,0:T(8,128)} async-done(((f32[16,2048,256]{2,1,0:T(8,128)}), f32[16,256,256]{2,1,0:T(8,128)}) %reduce-scatter.35.cloned.1.call-update) | async-done | bytes 4194320 | tf_op jit(solution)/shard_map/reduce_scatter | solution.py:371
  (792 shorter events, 1755.1 us)
Async XLA Ops:
  7.2 33.4 all-gather.14.cloned.1.call-start
  7.9 115.6 %all-gather.12.cloned.1.call-start = ((), (), s32[]{:S(2)}) async-start(), calls=%async_computation.12 | async-start | bytes 5242880 | tf_op jit(solution)/shard_map/all_gather | solution.py:139
  13.3 138.5 %all-gather.16.cloned.1.call-start = ((), (), s32[]{:S(2)}) async-start(), calls=%async_computation.14 | async-start | bytes 2359296 | tf_op jit(solution)/shard_map/all_gather | solution.py:122
  14.1 167.6 %all-gather.18.cloned.1.call-start = ((), (), s32[]{:S(2)}) async-start(), calls=%async_computation.15 | async-start | bytes 2359296 | tf_op jit(solution)/shard_map/all_gather | solution.py:123
  14.6 206.4 %all-gather.20.cloned.1.call-start = ((), (), s32[]{:S(2)}) async-start(), calls=%async_computation.16 | async-start | bytes 2359296 | tf_op jit(solution)/shard_map/all_gather | solution.py:124
  15.2 359.0 %reduce-scatter.13.cloned.1.call-start = ((), (), s32[]{:S(2)}) async-start(), calls=%async_computation.17 | async-start | bytes 10485760 | tf_op jit(solution)/shard_map/reduce_scatter | solution.py:180
  229.7 230.6 %all-gather.22.cloned.1.call-start = ((), (), s32[]{:S(2)}) async-start(), calls=%async_computation.18 | async-start | bytes 5242880 | tf_op jit(solution)/shard_map/all_gather | solution.py:191
  378.7 172.0 %all-gather.24.cloned.1.call-start = ((), (), s32[]{:S(2)}) async-start(), calls=%async_computation.19 | async-start | bytes 18874368 | tf_op jit(solution)/shard_map/all_gather | solution.py:125
  379.5 263.0 %all-gather.26.cloned.1.call-start = ((), (), s32[]{:S(2)}) async-start(), calls=%async_computation.20 | async-start | bytes 18874368 | tf_op jit(solution)/shard_map/all_gather | solution.py:126
  380.2 353.9 %all-gather.28.cloned.1.call-start = ((), (), s32[]{:S(2)}) async-start(), calls=%async_computation.21 | async-start | bytes 18874368 | tf_op jit(solution)/shard_map/all_gather | solution.py:127
  380.8 677.6 %all-gather.30.cloned.1.call-start = ((), (), s32[]{:S(2)}) async-start(), calls=%async_computation.23 | async-start | bytes 5242880 | tf_op jit(solution)/shard_map/all_gather | solution.py:221
  382.1 1820.2 %reduce-scatter.19.cloned.1.call-start = ((), (), s32[]{:S(2)}) async-start(), calls=%async_computation.25 | async-start | bytes 81920 | tf_op jit(solution)/shard_map/reduce_scatter | solution.py:268
  1745.3 458.7 %reduce-scatter.17.cloned.1.call-start = ((), (), s32[]{:S(2)}) async-start(), calls=%async_computation.24 | async-start | bytes 10485760 | tf_op jit(solution)/shard_map/reduce_scatter | solution.py:267
  1974.8 304.9 %reduce-scatter.15.cloned.1.call-start = ((), (), s32[]{:S(2)}) async-start(), calls=%async_computation.22 | async-start | bytes 5242880 | tf_op jit(solution)/shard_map/reduce_scatter | solution.py:215
  2202.3 163.6 %all-gather.32.cloned.1.call-start = ((), (), s32[]{:S(2)}) async-start(), calls=%async_computation.26 | async-start | bytes 5242880 | tf_op jit(solution)/shard_map/all_gather | solution.py:284
  2284.4 331.7 %reduce-scatter.21.cloned.1.call-start = ((), (), s32[]{:S(2)}) async-start(), calls=%async_computation.27 | async-start | bytes 10485760 | tf_op jit(solution)/shard_map/reduce_scatter | solution.py:361
  2472.5 272.9 %all-reduce.5.cloned.1.call-start = ((), (), s32[]{:S(2)}) async-start(), calls=%async_computation.35 | async-start | bytes 262144 | tf_op jit(solution)/shard_map/psum | solution.py:376
  2475.6 323.9 %reduce-scatter.25.cloned.1.call-start = ((), (), s32[]{:S(2)}) async-start(), calls=%async_computation.29 | async-start | bytes 4718592 | tf_op jit(solution)/shard_map/reduce_scatter | solution.py:366
  2483.2 372.1 %reduce-scatter.23.cloned.1.call-start = ((), (), s32[]{:S(2)}) async-start(), calls=%async_computation.28 | async-start | bytes 4718592 | tf_op jit(solution)/shard_map/reduce_scatter | solution.py:365
  2490.0 420.4 %reduce-scatter.29.cloned.1.call-start = ((), (), s32[]{:S(2)}) async-start(), calls=%async_computation.31 | async-start | bytes 4718592 | tf_op jit(solution)/shard_map/reduce_scatter | solution.py:368
  2497.0 469.0 %reduce-scatter.27.cloned.1.call-start = ((), (), s32[]{:S(2)}) async-start(), calls=%async_computation.30 | async-start | bytes 4718592 | tf_op jit(solution)/shard_map/reduce_scatter | solution.py:367
  2503.7 671.8 %reduce-scatter.31.cloned.1.call-start = ((), (), s32[]{:S(2)}) async-start(), calls=%async_computation.32 | async-start | bytes 37748736 | tf_op jit(solution)/shard_map/reduce_scatter | solution.py:369
  2504.4 880.8 %reduce-scatter.33.cloned.1.call-start = ((), (), s32[]{:S(2)}) async-start(), calls=%async_computation.33 | async-start | bytes 37748736 | tf_op jit(solution)/shard_map/reduce_scatter | solution.py:370
  2505.2 1089.4 %reduce-scatter.35.cloned.1.call-start = ((), (), s32[]{:S(2)}) async-start(), calls=%async_computation.34 | async-start | bytes 37748736 | tf_op jit(solution)/shard_map/reduce_scatter | solution.py:371
  (109 other events, 3643.4 us)
Sparse Core Ops, SparseCore 0:
  9.9 30.5 all-gather.13
  42.7 80.7 all-gather.11
  125.4 26.4 all-gather.15
  153.6 27.8 all-gather.17
  183.3 27.8 all-gather.19
  229.9 144.2 reduce-scatter.12
  378.9 81.4 all-gather.21
  462.3 88.3 all-gather.23
  552.6 89.8 all-gather.25
  644.3 89.8 all-gather.27
  736.3 80.7 all-gather.29
  1745.4 18.8 reduce-scatter.18
  1974.9 144.4 reduce-scatter.16
  2202.4 77.2 reduce-scatter.14
  2284.6 81.2 all-gather.31
  2472.6 143.4 reduce-scatter.20
  2622.1 123.2 all-reduce.4
  2749.2 50.3 reduce-scatter.24
  2803.9 51.3 reduce-scatter.22
  2859.0 51.2 reduce-scatter.28
  2914.7 51.3 reduce-scatter.26
  2970.2 205.2 reduce-scatter.30
  3180.0 205.2 reduce-scatter.32
  3389.3 205.2 reduce-scatter.34
where the time goes:
time: 3630 us; the launch traced here: 3600 us
  waiting for transfers between devices  1670 us (46%)
  local copies, waits for them, and re-layouts  1110 us (31%)
  matrix products  597 us (16%)
  other arithmetic  135 us (4%)
  blocking collectives  63.4 us (2%)
    gather x14, local copies, waits for them, and re-layouts, combine_slots(): total = total + flat_rows[slot_of[:, column]]  354 us
    reduce_scatter x1, waiting for transfers between devices, on_device(): lax.psum_scatter(grad_up_all, 'dp', scatter_dimension=1, tiled=True)  210 us
    reduce_scatter x1, waiting for transfers between devices, on_device(): lax.psum_scatter(grad_gate_all, 'dp', scatter_dimension=1, tiled=True)  209 us
    reduce_scatter x1, waiting for transfers between devices, on_device(): lax.psum_scatter(grad_down_all, 'dp', scatter_dimension=1, tiled=True)  209 us
    gather x16, local copies, waits for them, and re-layouts, expert_back(): rows_in = normed2_full[tokens_e]  152 us
    gather x16, local copies, waits for them, and re-layouts, expert_step(): rows_in = normed2_full[tokens_e]  145 us
    gather x16, local copies, waits for them, and re-layouts, expert_back(): upstream = final_full[tokens_e]  145 us
    reduce_scatter x1, waiting for transfers between devices, on_device(): lax.psum_scatter(lax.dot_general(mixed_heads, output_w, (((1,), (1,)), ((...  144 us
  transfers between devices with their start and end apart: 24, of which 19 were waited for; matrix products, arithmetic and copies ran while one was open for 29% of the time, Pallas kernels for 0%

commit v1 on v0

--- a/solution.py
+++ b/solution.py
@@ -1,12 +1,12 @@
 import jax
 import jax.numpy as jnp
 from jax import lax
+from jax.experimental import pallas as pl
+from jax.experimental.pallas import tpu as pltpu
 from jax.sharding import PartitionSpec as P
 
 HEAD = 128
-TOP = 8
 EXPERTS = 16
-CAP = 544
 
 
 EPS = 1e-05
@@ -62,29 +62,169 @@
     return same & causal & live
 
 
-def dispatch(route):
-    length = route.shape[0]
-    flat = route.reshape(-1)
-    onehot = (flat[:, None] == jnp.arange(EXPERTS, dtype=jnp.int32)[None, :]).astype(jnp.int32)
-    before = jnp.cumsum(onehot, axis=0) - onehot
-    rank = jnp.sum(before * onehot, axis=1)
-    slot = flat * CAP + rank
-    owner = jnp.arange(length * TOP, dtype=jnp.int32) // TOP
-    slot_token = jnp.zeros((EXPERTS * CAP,), jnp.int32).at[slot].set(owner)
-    slot_used = jnp.zeros((EXPERTS * CAP,), jnp.int32).at[slot].set(1)
-    return (
-        slot_token.reshape(EXPERTS, CAP),
-        slot_used.reshape(EXPERTS, CAP),
-        slot.reshape(length, TOP),
-    )
-
-
-def combine_slots(stacked, slot_of):
-    flat_rows = stacked.reshape(-1, stacked.shape[-1])
-    total = flat_rows[slot_of[:, 0]]
-    for column in range(1, slot_of.shape[1]):
-        total = total + flat_rows[slot_of[:, column]]
+NN = (((1,), (0,)), ((), ()))
+NT = (((1,), (1,)), ((), ()))
+
+
+def dot32(left, right, dims=NN):
+    return lax.dot_general(left, right, dims, preferred_element_type=jnp.float32)
+
+
+def ring_gather(own, axis):
+    n = lax.axis_size(axis)
+    right = [(i, (i + 1) % n) for i in range(n)]
+    chunks = [own]
+    for _ in range(n - 1):
+        chunks.append(lax.ppermute(chunks[-1], axis, right))
+    return chunks
+
+
+def in_order(chunks, axis):
+    n = lax.axis_size(axis)
+    here = lax.axis_index(axis)
+    rows = chunks[0].shape[0]
+    full = jnp.zeros((n * rows,) + chunks[0].shape[1:], chunks[0].dtype)
+    for step, chunk in enumerate(chunks):
+        full = lax.dynamic_update_slice_in_dim(full, chunk, ((here - step) % n) * rows, 0)
+    return full
+
+
+def ring_scatter(part_of, axis):
+    n = lax.axis_size(axis)
+    here = lax.axis_index(axis)
+    right = [(i, (i + 1) % n) for i in range(n)]
+    total = part_of((here - 1) % n)
+    for step in range(1, n):
+        moved = lax.ppermute(total.astype(jnp.bfloat16), axis, right)
+        total = moved.astype(jnp.float32) + part_of((here - 1 - step) % n)
     return total
+
+
+def all_sum(value, axes):
+    for axis in axes:
+        n = lax.axis_size(axis)
+        if n & (n - 1):
+            value = lax.psum(value, axis)
+            continue
+        bit = 1
+        while bit < n:
+            value = value + lax.ppermute(value, axis, [(i, i ^ bit) for i in range(n)])
+            bit *= 2
+    return value
+
+
+def moe_first(rows_in, upstream, weight, gate_all, up_all, down_all):
+    tokens, width = rows_in.shape
+    experts, _, hidden = gate_all.shape
+    block = min(512, tokens)
+    bf16 = jnp.bfloat16
+
+    def kernel(x_ref, f_ref, w_ref, g_ref, u_ref, d_ref, dx_ref, gp_ref, wh_ref, dg_ref, du_ref):
+        e = pl.program_id(0)
+
+        @pl.when(e == 0)
+        def _():
+            dx_ref[...] = jnp.zeros_like(dx_ref)
+            gp_ref[...] = jnp.zeros_like(gp_ref)
+
+        lane = lax.broadcasted_iota(jnp.int32, (block, experts), 1)
+        for r in range(tokens // block):
+            rs = pl.ds(r * block, block)
+            x = x_ref[rs, :]
+            w = jnp.sum(jnp.where(lane == e, w_ref[rs, :], 0.0), axis=1, keepdims=True)
+            gate_pre = dot32(x, g_ref[0])
+            up_pre = dot32(x, u_ref[0])
+            projected = dot32(f_ref[rs, :], d_ref[0])
+            sig = 1.0 / (1.0 + jnp.exp(-gate_pre))
+            act = gate_pre * sig
+            hidden_f = act * up_pre
+            wh_ref[0, rs, :] = (w * hidden_f).astype(bf16)
+            inner = jnp.sum(hidden_f * projected, axis=1, keepdims=True)
+            gp_ref[rs, :] = jnp.where(lane == e, inner, gp_ref[rs, :])
+            grad_hidden = w * projected
+            dg = (grad_hidden * up_pre * (sig + act * (1.0 - sig))).astype(bf16)
+            du = (grad_hidden * act).astype(bf16)
+            dg_ref[0, rs, :] = dg
+            du_ref[0, rs, :] = du
+            dx_ref[rs, :] += dot32(dg, g_ref[0], NT) + dot32(du, u_ref[0], NT)
+
+    once = pl.Buffered(1)
+
+    def whole(shape):
+        return pl.BlockSpec(shape, lambda e: (0, 0), pipeline_mode=once)
+
+    w_spec = pl.BlockSpec((1, width, hidden), lambda e: (e, 0, 0))
+    h_spec = pl.BlockSpec((1, tokens, hidden), lambda e: (e, 0, 0))
+    kept = jax.ShapeDtypeStruct((experts, tokens, hidden), bf16)
+    return pl.pallas_call(
+        kernel,
+        grid=(experts,),
+        in_specs=[whole((tokens, width)), whole((tokens, width)), whole((tokens, experts)), w_spec, w_spec, w_spec],
+        out_specs=[
+            pl.BlockSpec((tokens, width), lambda e: (0, 0)),
+            pl.BlockSpec((tokens, experts), lambda e: (0, 0)),
+            h_spec,
+            h_spec,
+            h_spec,
+        ],
+        out_shape=[
+            jax.ShapeDtypeStruct((tokens, width), jnp.float32),
+            jax.ShapeDtypeStruct((tokens, experts), jnp.float32),
+            kept,
+            kept,
+            kept,
+        ],
+        compiler_params=pltpu.CompilerParams(vmem_limit_bytes=58 << 20),
+        cost_estimate=pl.CostEstimate(
+            flops=10 * tokens * width * hidden * experts,
+            transcendentals=tokens * hidden * experts,
+            bytes_accessed=6 * experts * hidden * (width + tokens) + 12 * tokens * width,
+        ),
+        name="moe_first",
+    )(rows_in, upstream, weight, gate_all, up_all, down_all)
+
+
+def moe_second(x_t, f_t, wh, dg, du, down_all):
+    width, tokens = x_t.shape
+    experts, _, hidden = down_all.shape
+    bf16 = jnp.bfloat16
+
+    def kernel(x_ref, f_ref, wh_ref, dg_ref, du_ref, d_ref, out_ref, gd_ref, gg_ref, gu_ref, acc):
+        e = pl.program_id(0)
+
+        @pl.when(e == 0)
+        def _():
+            acc[...] = jnp.zeros_like(acc)
+
+        gd_ref[0] = dot32(f_ref[...], wh_ref[0]).astype(bf16)
+        gg_ref[0] = dot32(x_ref[...], dg_ref[0]).astype(bf16)
+        gu_ref[0] = dot32(x_ref[...], du_ref[0]).astype(bf16)
+        acc[...] += dot32(wh_ref[0], d_ref[0], NT)
+
+        @pl.when(e == experts - 1)
+        def _():
+            out_ref[...] = acc[...].astype(bf16)
+
+    once = pl.Buffered(1)
+    x_spec = pl.BlockSpec((width, tokens), lambda e: (0, 0), pipeline_mode=once)
+    w_spec = pl.BlockSpec((1, width, hidden), lambda e: (e, 0, 0))
+    h_spec = pl.BlockSpec((1, tokens, hidden), lambda e: (e, 0, 0))
+    grad = jax.ShapeDtypeStruct((experts, width, hidden), bf16)
+    return pl.pallas_call(
+        kernel,
+        grid=(experts,),
+        in_specs=[x_spec, x_spec, h_spec, h_spec, h_spec, w_spec],
+        out_specs=[pl.BlockSpec((tokens, width), lambda e: (0, 0)), w_spec, w_spec, w_spec],
+        out_shape=[jax.ShapeDtypeStruct((tokens, width), bf16), grad, grad, grad],
+        scratch_shapes=[pltpu.VMEM((tokens, width), jnp.float32)],
+        compiler_params=pltpu.CompilerParams(vmem_limit_bytes=58 << 20),
+        cost_estimate=pl.CostEstimate(
+            flops=8 * tokens * width * hidden * experts,
+            transcendentals=0,
+            bytes_accessed=2 * experts * hidden * (4 * width + 3 * tokens) + 10 * tokens * width,
+        ),
+        name="moe_second",
+    )(x_t, f_t, wh, dg, du, down_all)
 
 
 def on_device(
@@ -117,16 +257,17 @@
     length = seg_all.shape[0]
     row_offset = lax.axis_index("tensor") * rows_here
     scale = HEAD ** (-0.5)
-    gathered = (
-        lax.all_gather(query_weight, "dp", axis=0, tiled=True),
-        lax.all_gather(key_weight, "dp", axis=0, tiled=True),
-        lax.all_gather(value_weight, "dp", axis=0, tiled=True),
-        lax.all_gather(output_weight, "dp", axis=0, tiled=True),
-        lax.all_gather(gate_weight, "dp", axis=1, tiled=True),
-        lax.all_gather(up_weight, "dp", axis=1, tiled=True),
-        lax.all_gather(down_weight, "dp", axis=1, tiled=True),
-    )
-    query_w, key_w, value_w, output_w, gate_all, up_all, down_all = gathered
+    own_final = (
+        cotangent[0].astype(f32)
+        * lax.dynamic_slice_in_dim(valid_all, row_offset, rows_here).astype(f32)[:, None]
+    )
+    attn_all = lax.all_gather(
+        jnp.stack([query_weight, key_weight, value_weight, output_weight]), "dp", axis=1, tiled=True
+    )
+    query_w, key_w, value_w, output_w = (attn_all[i] for i in range(4))
+    gate_all = lax.all_gather(gate_weight, "dp", axis=1, tiled=True)
+    up_all = lax.all_gather(up_weight, "dp", axis=1, tiled=True)
+    down_all = lax.all_gather(down_weight, "dp", axis=1, tiled=True)
     local_cols = query_w.shape[1]
     heads_here = local_cols // HEAD
     head_offset = lax.axis_index("tensor") * local_cols
@@ -136,7 +277,8 @@
     gain_key = lax.dynamic_slice_in_dim(key_norm_gain.astype(f32), head_offset, local_cols)
     normed1, unit1, scale1 = rows_norm(local_x, gain_attn)
     normed1_low = normed1.astype(bf16)
-    normed1_full = lax.all_gather(normed1_low, "tensor", axis=0, tiled=True)
+    normed1_full = in_order(ring_gather(normed1_low, "tensor"), "tensor")
+    final_full = in_order(ring_gather(own_final.astype(bf16), "tensor"), "tensor")
     query_raw = jnp.dot(normed1_full, query_w, preferred_element_type=f32)
     key_raw = jnp.dot(normed1_full, key_w, preferred_element_type=f32)
     value_heads = (
@@ -177,96 +319,38 @@
 
     mixed_blocks, lse_blocks = lax.map(attend, starts)
     mixed_heads = mixed_blocks.reshape(length, local_cols)
-    attn_local = lax.psum_scatter(
-        lax.dot_general(
-            mixed_heads, output_w, (((1,), (1,)), ((), ())), preferred_element_type=f32
-        ),
-        "tensor",
-        scatter_dimension=0,
-        tiled=True,
+    def rows_of(array, chunk):
+        return lax.dynamic_slice_in_dim(array, chunk * rows_here, rows_here, 0)
+
+    attn_local = ring_scatter(
+        lambda c: dot32(rows_of(mixed_heads, c), output_w, NT), "tensor"
     )
     resid = local_x + attn_local
     normed2, unit2, scale2 = rows_norm(resid, gain_expert)
     normed2_low = normed2.astype(bf16)
-    normed2_full = lax.all_gather(normed2_low, "tensor", axis=0, tiled=True)
+    normed2_full = in_order(ring_gather(normed2_low, "tensor"), "tensor")
     router_f = router_weight.astype(f32)
     logits = jnp.dot(normed2_full, router_weight, preferred_element_type=f32)
     route_probs = jax.nn.softmax(logits, axis=-1)
-    slot_token, slot_used, slot_of = dispatch(route_all)
-    expert_ids = jnp.arange(EXPERTS, dtype=jnp.int32)[:, None]
-    used_float = slot_used.astype(f32)
-    gate_slot = route_probs[slot_token, expert_ids] * used_float
-
-    def expert_step(carried, pieces):
-        gate_e, up_e, down_e, tokens_e, weight_e = pieces
-        rows_in = normed2_full[tokens_e]
-        gate_pre = jnp.dot(rows_in, gate_e, preferred_element_type=f32)
-        up_pre = jnp.dot(rows_in, up_e, preferred_element_type=f32)
-        hidden_low = (jax.nn.silu(gate_pre) * up_pre).astype(bf16)
-        expert_out = lax.dot_general(
-            hidden_low, down_e, (((1,), (1,)), ((), ())), preferred_element_type=f32
-        )
-        return (carried, (expert_out * weight_e[:, None], gate_pre, up_pre))
-
-    _, (weighted_outs, gate_kept, up_kept) = lax.scan(
-        expert_step, jnp.zeros((), f32), (gate_all, up_all, down_all, slot_token, gate_slot)
-    )
-    moe_partial = combine_slots(weighted_outs, slot_of)
-    moe_local = lax.psum_scatter(
-        moe_partial.astype(jnp.bfloat16), "tensor", scatter_dimension=0, tiled=True
-    ).astype(jnp.float32)
-    layer_local = (resid + moe_local).astype(bf16)
-    valid_here = lax.dynamic_slice_in_dim(valid_all, row_offset, rows_here).astype(f32)
-    grad_final = cotangent[0].astype(f32) * valid_here[:, None]
-    final_full = lax.all_gather(grad_final.astype(bf16), "tensor", axis=0, tiled=True)
-
-    def expert_back(carried, pieces):
-        gate_e, up_e, down_e, tokens_e, weight_e, gate_pre, up_pre = pieces
-        rows_in = normed2_full[tokens_e]
-        upstream = final_full[tokens_e]
-        sig_gate = jax.nn.sigmoid(gate_pre)
-        activated = gate_pre * sig_gate
-        hidden_low = (activated * up_pre).astype(bf16)
-        projected = jnp.dot(upstream, down_e, preferred_element_type=f32)
-        grad_weight = jnp.sum(hidden_low.astype(f32) * projected, axis=1)
-        grad_eo = (upstream.astype(f32) * weight_e[:, None]).astype(bf16)
-        grad_hidden = jnp.dot(grad_eo, down_e, preferred_element_type=f32)
-        grad_down_e = lax.dot_general(
-            grad_eo, hidden_low, (((0,), (0,)), ((), ())), preferred_element_type=f32
-        )
-        grad_gpre = (grad_hidden * up_pre * sig_gate * (1.0 + gate_pre * (1.0 - sig_gate))).astype(
-            bf16
-        )
-        grad_upre = (grad_hidden * activated).astype(bf16)
-        grad_gate_e = lax.dot_general(
-            rows_in, grad_gpre, (((0,), (0,)), ((), ())), preferred_element_type=f32
-        )
-        grad_up_e = lax.dot_general(
-            rows_in, grad_upre, (((0,), (0,)), ((), ())), preferred_element_type=f32
-        )
-        grad_rows = lax.dot_general(
-            grad_gpre, gate_e, (((1,), (1,)), ((), ())), preferred_element_type=f32
-        )
-        grad_rows = grad_rows + lax.dot_general(
-            grad_upre, up_e, (((1,), (1,)), ((), ())), preferred_element_type=f32
-        )
-        return (carried, (grad_gate_e, grad_up_e, grad_down_e, grad_weight, grad_rows))
-
-    _, (grad_gate_all, grad_up_all, grad_down_all, grad_weight_slot, grad_rows_all) = lax.scan(
-        expert_back,
-        jnp.zeros((), f32),
-        (gate_all, up_all, down_all, slot_token, gate_slot, gate_kept, up_kept),
-    )
-    normed2_grad_part = combine_slots(grad_rows_all, slot_of)
-    picked = grad_weight_slot.reshape(-1)[slot_of]
-    route_match = (
-        route_all[:, :, None] == jnp.arange(EXPERTS, dtype=jnp.int32)[None, None, :]
-    ).astype(f32)
-    prob_grad_part = jnp.sum(route_match * picked[:, :, None], axis=1)
-    normed2_grad, prob_grad = (
-        lax.psum_scatter(normed2_grad_part, "tensor", scatter_dimension=0, tiled=True),
-        lax.psum_scatter(prob_grad_part, "tensor", scatter_dimension=0, tiled=True),
-    )
+    routed = jnp.any(
+        route_all[:, :, None] == jnp.arange(EXPERTS, dtype=jnp.int32)[None, None, :], axis=1
+    )
+    gate_weights = jnp.where(routed, route_probs, 0.0)
+    normed2_part, gate_grad_part, weighted_hidden, grad_gpre, grad_upre = moe_first(
+        normed2_full, final_full, gate_weights, gate_all, up_all, down_all
+    )
+    prob_grad = lax.psum_scatter(
+        jnp.where(routed, gate_grad_part, 0.0), "tensor", scatter_dimension=0, tiled=True
+    )
+    normed2_grad = ring_scatter(lambda c: rows_of(normed2_part, c), "tensor")
+    moe_partial, grad_down_all, grad_gate_all, grad_up_all = moe_second(
+        normed2_full.T, final_full.T, weighted_hidden, grad_gpre, grad_upre, down_all
+    )
+    reduced_experts = tuple(
+        lax.psum_scatter(grad, "dp", scatter_dimension=1, tiled=True).astype(f32)
+        for grad in (grad_gate_all, grad_up_all, grad_down_all)
+    )
+    grad_final = own_final
     probs_here = lax.dynamic_slice_in_dim(route_probs, row_offset, rows_here, 0)
     grad_logits = probs_here * (prob_grad - jnp.sum(probs_here * prob_grad, axis=1, keepdims=True))
     normed2_grad = normed2_grad + jnp.dot(
@@ -281,7 +365,9 @@
     )
     resid_norm_grad, grad_expert_part = norm_back(normed2_grad, gain_expert, unit2, scale2)
     grad_resid = grad_final + resid_norm_grad
-    resid_full = lax.all_gather(grad_resid.astype(bf16), "tensor", axis=0, tiled=True)
+    resid_full = in_order(ring_gather(grad_resid.astype(bf16), "tensor"), "tensor")
+    moe_local = ring_scatter(lambda c: rows_of(moe_partial, c).astype(f32), "tensor")
+    layer_local = (resid + moe_local).astype(bf16)
     grad_output_part = lax.dot_general(
         resid_full, mixed_heads, (((0,), (0,)), ((), ())), preferred_element_type=f32
     )
@@ -349,49 +435,45 @@
     grad_value_part = lax.dot_general(
         normed1_full, value_low, (((0,), (0,)), ((), ())), preferred_element_type=f32
     )
-    total_rows = lax.dot_general(
-        query_raw_low, query_w, (((1,), (1,)), ((), ())), preferred_element_type=f32
-    )
-    total_rows = total_rows + lax.dot_general(
-        key_raw_low, key_w, (((1,), (1,)), ((), ())), preferred_element_type=f32
-    )
-    total_rows = total_rows + lax.dot_general(
-        value_low, value_w, (((1,), (1,)), ((), ())), preferred_element_type=f32
-    )
-    normed1_grad = lax.psum_scatter(total_rows, "tensor", scatter_dimension=0, tiled=True)
+    normed1_grad = ring_scatter(
+        lambda c: dot32(rows_of(query_raw_low, c), query_w, NT)
+        + dot32(rows_of(key_raw_low, c), key_w, NT)
+        + dot32(rows_of(value_low, c), value_w, NT),
+        "tensor",
+    )
     input_norm_grad, grad_attn_part = norm_back(normed1_grad, gain_attn, unit1, scale1)
     grad_input = grad_resid + input_norm_grad
-    reduced = (
-        lax.psum_scatter(grad_query_part, "dp", scatter_dimension=0, tiled=True),
-        lax.psum_scatter(grad_key_part, "dp", scatter_dimension=0, tiled=True),
-        lax.psum_scatter(grad_value_part, "dp", scatter_dimension=0, tiled=True),
-        lax.psum_scatter(grad_output_part, "dp", scatter_dimension=0, tiled=True),
-        lax.psum_scatter(grad_gate_all, "dp", scatter_dimension=1, tiled=True),
-        lax.psum_scatter(grad_up_all, "dp", scatter_dimension=1, tiled=True),
-        lax.psum_scatter(grad_down_all, "dp", scatter_dimension=1, tiled=True),
+    reduced_qkv = lax.psum_scatter(
+        jnp.stack([grad_query_part, grad_key_part, grad_value_part]).astype(bf16),
+        "dp",
+        scatter_dimension=1,
+        tiled=True,
+    ).astype(f32)
+    reduced_output = lax.psum_scatter(
+        grad_output_part.astype(bf16), "dp", scatter_dimension=0, tiled=True
+    ).astype(f32)
+    early = all_sum(
+        jnp.concatenate([grad_router_part.T, grad_expert_part[None]]), ("tensor", "dp")
     )
     zeros_width = jnp.zeros((model_width,), f32)
     qgain_full = lax.dynamic_update_slice(zeros_width, grad_qgain_here, (head_offset,))
     kgain_full = lax.dynamic_update_slice(zeros_width, grad_kgain_here, (head_offset,))
-    summed = lax.psum(
-        (grad_attn_part, grad_expert_part, qgain_full, kgain_full, grad_router_part),
-        ("dp", "tensor"),
-    )
+    late = all_sum(jnp.stack([qgain_full, kgain_full, grad_attn_part]), ("tensor", "dp"))
     return (
         layer_local[None],
         grad_input[None],
-        reduced[0],
-        reduced[1],
-        reduced[2],
-        reduced[3],
-        reduced[4],
-        reduced[5],
-        reduced[6],
-        summed[4],
-        summed[0],
-        summed[1],
-        summed[2],
-        summed[3],
+        reduced_qkv[0],
+        reduced_qkv[1],
+        reduced_qkv[2],
+        reduced_output,
+        reduced_experts[0],
+        reduced_experts[1],
+        reduced_experts[2],
+        early[:EXPERTS].T,
+        late[2],
+        early[EXPERTS],
+        late[0],
+        late[1],
     )
 
 

time: 3630 us -> 1260 us (0.35)
  local copies, waits for them, and re-layouts: 1110 us -> 107 us
  waiting for transfers between devices: 1670 us -> 675 us
  matrix products: 597 us -> 114 us
  Pallas kernels: 0 us -> 200 us
  blocking collectives: 63.4 us -> 17.2 us
  other arithmetic: 135 us -> 95.2 us
    reduce_scatter x12 -> x6, waiting for transfers between devices: 1170 us -> 185 us  [the longest x3 160 us: on_device(): lax.psum_scatter(grad, 'dp', scatter_dimension=1, tiled=True).astype(f32)]
    gather x68 -> x0, local copies, waits for them, and re-layouts: 962 us -> none  [the longest x14 354 us: combine_slots(): total = total + flat_rows[slot_of[:, column]]]
    ppermute x0 -> x34, waiting for transfers between devices: none -> 488 us  [the longest x12 247 us: ring_gather(): chunks.append(lax.ppermute(chunks[-1], axis, right))]
    dot_general x164 -> x16, matrix products: 491 us -> 27 us  [dot32(): lax.dot_general(left, right, dims, preferred_element_type=jnp.float32)]
    all_gather x11 -> x4, waiting for transfers between devices: 412 us -> 0.01 us  [the longest x1 0.01 us: on_device(): lax.all_gather(jnp.stack([query_weight, key_weight, value_weight, output_...]
    pallas_call x0 -> x2, Pallas kernels: none -> 200 us  [the longest x1 119 us: moe_first(): pl.pallas_call(kernel, grid=(experts,), in_specs=[whole((tokens, width)),...]
    psum x1 -> x0, waiting for transfers between devices: 81.3 us -> none  [on_device(): lax.psum((grad_attn_part, grad_expert_part, qgain_full, kgain_full, grad_...]
    scatter x2 -> x0, local copies, waits for them, and re-layouts: 60.9 us -> none  [the longest x1 30.5 us: dispatch(): slot_token = jnp.zeros((EXPERTS * CAP,), jnp.int32).at[slot].set(owner)]
  transfers between devices with their start and end apart: 24 -> 44, of which waited for: 19 -> 27; matrix products, arithmetic and copies ran while one was open for 29% -> 16% of each run, Pallas kernels for 0% -> 7%
where the time goes in v1:
time: 1260 us; the launch traced here: 1250 us
  waiting for transfers between devices  675 us (54%)
  Pallas kernels  200 us (16%)
  matrix products  114 us (9%)
  local copies, waits for them, and re-layouts  107 us (8%)
  other arithmetic  95.2 us (8%)
  starting transfers between devices  20.6 us (2%)
  blocking collectives  17.2 us (1%)
  between operations  15.8 us (1%)
    ppermute x12, waiting for transfers between devices, ring_gather(): chunks.append(lax.ppermute(chunks[-1], axis, right))  247 us
    ppermute x12, waiting for transfers between devices, ring_scatter(): moved = lax.ppermute(total.astype(jnp.bfloat16), axis, right)  167 us
    reduce_scatter x3, waiting for transfers between devices, on_device(): lax.psum_scatter(grad, 'dp', scatter_dimension=1, tiled=True).astype(f32)  160 us
    pallas_call x1, Pallas kernels, moe_first(): pl.pallas_call(kernel, grid=(experts,), in_specs=[whole((tokens, width)),...  119 us
    pallas_call x1, Pallas kernels, moe_second(): pl.pallas_call(kernel, grid=(experts,), in_specs=[x_spec, x_spec, h_spec,...  81.7 us
    ppermute x10, waiting for transfers between devices, all_sum(): value = value + lax.ppermute(value, axis, [(i, i ^ bit) for i in range(n)])  73.9 us
    dynamic_update_slice x14, local copies, waits for them, and re-layouts, in_order(): lax.dynamic_update_slice_in_dim(full, chunk, (here - step) % n * rows, 0)  36.7 us
    dot_general x16, matrix products, dot32(): lax.dot_general(left, right, dims, preferred_element_type=jnp.float32)  27 us
  transfers between devices with their start and end apart: 44, of which 27 were waited for; matrix products, arithmetic and copies ran while one was open for 16% of the time, Pallas kernels for 7%

profile of v1, /device:TPU:0, one launch (start us, length us, event | category | flops | bytes accessed | tf_op | source)
XLA Modules:
  0.0 1253.9 jit_solution(14414243335262277067)
XLA Ops:
  18.6 25.2 %collective-permute-done = bf16[256,2048]{0,1:T(8,128)(2,1)S(1)} collective-permute-done((bf16[256,2048]{0,1:T(8,128)(2,1)S(1)}, bf16[256,2048]{0,1:T(8,128)(2,1)S(1)}, u32[]{:S(2)}, u32[]{:S(2)}) %collective-permute-start) | collective-permute-done | bytes 1048608 | tf_op jit(solution)/shard_map/ppermute | solution.py:78
  43.8 26.1 %collective-permute-done.1 = bf16[256,2048]{0,1:T(8,128)(2,1)S(1)} collective-permute-done((bf16[256,2048]{0,1:T(8,128)(2,1)S(1)}, bf16[256,2048]{0,1:T(8,128)(2,1)S(1)}, u32[]{:S(2)}, u32[]{:S(2)}) %collective-permute-start.1) | collective-permute-done | bytes 1048608 | tf_op jit(solution)/shard_map/ppermute | solution.py:78
  75.7 19.5 %collective-permute-done.2 = bf16[256,2048]{0,1:T(8,128)(2,1)S(1)} collective-permute-done((bf16[256,2048]{0,1:T(8,128)(2,1)S(1)}, bf16[256,2048]{0,1:T(8,128)(2,1)S(1)}, u32[]{:S(2)}, u32[]{:S(2)}) %collective-permute-start.2) | collective-permute-done | bytes 1048608 | tf_op jit(solution)/shard_map/ppermute | solution.py:78
  142.3 25.6 %while.27 = (s32[]{:T(128)}, bf16[2,512,4,128]{3,2,1,0:T(4,128)(2,1)}, f32[2,4,512]{2,1,0:T(4,128)S(1)}, s32[2]{0:T(128)S(1)}, s32[1024]{0:T(1024)S(1)}, /*index...) while((s32[]{:T(128)}, ...), condition=%wide.region_8.9_spmd, body=%wide.region_5.8_spmd.sunk | while | flops 1102315008 | bytes 31543996 | solution.py:320
  175.1 20.9 %collective-permute-done.3 = bf16[256,2048]{0,1:T(8,128)(2,1)S(1)} collective-permute-done((bf16[256,2048]{0,1:T(8,128)(2,1)S(1)}, bf16[256,2048]{0,1:T(8,128)(2,1)S(1)}, u32[]{:S(2)}, u32[]{:S(2)}) %collective-permute-start.3) | collective-permute-done | bytes 1048608 | tf_op jit(solution)/shard_map/ppermute | solution.py:98
  200.7 19.5 %collective-permute-done.4 = bf16[256,2048]{0,1:T(8,128)(2,1)S(1)} collective-permute-done((bf16[256,2048]{0,1:T(8,128)(2,1)S(1)}, bf16[256,2048]{0,1:T(8,128)(2,1)S(1)}, u32[]{:S(2)}, u32[]{:S(2)}) %collective-permute-start.4) | collective-permute-done | bytes 1048608 | tf_op jit(solution)/shard_map/ppermute | solution.py:98
  229.6 20.3 %collective-permute-done.5 = bf16[256,2048]{0,1:T(8,128)(2,1)} collective-permute-done((bf16[256,2048]{0,1:T(8,128)(2,1)}, bf16[256,2048]{0,1:T(8,128)(2,1)}, u32[]{:S(2)}, u32[]{:S(2)}) %collective-permute-start.5) | collective-permute-done | bytes 1048608 | tf_op jit(solution)/shard_map/ppermute | solution.py:98
  272.3 22.5 %collective-permute-done.6 = bf16[256,2048]{0,1:T(8,128)(2,1)} collective-permute-done((bf16[256,2048]{0,1:T(8,128)(2,1)S(1)}, bf16[256,2048]{0,1:T(8,128)(2,1)}, u32[]{:S(2)}, u32[]{:S(2)}) %collective-permute-start.6) | collective-permute-done | bytes 1048608 | tf_op jit(solution)/shard_map/ppermute | solution.py:78
  294.8 22.5 %collective-permute-done.10 = bf16[256,2048]{0,1:T(8,128)(2,1)} collective-permute-done((bf16[256,2048]{0,1:T(8,128)(2,1)}, bf16[256,2048]{0,1:T(8,128)(2,1)}, u32[]{:S(2)}, u32[]{:S(2)}) %collective-permute-start.10) | collective-permute-done | bytes 1048608 | tf_op jit(solution)/shard_map/ppermute | solution.py:78
  317.6 22.1 %collective-permute-done.7 = bf16[256,2048]{0,1:T(8,128)(2,1)} collective-permute-done((bf16[256,2048]{0,1:T(8,128)(2,1)}, bf16[256,2048]{0,1:T(8,128)(2,1)}, u32[]{:S(2)}, u32[]{:S(2)}) %collective-permute-start.7) | collective-permute-done | bytes 1048608 | tf_op jit(solution)/shard_map/ppermute | solution.py:78
  394.0 118.6 %moe_first.1 = (f32[1024,2048]{1,0:T(8,128)}, f32[1024,16]{1,0:T(8,128)}, bf16[16,1024,256]{2,1,0:T(8,128)(2,1)}, bf16[16,1024,256]{2,1,0:T(8,128)(2,1)}, bf16[16,1024,256]{2,1,0:T(8,128)(2,1)}) custom-call(bf16[1024,2048]{1,0:T(8,128)(2,1)} %copy.137.x_ref, bf16[1024,2048]{1,0:T(8,128)(2,1)} %copy.138.f_ref, f32[1024,16]{1,0:T(8,128)} %get-tuple-element.373.w_ref, ...), custom_call_target="tpu_custom_call" | custom-call | flops 85899345920 | bytes 100663296 | tf_op jit(solution)/shard_map/moe_first/pallas_call | solution.py:159
  523.9 21.3 %collective-permute-done.15 = bf16[256,2048]{0,1:T(8,128)(2,1)S(1)} collective-permute-done((bf16[256,2048]{0,1:T(8,128)(2,1)S(1)}, bf16[256,2048]{0,1:T(8,128)(2,1)S(1)}, u32[]{:S(2)}, u32[]{:S(2)}) %collective-permute-start.15) | collective-permute-done | bytes 1048608 | tf_op jit(solution)/shard_map/ppermute | solution.py:98
  547.2 20.2 %collective-permute-done.16 = bf16[256,2048]{0,1:T(8,128)(2,1)S(1)} collective-permute-done((bf16[256,2048]{0,1:T(8,128)(2,1)S(1)}, bf16[256,2048]{0,1:T(8,128)(2,1)S(1)}, u32[]{:S(2)}, u32[]{:S(2)}) %collective-permute-start.16) | collective-permute-done | bytes 1048608 | tf_op jit(solution)/shard_map/ppermute | solution.py:98
  571.3 24.4 %reduce-scatter.7.cloned.1.call-done = f32[256,16]{1,0:T(8,128)} async-done(((f32[1024,16]{1,0:T(8,128)}), f32[256,16]{1,0:T(8,128)}) %reduce-scatter.7.cloned.1.call-update) | async-done | bytes 16400 | tf_op jit(solution)/shard_map/reduce_scatter | solution.py:342
  605.6 26.4 %collective-permute-done.18 = bf16[256,2048]{0,1:T(8,128)(2,1)S(1)} collective-permute-done((bf16[256,2048]{0,1:T(8,128)(2,1)S(1)}, bf16[256,2048]{0,1:T(8,128)(2,1)S(1)}, u32[]{:S(2)}, u32[]{:S(2)}) %collective-permute-start.18) | collective-permute-done | bytes 1048608 | tf_op jit(solution)/shard_map/ppermute | solution.py:78
  632.0 26.2 %collective-permute-done.19 = bf16[256,2048]{0,1:T(8,128)(2,1)} collective-permute-done((bf16[256,2048]{0,1:T(8,128)(2,1)S(1)}, bf16[256,2048]{0,1:T(8,128)(2,1)}, u32[]{:S(2)}, u32[]{:S(2)}) %collective-permute-start.19) | collective-permute-done | bytes 1048608 | tf_op jit(solution)/shard_map/ppermute | solution.py:78
  662.8 21.0 %collective-permute-done.20 = bf16[256,2048]{0,1:T(8,128)(2,1)} collective-permute-done((bf16[256,2048]{0,1:T(8,128)(2,1)}, bf16[256,2048]{0,1:T(8,128)(2,1)}, u32[]{:S(2)}, u32[]{:S(2)}) %collective-permute-start.20) | collective-permute-done | bytes 1048608 | tf_op jit(solution)/shard_map/ppermute | solution.py:78
  698.5 51.7 %while.28 = (s32[]{:T(128)}, f32[1024,4,128]{0,2,1:T(8,128)S(1)}, f32[1024,4,128]{0,2,1:T(8,128)}, f32[2,512,4,128]{3,1,0,2:T(8,128)}, s32[2]{0:T(128)S(1)}, /*i...) while((s32[]{:T(128)}, f32[1024,4,128]{0,2,1:T(8,128)S(1)}, ...), condition=%wide.region_18.19_spmd.clone, body=%wide.region_16.18_spmd.clone.sunk | while | flops 2721840640 | bytes 180433904 | solution.py:408
  800.8 81.7 %moe_second.1 = (bf16[1024,2048]{1,0:T(8,128)(2,1)}, bf16[16,2048,256]{2,1,0:T(8,128)(2,1)}, bf16[16,2048,256]{2,1,0:T(8,128)(2,1)}, bf16[16,2048,256]{2,1,0:T(8,128)(2,1)}) custom-call(bf16[2048,1024]{1,0:T(8,128)(2,1)} %bitcast.19.x_ref, bf16[2048,1024]{1,0:T(8,128)(2,1)} %bitcast.22.f_ref, bf16[16,1024,256]{2,1,0:T(8,128)(2,1)} %get-tuple-element.146.wh_ref, ...), custom_call_target="tpu_custom_call" | custom-call | flops 68719476736 | bytes 113246208 | tf_op jit(solution)/shard_map/moe_second/pallas_call | solution.py:213
  908.9 47.9 %collective-permute-done.25 = f32[17,2048]{1,0:T(8,128)S(1)} collective-permute-done((f32[17,2048]{1,0:T(8,128)S(1)}, f32[17,2048]{1,0:T(8,128)S(1)}, u32[]{:S(2)}, u32[]{:S(2)}) %collective-permute-start.25) | collective-permute-done | bytes 139296 | tf_op jit(solution)/shard_map/ppermute | solution.py:111
  961.6 25.1 %collective-permute-done.22 = bf16[256,2048]{0,1:T(8,128)(2,1)S(1)} collective-permute-done((bf16[256,2048]{0,1:T(8,128)(2,1)S(1)}, bf16[256,2048]{0,1:T(8,128)(2,1)S(1)}, u32[]{:S(2)}, u32[]{:S(2)}) %collective-permute-start.22) | collective-permute-done | bytes 1048608 | tf_op jit(solution)/shard_map/ppermute | solution.py:98
  990.6 24.3 %collective-permute-done.23 = bf16[256,2048]{0,1:T(8,128)(2,1)S(1)} collective-permute-done((bf16[256,2048]{0,1:T(8,128)(2,1)S(1)}, bf16[256,2048]{0,1:T(8,128)(2,1)S(1)}, u32[]{:S(2)}, u32[]{:S(2)}) %collective-permute-start.23) | collective-permute-done | bytes 1048608 | tf_op jit(solution)/shard_map/ppermute | solution.py:98
  1078.4 45.0 %reduce-scatter.15.cloned.1.call-done = bf16[16,256,256]{2,1,0:T(8,128)(2,1)} async-done(((bf16[16,2048,256]{2,1,0:T(8,128)(2,1)}), bf16[16,256,256]{2,1,0:T(8,128)(2,1)}) %reduce-scatter.15.cloned.1.call-update) | async-done | bytes 2097168 | tf_op jit(solution)/shard_map/reduce_scatter | solution.py:350
  1127.4 115.3 %reduce-scatter.17.cloned.1.call-done = bf16[16,256,256]{2,1,0:T(8,128)(2,1)} async-done(((bf16[16,2048,256]{2,1,0:T(8,128)(2,1)}), bf16[16,256,256]{2,1,0:T(8,128)(2,1)}) %reduce-scatter.17.cloned.1.call-update) | async-done | bytes 2097168 | tf_op jit(solution)/shard_map/reduce_scatter | solution.py:350
  (445 shorter events, 433.8 us)
Async XLA Ops:
  7.2 89.0 %all-gather.5.cloned.1.call-start = ((), (), s32[]{:S(2)}) async-start(), calls=%async_computation.6 | async-start | bytes 9437184 | tf_op jit(solution)/shard_map/all_gather | solution.py:264
  9.6 384.5 %all-gather.11.cloned.1.call-start = ((), (), s32[]{:S(2)}) async-start(), calls=%async_computation.9 | async-start | bytes 18874368 | tf_op jit(solution)/shard_map/all_gather | solution.py:270
  10.3 383.7 %all-gather.7.cloned.1.call-start = ((), (), s32[]{:S(2)}) async-start(), calls=%async_computation.7 | async-start | bytes 18874368 | tf_op jit(solution)/shard_map/all_gather | solution.py:268
  11.1 383.0 %all-gather.9.cloned.1.call-start = ((), (), s32[]{:S(2)}) async-start(), calls=%async_computation.8 | async-start | bytes 18874368 | tf_op jit(solution)/shard_map/all_gather | solution.py:269
  11.6 584.0 %reduce-scatter.7.cloned.1.call-start = ((), (), s32[]{:S(2)}) async-start(), calls=%async_computation.10 | async-start | bytes 655360 | tf_op jit(solution)/shard_map/reduce_scatter | solution.py:342
  221.6 28.2 %collective-permute-start.5 = (bf16[256,2048]{0,1:T(8,128)(2,1)}, bf16[256,2048]{0,1:T(8,128)(2,1)}, u32[]{:S(2)}, u32[]{:S(2)}) collective-permute-start(bf16[256,2048]{0,1:T(8,128)(2,1)} %add_convert_fusion.7), channel_id=1, source_target_pairs={{0,1},{1,2},{2,3},{3,0},{4,5},{5,6},{6,7},{7,4},{8,9},{9,10},{10,1... | collective-permute-start | bytes 3145736 | tf_op jit(solution)/shard_map/ppermute | solution.py:98
  226.4 45.9 %collective-permute-start.9 = (bf16[256,2048]{0,1:T(8,128)(2,1)}, bf16[256,2048]{0,1:T(8,128)(2,1)}, u32[]{:S(2)}, u32[]{:S(2)}) collective-permute-start(bf16[256,2048]{0,1:T(8,128)(2,1)} %get-tuple-element.376), channel_id=1, source_target_pairs={{0,1},{1,2},{2,3},{3,0},{4,5},{5,6},{6,7},{7,4},{8,9},{9,10},{10,1... | collective-permute-start | bytes 3145736 | tf_op jit(solution)/shard_map/ppermute | solution.py:78
  256.6 38.2 %collective-permute-start.6 = (bf16[256,2048]{0,1:T(8,128)(2,1)S(1)}, bf16[256,2048]{0,1:T(8,128)(2,1)}, u32[]{:S(2)}, u32[]{:S(2)}) collective-permute-start(bf16[256,2048]{0,1:T(8,128)(2,1)S(1)} %get-tuple-element.378), channel_id=1, source_target_pairs={{0,1},{1,2},{2,3},{3,0},{4,5},{5,6},{6,7},{7,4},{8,9},{9,10},{10,1... | collective-permute-start | bytes 3145736 | tf_op jit(solution)/shard_map/ppermute | solution.py:78
  272.3 44.9 %collective-permute-start.10 = (bf16[256,2048]{0,1:T(8,128)(2,1)}, bf16[256,2048]{0,1:T(8,128)(2,1)}, u32[]{:S(2)}, u32[]{:S(2)}) collective-permute-start(bf16[256,2048]{0,1:T(8,128)(2,1)} %collective-permute-done.9), channel_id=1, source_target_pairs={{0,1},{1,2},{2,3},{3,0},{4,5},{5,6},{6,7},{7,4},{8,9},{9,10},{10,1... | collective-permute-start | bytes 3145736 | tf_op jit(solution)/shard_map/ppermute | solution.py:78
  294.8 44.9 %collective-permute-start.7 = (bf16[256,2048]{0,1:T(8,128)(2,1)}, bf16[256,2048]{0,1:T(8,128)(2,1)}, u32[]{:S(2)}, u32[]{:S(2)}) collective-permute-start(bf16[256,2048]{0,1:T(8,128)(2,1)} %collective-permute-done.6), channel_id=1, source_target_pairs={{0,1},{1,2},{2,3},{3,0},{4,5},{5,6},{6,7},{7,4},{8,9},{9,10},{10,1... | collective-permute-start | bytes 3145736 | tf_op jit(solution)/shard_map/ppermute | solution.py:78
  317.2 44.9 %collective-permute-start.11 = (bf16[256,2048]{0,1:T(8,128)(2,1)}, bf16[256,2048]{0,1:T(8,128)(2,1)}, u32[]{:S(2)}, u32[]{:S(2)}) collective-permute-start(bf16[256,2048]{0,1:T(8,128)(2,1)} %collective-permute-done.10), channel_id=1, source_target_pairs={{0,1},{1,2},{2,3},{3,0},{4,5},{5,6},{6,7},{7,4},{8,9},{9,10},{10,1... | collective-permute-start | bytes 3145736 | tf_op jit(solution)/shard_map/ppermute | solution.py:78
  339.7 38.0 %collective-permute-start.8 = (bf16[256,2048]{0,1:T(8,128)(2,1)}, bf16[256,2048]{0,1:T(8,128)(2,1)}, u32[]{:S(2)}, u32[]{:S(2)}) collective-permute-start(bf16[256,2048]{0,1:T(8,128)(2,1)} %collective-permute-done.7), channel_id=1, source_target_pairs={{0,1},{1,2},{2,3},{3,0},{4,5},{5,6},{6,7},{7,4},{8,9},{9,10},{10,1... | collective-permute-start | bytes 3145736 | tf_op jit(solution)/shard_map/ppermute | solution.py:78
  570.3 28.5 %collective-permute-start.17 = (bf16[256,2048]{0,1:T(8,128)(2,1)}, bf16[256,2048]{0,1:T(8,128)(2,1)}, u32[]{:S(2)}, u32[]{:S(2)}) collective-permute-start(bf16[256,2048]{0,1:T(8,128)(2,1)} %add_convert_fusion.2), channel_id=1, source_target_pairs={{0,1},{1,2},{2,3},{3,0},{4,5},{5,6},{6,7},{7,4},{8,9},{9,10},{10,1... | collective-permute-start | bytes 3145736 | tf_op jit(solution)/shard_map/ppermute | solution.py:98
  571.2 498.0 %reduce-scatter.11.cloned.1.call-start = ((), (), s32[]{:S(2)}) async-start(), calls=%async_computation.12 | async-start | bytes 2359296 | tf_op jit(solution)/shard_map/reduce_scatter | solution.py:452
  774.5 297.1 %reduce-scatter.9.cloned.1.call-start = ((), (), s32[]{:S(2)}) async-start(), calls=%async_computation.11 | async-start | bytes 7077888 | tf_op jit(solution)/shard_map/reduce_scatter | solution.py:446
  800.6 273.7 %reduce-scatter.13.cloned.1.call-start = ((), (), s32[]{:S(2)}) async-start(), calls=%async_computation.13 | async-start | bytes 18874368 | tf_op jit(solution)/shard_map/reduce_scatter | solution.py:350
  882.5 240.8 %reduce-scatter.15.cloned.1.call-start = ((), (), s32[]{:S(2)}) async-start(), calls=%async_computation.14 | async-start | bytes 18874368 | tf_op jit(solution)/shard_map/reduce_scatter | solution.py:350
  883.3 359.5 %reduce-scatter.17.cloned.1.call-start = ((), (), s32[]{:S(2)}) async-start(), calls=%async_computation.15 | async-start | bytes 18874368 | tf_op jit(solution)/shard_map/reduce_scatter | solution.py:350
  904.1 54.2 %collective-permute-start.21 = (bf16[256,2048]{0,1:T(8,128)(2,1)S(1)}, bf16[256,2048]{0,1:T(8,128)(2,1)S(1)}, u32[]{:S(2)}, u32[]{:S(2)}) collective-permute-start(bf16[256,2048]{0,1:T(8,128)(2,1)S(1)} %fusion.46), channel_id=1, source_target_pairs={{0,1},{1,2},{2,3},{3,0},{4,5},{5,6},{6,7},{7,4},{8,9},{9,10},{10,1... | collective-permute-start | bytes 3145736 | tf_op jit(solution)/shard_map/ppermute | solution.py:98
  904.6 52.2 %collective-permute-start.25 = (f32[17,2048]{1,0:T(8,128)S(1)}, f32[17,2048]{1,0:T(8,128)S(1)}, u32[]{:S(2)}, u32[]{:S(2)}) collective-permute-start(f32[17,2048]{1,0:T(8,128)S(1)} %fusion.109), channel_id=1, source_target_pairs={{0,2},{1,3},{2,0},{3,1},{4,6},{5,7},{6,4},{7,5},{8,10},{9,11},{10,... | collective-permute-start | bytes 417800 | tf_op jit(solution)/shard_map/ppermute | solution.py:111
  905.6 81.5 %collective-permute-start.12 = (bf16[256,2048]{0,1:T(8,128)(2,1)S(1)}, bf16[256,2048]{0,1:T(8,128)(2,1)S(1)}, u32[]{:S(2)}, u32[]{:S(2)}) collective-permute-start(bf16[256,2048]{0,1:T(8,128)(2,1)S(1)} %constant_dynamic-slice_fusion), channel_id=1, source_target_pairs={{0,1},{1,2},{2,3},{3,0},{4,5},{5,6},{6,7},{7,4},{8,9},{9,10},{10,1... | collective-permute-start | bytes 3145736 | tf_op jit(solution)/shard_map/ppermute | solution.py:98
  956.8 30.8 %collective-permute-start.26 = (f32[17,2048]{1,0:T(8,128)S(1)}, f32[17,2048]{1,0:T(8,128)S(1)}, u32[]{:S(2)}, u32[]{:S(2)}) collective-permute-start(f32[17,2048]{1,0:T(8,128)S(1)} %add.376), channel_id=1, source_target_pairs={{0,4},{4,0},{8,12},{12,8},{16,20},{20,16},{24,28},{28,24},{1,5},{5... | collective-permute-start | bytes 417800 | tf_op jit(solution)/shard_map/ppermute | solution.py:111
  987.5 50.0 %collective-permute-start.13 = (bf16[256,2048]{0,1:T(8,128)(2,1)S(1)}, bf16[256,2048]{0,1:T(8,128)(2,1)S(1)}, u32[]{:S(2)}, u32[]{:S(2)}) collective-permute-start(bf16[256,2048]{0,1:T(8,128)(2,1)S(1)} %add_convert_fusion.6), channel_id=1, source_target_pairs={{0,1},{1,2},{2,3},{3,0},{4,5},{5,6},{6,7},{7,4},{8,9},{9,10},{10,1... | collective-permute-start | bytes 3145736 | tf_op jit(solution)/shard_map/ppermute | solution.py:98
  987.6 28.7 %collective-permute-start.27 = (f32[17,2048]{1,0:T(8,128)S(1)}, f32[17,2048]{1,0:T(8,128)S(1)}, u32[]{:S(2)}, u32[]{:S(2)}) collective-permute-start(f32[17,2048]{1,0:T(8,128)S(1)} %add.377), channel_id=1, source_target_pairs={{0,8},{4,12},{8,0},{12,4},{16,24},{20,28},{24,16},{28,20},{1,9},{5... | collective-permute-start | bytes 417800 | tf_op jit(solution)/shard_map/ppermute | solution.py:111
  (108 other events, 3353.1 us)
Sparse Core Ops, SparseCore 0:
  10.5 57.0 all-gather.4
  69.5 89.8 all-gather.10
  161.3 89.8 all-gather.6
  253.0 89.8 all-gather.8
  571.3 24.2 reduce-scatter.6
  774.6 39.3 reduce-scatter.10
  817.8 61.7 reduce-scatter.8
  883.1 120.0 reduce-scatter.12
  1006.8 116.5 reduce-scatter.14
  1126.8 115.9 reduce-scatter.16

commit v2 on v1

v2 whole, which is shorter than its diff:
```python
import jax
import jax.numpy as jnp
from jax import lax
from jax.experimental import pallas as pl
from jax.experimental.pallas import tpu as pltpu
from jax.sharding import PartitionSpec as P

HEAD = 128
EXPERTS = 16


EPS = 1e-05
THETA = 10000.0
MASKED = -1e30
PRECISE = lax.Precision.HIGHEST


def rows_norm(values, gain):
    scale = lax.rsqrt(jnp.mean(values * values, axis=-1, keepdims=True) + EPS)
    normed = values * scale
    return (normed * gain, normed, scale)


def norm_back(grad_out, gain, normed, scale):
    grad_normed = grad_out * gain
    inner_mean = jnp.mean(grad_normed * normed, axis=-1, keepdims=True)
    return (scale * (grad_normed - normed * inner_mean), jnp.sum(grad_out * normed, axis=0))


def rotary_tables(length, width):
    half = width // 2
    freq = THETA ** (-(jnp.arange(half, dtype=jnp.float32) * 2.0) / width)
    angle = jnp.arange(length, dtype=jnp.float32)[:, None] * freq[None, :]
    return (jnp.cos(angle)[:, None, :], jnp.sin(angle)[:, None, :])


NN = (((1,), (0,)), ((), ()))
NT = (((1,), (1,)), ((), ()))


def dot32(left, right, dims=NN):
    return lax.dot_general(left, right, dims, preferred_element_type=jnp.float32)


def in_order(chunks, axis):
    n = lax.axis_size(axis)
    here = lax.axis_index(axis)
    rows = chunks[0].shape[0]
    full = jnp.zeros((n * rows,) + chunks[0].shape[1:], chunks[0].dtype)
    for step, chunk in enumerate(chunks):
        full = lax.dynamic_update_slice_in_dim(full, chunk, ((here - step) % n) * rows, 0)
    return full


def held_until(value, *others):
    return lax.optimization_barrier((value,) + others)[0]


def bits_of(n):
    return [1 << k for k in range(n.bit_length() - 1)]


def swap(value, axis, bit):
    n = lax.axis_size(axis)
    return lax.ppermute(value, axis, [(i, i ^ bit) for i in range(n)])


def cube_orders(axis):
    far = bits_of(lax.axis_size(axis))[1:]
    return [far, far[::-1]]


class CubeScatter:
    def __init__(self, stay, axis):
        self.axis = axis
        self.orders = [order[1:] for order in cube_orders(axis)]
        far = bits_of(lax.axis_size(axis))[1:]
        self.left = [[b for b in far[::-1] if b in order] for order in self.orders]
        self.pieces = [
            s.reshape(s.shape[:1] + (2,) * len(order) + s.shape[2:])
            for s, order in zip(stay, self.orders)
        ]

    def start(self):
        flying, stay = [], []
        for part, piece in enumerate(self.pieces):
            bit = self.orders[part].pop(0)
            place = 1 + self.left[part].index(bit)
            self.left[part].remove(bit)
            sent = lax.index_in_dim(piece, 1, place, keepdims=False).astype(jnp.bfloat16)
            flying.append(swap(sent, self.axis, bit))
            stay.append(lax.index_in_dim(piece, 0, place, keepdims=False))
        self.pieces = stay
        return flying

    def finish(self, arrived):
        self.pieces = [
            stay.astype(jnp.float32) + came.reshape(stay.shape).astype(jnp.float32)
            for stay, came in zip(self.pieces, arrived)
        ]

    def result(self):
        return jnp.concatenate(self.pieces)


def ring_hop(total, axis):
    n = lax.axis_size(axis)
    return lax.ppermute(total, axis, [(i, (i + 1) % n) for i in range(n)])


def all_sum(value, axes):
    flat = value.reshape(-1)
    for axis in axes:
        n = lax.axis_size(axis)
        if n & (n - 1):
            flat = lax.psum(flat, axis)
            continue
        for bit in bits_of(n):
            flat = flat + swap(flat, axis, bit)
    return flat.reshape(value.shape)


def together(*values):
    return lax.optimization_barrier(values)


def xor_blocks(value, axis):
    n = lax.axis_size(axis)
    here = lax.axis_index(axis)
    blocks = jnp.split(value, n, axis=1)
    for bit in bits_of(n):
        turned = (here // bit) % 2 == 1
        blocks = [jnp.where(turned, blocks[j ^ bit], blocks[j]) for j in range(n)]
    return jnp.concatenate(blocks, axis=1)


def same_core(axis):
    n = lax.axis_size(axis)
    return [list(range(0, n, 2)), list(range(1, n, 2))]


DOC_MOST = 512
TILE = 256


def key_span(tile):
    first = max(0, tile - (DOC_MOST + TILE - 2) // TILE)
    return first * TILE, (tile + 1 - first) * TILE


def rotary_full(length, width):
    cosine, sine = rotary_tables(length, width)
    cosine, sine = cosine[:, 0], sine[:, 0]
    return jnp.concatenate([cosine, cosine], axis=1), jnp.concatenate([-sine, sine], axis=1)


def row_sums(values):
    sums = jnp.sum(values, axis=1, keepdims=True)
    return jnp.broadcast_to(sums, (values.shape[0], 128)).T[:8]


def projections(chunks, weights, places, n, filled):
    count = len(chunks)
    rows, width = chunks[0].shape
    columns = weights.shape[2]
    f32, bf16 = jnp.float32, jnp.bfloat16
    before = [] if filled is None else list(filled)

    def kernel(place_ref, *refs):
        w_ref = refs[count]
        q_ref, k_ref, v_ref, s_ref = refs[-4:]
        for s in range(count):

            @pl.when(pl.program_id(0) == s)
            def _(s=s):
                x = refs[s][...]
                for i, out in enumerate((q_ref, k_ref)):
                    raw = dot32(x, w_ref[i])
                    out[...] = raw
                    s_ref[i] = row_sums(raw * raw)
                v_ref[...] = dot32(x, w_ref[2]).astype(bf16)

    out = pl.BlockSpec((rows, columns), lambda s, place: (place[s], 0))
    return pl.pallas_call(
        kernel,
        grid_spec=pltpu.PrefetchScalarGridSpec(
            num_scalar_prefetch=1,
            grid=(count,),
            in_specs=[
                pl.BlockSpec((rows, width), lambda s, place: (0, 0), pipeline_mode=pl.Buffered(1))
            ]
            * count
            + [
                pl.BlockSpec(
                    (3, width, columns), lambda s, place: (0, 0, 0), pipeline_mode=pl.Buffered(1)
                )
            ]
            + [pl.BlockSpec(memory_space=pl.ANY)] * len(before),
            out_specs=[out, out, out, pl.BlockSpec((2, 8, rows), lambda s, place: (0, 0, place[s]))],
        ),
        out_shape=[
            jax.ShapeDtypeStruct((n * rows, columns), f32),
            jax.ShapeDtypeStruct((n * rows, columns), f32),
            jax.ShapeDtypeStruct((n * rows, columns), bf16),
            jax.ShapeDtypeStruct((2, 8, n * rows), f32),
        ],
        input_output_aliases={2 + count + i: i for i in range(len(before))},
        compiler_params=pltpu.CompilerParams(vmem_limit_bytes=58 << 20),
        cost_estimate=pl.CostEstimate(
            flops=6 * count * rows * width * columns,
            transcendentals=0,
            bytes_accessed=6 * width * columns + count * rows * (2 * width + 10 * columns),
        ),
        name="projections",
    )(jnp.stack(places).astype(jnp.int32), *chunks, weights, *before)


def projection_back(raws, gaineds, value_low, scales, inner, weights, order):
    count = len(order)
    length, columns = value_low.shape
    rows = length // count
    width = weights.shape[1]
    f32, bf16 = jnp.float32, jnp.bfloat16

    def kernel(place_ref, qr, kr, qg, kg, v_ref, s_ref, i_ref, w_ref, ql, kl, out_ref):
        total = dot32(v_ref[...], w_ref[2], NT)
        for j, (raw, gained, low) in enumerate(((qr, qg, ql), (kr, kg, kl))):
            scale = s_ref[:, j : j + 1]
            value = scale * (gained[...] - raw[...] * scale * i_ref[:, j : j + 1])
            low[...] = value.astype(bf16)
            total += dot32(value.astype(bf16), w_ref[j], NT)
        out_ref[0] = total.astype(bf16)

    part = pl.BlockSpec((rows, columns), lambda s, place: (place[s], 0))
    pair = pl.BlockSpec((rows, 2), lambda s, place: (place[s], 0))
    low_shape = jax.ShapeDtypeStruct((length, columns), bf16)
    return pl.pallas_call(
        kernel,
        grid_spec=pltpu.PrefetchScalarGridSpec(
            num_scalar_prefetch=1,
            grid=(count,),
            in_specs=[part] * 5
            + [
                pair,
                pair,
                pl.BlockSpec(
                    (3, width, columns), lambda s, place: (0, 0, 0), pipeline_mode=pl.Buffered(1)
                ),
            ],
            out_specs=[part, part, pl.BlockSpec((1, rows, width), lambda s, place: (s, 0, 0))],
        ),
        out_shape=[low_shape, low_shape, jax.ShapeDtypeStruct((count, rows, width), bf16)],
        compiler_params=pltpu.CompilerParams(vmem_limit_bytes=58 << 20),
        cost_estimate=pl.CostEstimate(
            flops=6 * length * width * columns,
            transcendentals=0,
            bytes_accessed=6 * width * columns + length * (22 * columns + 2 * width),
        ),
        name="projection_back",
    )(jnp.stack(order).astype(jnp.int32), *raws, *gaineds, value_low, scales, inner, weights)


def pair_sum(first, second):
    block = pl.BlockSpec((1,) + first.shape[1:], lambda i: (i, 0, 0, 0))

    def kernel(a_ref, b_ref, out_ref):
        add_pair((a_ref, b_ref), (out_ref,))

    return pl.pallas_call(
        kernel,
        grid=(first.shape[0],),
        in_specs=[block, block],
        out_specs=block,
        out_shape=jax.ShapeDtypeStruct(first.shape, first.dtype),
        compiler_params=pltpu.CompilerParams(vmem_limit_bytes=58 << 20),
        cost_estimate=pl.CostEstimate(flops=first.size, transcendentals=0, bytes_accessed=6 * first.size),
        name="pair_sum",
    )(first, second)


def projection_grads(firsts, places, seconds, lows, axis):
    n = lax.axis_size(axis)
    count = len(firsts)
    chunk, width = firsts[0].shape
    rows, columns = lows[0].shape
    arrays = len(lows)
    block = width // n
    half = pl.BlockSpec((1, n // 2, block, columns), lambda i, place: (i, 0, 0, 0))
    shape = jax.ShapeDtypeStruct((arrays, n // 2, block, columns), jnp.bfloat16)

    def kernel(place_ref, *refs):
        low_refs = refs[2 * count : 2 * count + arrays]
        keep_ref, send_ref, turned = refs[-3:]
        i = pl.program_id(0)
        for begin, group in ((0, refs[:count]), (arrays - 1, refs[count : 2 * count])):

            @pl.when(i == begin)
            def _(group=group):
                for s in range(count):
                    at = pl.multiple_of(place_ref[s] * chunk, chunk)
                    turned[:, pl.ds(at, chunk)] = group[s][...].T

        for j in range(arrays):

            @pl.when(i == j)
            def _(j=j):
                for q in range(n // 2):
                    for out, side in ((keep_ref, place_ref[count]), (send_ref, 1 - place_ref[count])):
                        at = pl.multiple_of((2 * q + side) * block, block)
                        product = dot32(turned[pl.ds(at, block), :], low_refs[j][...])
                        out[0, q] = product.astype(jnp.bfloat16)

    def whole(shape):
        return pl.BlockSpec(shape, lambda i, place: (0, 0), pipeline_mode=pl.Buffered(1))

    return pl.pallas_call(
        kernel,
        grid_spec=pltpu.PrefetchScalarGridSpec(
            num_scalar_prefetch=1,
            grid=(arrays,),
            in_specs=[whole((chunk, width))] * (2 * count) + [whole((rows, columns))] * arrays,
            out_specs=[half, half],
            scratch_shapes=[pltpu.VMEM((width, rows), jnp.bfloat16)],
        ),
        out_shape=[shape, shape],
        compiler_params=pltpu.CompilerParams(vmem_limit_bytes=58 << 20),
        cost_estimate=pl.CostEstimate(
            flops=2 * arrays * rows * width * columns,
            transcendentals=0,
            bytes_accessed=4 * rows * width + 2 * arrays * columns * (width + rows),
        ),
        name="projection_grads",
    )(jnp.stack([*places, lax.axis_index(axis) % 2]).astype(jnp.int32), *firsts, *seconds, *lows)


def attention_forward(query_raw, key_raw, values, scales, gains, tables, marks):
    length, columns = query_raw.shape
    heads = columns // HEAD
    tiles = length // TILE
    f32, bf16 = jnp.float32, jnp.bfloat16
    widest = max(key_span(t)[1] for t in range(tiles))

    def kernel(q_ref, k_ref, v_ref, s_ref, g_ref, cos_ref, sin_ref, col_ref, row_ref, qo, ko, mo, bias):
        @pl.when(pl.program_id(0) == 0)
        def _():
            for t in range(tiles):
                start, width = key_span(t)
                rows = pl.ds(t * TILE, TILE)
                keys = pl.ds(start, width)
                same = col_ref[rows, 0:1] == row_ref[0:1, keys]
                query_at = t * TILE + lax.broadcasted_iota(jnp.int32, (TILE, width), 0)
                key_at = start + lax.broadcasted_iota(jnp.int32, (TILE, width), 1)
                live = (row_ref[1:2, keys] == 1) | (key_at == query_at)
                ok = same & (key_at <= query_at) & live
                bias[rows, 0:width] = jnp.where(ok, 0.0, MASKED)

        cosine, sine = cos_ref[...], sin_ref[...]
        for place, (raw, out) in enumerate(((q_ref, qo), (k_ref, ko))):
            unit = raw[...] * s_ref[:, place : place + 1] * g_ref[place : place + 1, :]
            out[...] = (unit * cosine + pltpu.roll(unit, HEAD // 2, 1) * sine).astype(bf16)
        for t in range(tiles):
            start, width = key_span(t)
            rows = pl.ds(t * TILE, TILE)
            keys = pl.ds(start, width)
            scores = dot32(qo[rows, :], ko[keys, :], NT) * HEAD ** (-0.5) + bias[rows, 0:width]
            raised = jnp.exp(scores - jnp.max(scores, axis=1, keepdims=True))
            probs = (raised * (1.0 / jnp.sum(raised, axis=1, keepdims=True))).astype(bf16)
            mo[rows, :] = dot32(probs, v_ref[keys, :]).astype(bf16)

    head = pl.BlockSpec((length, HEAD), lambda h: (0, h))

    def whole(shape):
        return pl.BlockSpec(shape, lambda h: (0, 0))

    low = jax.ShapeDtypeStruct((length, columns), bf16)
    return pl.pallas_call(
        kernel,
        grid=(heads,),
        in_specs=[
            head,
            head,
            head,
            whole((length, 2)),
            pl.BlockSpec((2, HEAD), lambda h: (0, h)),
            whole((length, HEAD)),
            whole((length, HEAD)),
            whole((length, 2)),
            whole((2, length)),
        ],
        out_specs=[head, head, head],
        out_shape=[low, low, low],
        scratch_shapes=[pltpu.VMEM((length, widest), f32)],
        compiler_params=pltpu.CompilerParams(vmem_limit_bytes=58 << 20),
        cost_estimate=pl.CostEstimate(
            flops=4 * length * widest * columns,
            transcendentals=heads * length * widest,
            bytes_accessed=16 * length * columns,
        ),
        name="attention_forward",
    )(query_raw, key_raw, values, scales, gains, *tables, marks.T, marks)


def attention_backward(
    query_rot, key_rot, values, grad_mixed, query_raw, key_raw, scales, gains, tables, marks, addends, axis
):
    length, columns = query_raw.shape
    heads = columns // HEAD
    tiles = length // TILE
    f32, bf16 = jnp.float32, jnp.bfloat16
    widest = max(key_span(t)[1] for t in range(tiles))
    tn = (((0,), (0,)), ((), ()))
    experts, blocks = addends[0].shape[:2]
    each = experts // heads
    part = pl.BlockSpec((each,) + addends[0].shape[1:], lambda h: (h, 0, 0, 0))
    fewer = (blocks // 2,) + addends[0].shape[2:]
    split_specs = [
        pl.BlockSpec((each,) + fewer, lambda h: (jnp.minimum(h, heads // 2 - 1), 0, 0, 0)),
        pl.BlockSpec((each,) + fewer, lambda h: (jnp.maximum(h - heads // 2, 0), 0, 0, 0)),
    ]
    firsts = [order[0] // 2 for order in cube_orders(axis)]

    def kernel(
        q_ref, k_ref, v_ref, m_ref, qr_ref, kr_ref, s_ref, g_ref, cos_ref, sin_ref, col_ref, row_ref, a_ref, b_ref,
        dq_out, dk_out, dv_out, inner_out, gain_out, stay_0, stay_1, send_0, send_1, bias, dq, dk, dv,
    ):
        h = pl.program_id(0)
        for p, (stay, send) in enumerate(((stay_0, send_0), (stay_1, send_1))):

            @pl.when((h >= heads // 2) == bool(p))
            def _(p=p, stay=stay, send=send):
                at = [0, 0]
                for m in range(blocks):
                    out = 1 if m & firsts[p] else 0
                    total = a_ref[:, m].astype(f32) + b_ref[:, m].astype(f32)
                    (stay, send)[out][:, at[out]] = total.astype(bf16)
                    at[out] += 1

        @pl.when(h == 0)
        def _():
            inner_out[...] = jnp.zeros_like(inner_out)
            for t in range(tiles):
                start, width = key_span(t)
                rows = pl.ds(t * TILE, TILE)
                keys = pl.ds(start, width)
                same = col_ref[keys, 0:1] == row_ref[0:1, rows]
                key_at = start + lax.broadcasted_iota(jnp.int32, (width, TILE), 0)
                query_at = t * TILE + lax.broadcasted_iota(jnp.int32, (width, TILE), 1)
                live = (col_ref[keys, 1:2] == 1) | (key_at == query_at)
                ok = same & (key_at <= query_at) & live
                bias[0:width, rows] = jnp.where(ok, 0.0, MASKED)

        dk[...] = jnp.zeros_like(dk)
        dv[...] = jnp.zeros_like(dv)
        for t in range(tiles):
            start, width = key_span(t)
            rows = pl.ds(t * TILE, TILE)
            keys = pl.ds(start, width)
            scores = dot32(k_ref[keys, :], q_ref[rows, :], NT) * HEAD ** (-0.5) + bias[0:width, rows]
            raised = jnp.exp(scores - jnp.max(scores, axis=0, keepdims=True))
            probs = raised * (1.0 / jnp.sum(raised, axis=0, keepdims=True))
            dv[keys, :] += dot32(probs.astype(bf16), m_ref[rows, :])
            grad_probs = dot32(v_ref[keys, :], m_ref[rows, :], NT)
            row_dot = jnp.sum(probs * grad_probs, axis=0, keepdims=True)
            grad_scores = (probs * (grad_probs - row_dot)).astype(bf16)
            dk[keys, :] += dot32(grad_scores, q_ref[rows, :])
            dq[rows, :] = dot32(grad_scores, k_ref[keys, :], tn)
        dv_out[...] = dv[...].astype(bf16)
        cosine, sine = cos_ref[...], sin_ref[...]
        for place, (grad, raw, out) in enumerate(((dq, qr_ref, dq_out), (dk, kr_ref, dk_out))):
            turned = grad[...] * HEAD ** (-0.5)
            turned = turned * cosine + pltpu.roll(turned * sine, HEAD // 2, 1)
            unit = raw[...] * s_ref[:, place : place + 1]
            gain_out[place : place + 1, :] = jnp.sum(turned * unit, axis=0, keepdims=True)
            gained = turned * g_ref[place : place + 1, :]
            out[...] = gained
            inner_out[place] += row_sums(gained * unit)

    head = pl.BlockSpec((length, HEAD), lambda h: (0, h))

    def whole(shape):
        return pl.BlockSpec(shape, lambda h: (0, 0))

    pair = pl.BlockSpec((2, HEAD), lambda h: (0, h))
    wide = jax.ShapeDtypeStruct((length, columns), f32)
    return pl.pallas_call(
        kernel,
        grid=(heads,),
        in_specs=[
            head,
            head,
            head,
            head,
            head,
            head,
            whole((length, 2)),
            pair,
            whole((length, HEAD)),
            whole((length, HEAD)),
            whole((length, 2)),
            whole((2, length)),
            part,
            part,
        ],
        out_specs=[head, head, head, pl.BlockSpec((2, 8, length), lambda h: (0, 0, 0)), pair]
        + split_specs * 2,
        out_shape=[
            wide,
            wide,
            jax.ShapeDtypeStruct((length, columns), bf16),
            jax.ShapeDtypeStruct((2, 8, length), f32),
            jax.ShapeDtypeStruct((2, columns), f32),
        ]
        + [jax.ShapeDtypeStruct((experts // 2,) + fewer, bf16)] * 4,
        scratch_shapes=[
            pltpu.VMEM((widest, length), f32),
            pltpu.VMEM((length, HEAD), f32),
            pltpu.VMEM((length, HEAD), f32),
            pltpu.VMEM((length, HEAD), f32),
        ],
        compiler_params=pltpu.CompilerParams(vmem_limit_bytes=58 << 20),
        cost_estimate=pl.CostEstimate(
            flops=10 * length * widest * columns,
            transcendentals=heads * length * widest,
            bytes_accessed=26 * length * columns,
        ),
        name="attention_backward",
    )(
        query_rot, key_rot, values, grad_mixed, query_raw, key_raw, scales, gains, *tables, marks.T, marks, *addends
    )


def moe_first(xs, fs, weight, arrays, filled, first, total, side):
    count = len(xs)
    chunk, width = xs[0].shape
    rows = count * chunk
    parted = [isinstance(a, list) for a in arrays]
    experts = weight.shape[1]
    pieces = [a if p else [(0, experts, 0, [a])] for a, p in zip(arrays, parted)]
    hidden = pieces[0][0][3][0].shape[-1]
    step = 2 if any(parted) else (4 if count == 1 else 1)
    bf16 = jnp.bfloat16
    before = [] if filled is None else list(filled)
    flat = [(i, *group) for i, groups in enumerate(pieces) for group in groups]
    sizes = [len(entry[-1]) for entry in flat]

    def kernel(side_ref, *refs):
        x_refs, f_refs, w_ref = refs[:count], refs[count : 2 * count], refs[2 * count]
        at = 2 * count + 1
        groups = []
        for size in sizes:
            groups.append(refs[at : at + size])
            at += size
        outs = refs[at + len(before) :]
        dx_ref, gp_ref, wh_ref, dg_ref, du_ref, acc = *outs[:5], outs[-1]
        made = list(outs[5:-1])
        s = pl.program_id(0)
        ready = []
        for i in range(3):
            if not parted[i]:
                ready.append(next(g[0] for g, entry in zip(groups, flat) if entry[0] == i))
                continue
            target = made.pop(0)
            ready.append(target)
            mine = [(g, *entry[1:]) for g, entry in zip(groups, flat) if entry[0] == i]
            for refs_in, begin, held, _, blocks in mine:

                @pl.when((s * step >= begin) & (s * step < begin + held))
                def _(refs_in=refs_in, blocks=blocks, target=target, i=i):
                    high = blocks[0].shape[1]
                    for m in range(len(blocks)):
                        place = 0 if len(blocks) == 1 else (side_ref[i] ^ m) * high
                        place = 0 if len(blocks) == 1 else pl.multiple_of(place, high)
                        target[:, pl.ds(place, high), :] = refs_in[m][...]

        g_ref, u_ref, d_ref = ready

        @pl.when(s == 0)
        def _():
            acc[...] = jnp.zeros_like(acc)
            gp_ref[...] = jnp.zeros_like(gp_ref)

        lane = lax.broadcasted_iota(jnp.int32, (chunk, experts), 1)
        for r in range(count):
            rs = pl.ds(r * chunk, chunk)
            x, f = x_refs[r][...], f_refs[r][...]
            dx = None
            for j in range(step):
                e = s * step + j
                w = jnp.sum(jnp.where(lane == e, w_ref[rs, :], 0.0), axis=1, keepdims=True)
                gate_pre = dot32(x, g_ref[j])
                up_pre = dot32(x, u_ref[j])
                projected = dot32(f, d_ref[j])
                sig = 1.0 / (1.0 + jnp.exp(-gate_pre))
                act = gate_pre * sig
                hidden_f = act * up_pre
                wh_ref[j, rs, :] = (w * hidden_f).astype(bf16)
                inner = jnp.sum(hidden_f * projected, axis=1, keepdims=True)
                gp_ref[rs, :] = jnp.where(lane == e, inner, gp_ref[rs, :])
                grad_hidden = w * projected
                dg = (grad_hidden * up_pre * (sig + act * (1.0 - sig))).astype(bf16)
                du = (grad_hidden * act).astype(bf16)
                dg_ref[j, rs, :] = dg
                du_ref[j, rs, :] = du
                term = dot32(dg, g_ref[j], NT) + dot32(du, u_ref[j], NT)
                dx = term if dx is None else dx + term
            acc[rs, :] += dx

        @pl.when(s == experts // step - 1)
        def _():
            dx_ref[...] = acc[...].astype(bf16)

    def whole(shape):
        return pl.BlockSpec(shape, lambda s, side: (0, 0), pipeline_mode=pl.Buffered(1))

    def block_of(block, begin, held, base):
        return pl.BlockSpec(
            (step,) + block.shape[1:],
            lambda s, side: (base // step + jnp.clip(s - begin // step, 0, held // step - 1), 0, 0),
        )

    w_spec = pl.BlockSpec((step, width, hidden), lambda s, side: (s, 0, 0))
    h_spec = pl.BlockSpec((step, rows, hidden), lambda s, side: (s, first // count, 0))
    kept = jax.ShapeDtypeStruct((experts, total, hidden), bf16)
    blocks_in = [block for entry in flat for block in entry[-1]]
    made_count = sum(parted)
    return pl.pallas_call(
        kernel,
        grid_spec=pltpu.PrefetchScalarGridSpec(
            num_scalar_prefetch=1,
            grid=(experts // step,),
            in_specs=[whole((chunk, width))] * (2 * count)
            + [whole((rows, experts))]
            + [block_of(block, *entry[1:-1]) for entry in flat for block in entry[-1]]
            + [pl.BlockSpec(memory_space=pl.ANY)] * len(before),
            out_specs=[
                pl.BlockSpec((rows, width), lambda s, side: (0, 0)),
                pl.BlockSpec((rows, experts), lambda s, side: (0, 0)),
                h_spec,
                h_spec,
                h_spec,
            ]
            + [w_spec] * made_count,
            scratch_shapes=[pltpu.VMEM((rows, width), jnp.float32)],
        ),
        out_shape=[
            jax.ShapeDtypeStruct((rows, width), bf16),
            jax.ShapeDtypeStruct((rows, experts), jnp.float32),
            kept,
            kept,
            kept,
        ]
        + [jax.ShapeDtypeStruct((experts, width, hidden), bf16)] * made_count,
        input_output_aliases={
            2 + 2 * count + len(blocks_in) + i: 2 + i for i in range(len(before))
        },
        compiler_params=pltpu.CompilerParams(vmem_limit_bytes=58 << 20),
        cost_estimate=pl.CostEstimate(
            flops=10 * rows * width * hidden * experts,
            transcendentals=rows * hidden * experts,
            bytes_accessed=6 * experts * hidden * (width + rows) + 12 * rows * width,
        ),
        name="moe_first",
    )(side, *xs, *fs, weight, *blocks_in, *before)


def add_pair(adds, sums):
    for out in sums:
        total = adds[0][...].astype(jnp.float32) + adds[1][...].astype(jnp.float32)
        out[...] = total.astype(out.dtype)


def moe_grad_split(xs, kept, axis, side, addends=()):
    chunk, width = xs[0].shape
    experts, tokens, hidden = kept.shape
    n = lax.axis_size(axis)
    block = width // n
    count = len(xs)

    def kernel(side_ref, *refs):
        h_ref, *adds = refs[count : count + 1 + len(addends)]
        keep_ref, send_ref, *sums, turned = refs[count + 1 + len(addends) :]
        add_pair(adds, sums)

        @pl.when(pl.program_id(0) == 0)
        def _():
            for r in range(count):
                turned[:, r * chunk : (r + 1) * chunk] = refs[r][...].T

        mine = side_ref[0]
        for q in range(n // 2):
            for out, side in ((keep_ref, mine), (send_ref, 1 - mine)):
                at = pl.multiple_of((2 * q + side) * block, block)
                out[0, q] = dot32(turned[pl.ds(at, block), :], h_ref[0]).astype(jnp.bfloat16)

    half = pl.BlockSpec((1, n // 2, block, hidden), lambda e, side: (e, 0, 0, 0))
    shape = jax.ShapeDtypeStruct((experts, n // 2, block, hidden), jnp.bfloat16)
    return pl.pallas_call(
        kernel,
        grid_spec=pltpu.PrefetchScalarGridSpec(
            num_scalar_prefetch=1,
            grid=(experts,),
            in_specs=[
                pl.BlockSpec((chunk, width), lambda e, side: (0, 0), pipeline_mode=pl.Buffered(1))
            ]
            * count
            + [pl.BlockSpec((1, tokens, hidden), lambda e, side: (e, 0, 0))]
            + [half] * len(addends),
            out_specs=[half, half] + [half] * (len(addends) // 2),
            scratch_shapes=[pltpu.VMEM((width, tokens), jnp.bfloat16)],
        ),
        out_shape=[shape, shape] + [shape] * (len(addends) // 2),
        compiler_params=pltpu.CompilerParams(vmem_limit_bytes=58 << 20),
        cost_estimate=pl.CostEstimate(
            flops=2 * tokens * width * hidden * experts,
            transcendentals=0,
            bytes_accessed=2 * experts * hidden * (width + tokens) + 2 * tokens * width,
        ),
        name="moe_grad_split",
    )(jnp.asarray(side, jnp.int32).reshape(1), *xs, kept, *addends)


def moe_out(wh, down_all):
    experts, tokens, hidden = wh.shape
    width = down_all.shape[1]

    def kernel(h_ref, d_ref, out_ref, acc):
        e = pl.program_id(0)

        @pl.when(e == 0)
        def _():
            acc[...] = jnp.zeros_like(acc)

        acc[...] += dot32(h_ref[0], d_ref[0], NT)

        @pl.when(e == experts - 1)
        def _():
            out_ref[...] = acc[...].astype(jnp.bfloat16)

    return pl.pallas_call(
        kernel,
        grid=(experts,),
        in_specs=[
            pl.BlockSpec((1, tokens, hidden), lambda e: (e, 0, 0)),
            pl.BlockSpec((1, width, hidden), lambda e: (e, 0, 0)),
        ],
        out_specs=pl.BlockSpec((tokens, width), lambda e: (0, 0)),
        out_shape=jax.ShapeDtypeStruct((tokens, width), jnp.bfloat16),
        scratch_shapes=[pltpu.VMEM((tokens, width), jnp.float32)],
        compiler_params=pltpu.CompilerParams(vmem_limit_bytes=58 << 20),
        cost_estimate=pl.CostEstimate(
            flops=2 * tokens * width * hidden * experts,
            transcendentals=0,
            bytes_accessed=2 * experts * hidden * (width + tokens) + 2 * tokens * width,
        ),
        name="moe_out",
    )(wh, down_all)


def on_device(
    tokens,
    segments,
    valid,
    routes,
    cotangent,
    query_weight,
    key_weight,
    value_weight,
    output_weight,
    attn_norm_gain,
    expert_norm_gain,
    query_norm_gain,
    key_norm_gain,
    router_weight,
    gate_weight,
    up_weight,
    down_weight,
):
    f32 = jnp.float32
    bf16 = jnp.bfloat16
    local_x = tokens[0].astype(f32)
    rows_here, model_width = local_x.shape
    route_all = routes[0]
    length = segments.shape[1]
    here = lax.axis_index("tensor")
    around = lax.axis_size("tensor")
    ring_chunks = [(here - step) % around for step in range(around)]

    def rows_of(array, chunk):
        return lax.dynamic_slice_in_dim(array, chunk * rows_here, rows_here, 0)

    def hop(value):
        return ring_hop(value, "tensor")

    own_side = lax.axis_index("dp") % 2
    own_final = cotangent[0].astype(f32) * rows_of(valid[0], here).astype(f32)[:, None]

    attn_all = lax.all_gather(
        jnp.stack([query_weight, key_weight, value_weight, output_weight]), "dp", axis=1, tiled=True
    )
    query_w, key_w, value_w, output_w = (attn_all[i] for i in range(4))
    experts = down_weight.shape[0]
    half = experts // 2
    bits = bits_of(lax.axis_size("dp"))
    exchanged = [
        {0: jnp.concatenate([w[at : at + half] for w in (gate_weight, up_weight, down_weight)])}
        for at in (0, half)
    ]
    far_orders = cube_orders("dp")

    def exchange_far(stage):
        for pieces, order in zip(exchanged, far_orders):
            for mask in list(pieces):
                pieces[mask ^ order[stage]] = swap(pieces[mask], "dp", order[stage])

    def exchange_near():
        for pieces in exchanged:
            for mask in list(pieces):
                if mask ^ 1 not in pieces and not mask & 1:
                    pieces[mask ^ 1] = swap(pieces[mask], "dp", 1)

    def exchange_with(*values):
        leaves, tree = jax.tree.flatten(exchanged)
        out = together(*values, *leaves)
        exchanged[:] = jax.tree.unflatten(tree, out[len(values) :])
        return out[: len(values)]

    head_offset = here * query_w.shape[1]
    gain_attn = attn_norm_gain.astype(f32)
    gain_expert = expert_norm_gain.astype(f32)
    norm_gains = jnp.stack(
        [
            lax.dynamic_slice_in_dim(gain.astype(f32), head_offset, query_w.shape[1])
            for gain in (query_norm_gain, key_norm_gain)
        ]
    )
    normed1, unit1, scale1 = rows_norm(local_x, gain_attn)
    normed1_ring = [normed1.astype(bf16)]
    exchange_far(0)
    for _ in range(1, around):
        normed1_ring.append(hop(normed1_ring[-1]))
    normed1_ring[-2], attn_all = together(normed1_ring[-2], attn_all)
    projected = projections(normed1_ring[:-1], attn_all, ring_chunks[:-1], around, None)
    normed1_ring[-1], *projected = exchange_with(normed1_ring[-1], *projected)
    first_pieces = [dict(pieces) for pieces in exchanged]
    for stage in range(1, len(far_orders[0])):
        exchange_far(stage)
    query_raw, key_raw, value_heads, squares = projections(
        normed1_ring[-1:], attn_all, ring_chunks[-1:], around, projected
    )
    squares = all_sum(squares[:, 0], ("tensor",))
    final_ring = [held_until(xor_blocks(own_final.astype(bf16), "dp"), squares)]
    final_ring.append(hop(final_ring[0]))
    norm_scales = lax.rsqrt(squares / model_width + EPS).T
    tables = rotary_full(length, HEAD)
    marks = jnp.stack([segments[0], valid[0]])
    query_rot, key_rot, mixed_heads = attention_forward(
        query_raw, key_raw, value_heads, norm_scales, norm_gains, tables, marks
    )
    mixed_heads, final_ring[-1] = together(mixed_heads, final_ring[-1])
    for pieces, early in zip(exchanged, first_pieces):
        for mask, piece in early.items():
            pieces[mask ^ 1] = swap(held_until(piece, mixed_heads), "dp", 1)
    attn_local = dot32(rows_of(mixed_heads, (here - 1) % around), output_w, NT)
    for step in range(1, around):
        moved = hop(attn_local.astype(bf16))
        if step + 1 == around:
            (moved,) = exchange_with(moved)
            exchange_near()
        attn_local = moved.astype(f32) + dot32(
            rows_of(mixed_heads, (here - 1 - step) % around), output_w, NT
        )
    resid = local_x + attn_local
    normed2, unit2, scale2 = rows_norm(resid, gain_expert)

    normed2_ring = [normed2.astype(bf16)]
    router_f = router_weight.astype(f32)
    probs_ring, routed_ring, dx_ring, gate_grad_ring = [], [], [], []
    kept = None
    total = total_gate = None
    arrays = [
        [
            (part * half, half, i * half, [pieces[mask] for mask in sorted(pieces)])
            for part, pieces in enumerate(exchanged)
        ]
        for i in range(3)
    ]
    here_dp = lax.axis_index("dp")
    sides = jnp.stack([here_dp, here_dp, jnp.zeros_like(here_dp)]).astype(jnp.int32)
    for call in [[s] for s in range(around)]:
        last = call[-1]
        if last + 1 < around:
            normed2_ring.append(hop(normed2_ring[last]))
        if len(final_ring) < around:
            final_ring.append(hop(held_until(final_ring[-1], normed2_ring[last])))
        for s in call:
            probs_ring.append(jax.nn.softmax(dot32(normed2_ring[s], router_weight), axis=-1))
            route = rows_of(route_all, ring_chunks[s])
            routed_ring.append(
                jnp.any(route[:, :, None] == jnp.arange(EXPERTS, dtype=jnp.int32), axis=1)
            )
        weights = jnp.concatenate(
            [jnp.where(routed_ring[s], probs_ring[s], 0.0) for s in call]
        )
        if last >= 2:
            sent = dx_ring[last - 1] if total is None else (total + dx_ring[last - 1]).astype(bf16)
            sent_gate = gate_grad_ring[last - 1] if total is None else total_gate + gate_grad_ring[last - 1]
            moved, moved_gate = hop(sent), hop(sent_gate)
        outs = moe_first(
            [normed2_ring[s] for s in call],
            [final_ring[s] for s in call],
            weights,
            arrays,
            kept,
            call[0],
            length,
            sides,
        )
        waiting = [normed2_ring[-1], final_ring[-1]] + ([moved, moved_gate] if last >= 2 else [])
        held = together(*outs, *waiting)
        outs, waiting = held[: len(outs)], held[len(outs) :]
        normed2_ring[-1], final_ring[-1] = waiting[:2]
        if last >= 2:
            total, total_gate = waiting[2].astype(f32), waiting[3]
        for i, s in enumerate(call):
            dx_ring.append(outs[0][i * rows_here : (i + 1) * rows_here])
            grads = jnp.where(routed_ring[s], outs[1][i * rows_here : (i + 1) * rows_here], 0.0)
            gate_grad_ring.append(grads.T.reshape(-1))
        kept = outs[2:5]
        if len(outs) > 5:
            arrays = outs[5:]
    weighted_hidden, grad_gpre, grad_upre = kept
    down_all = arrays[2]
    sent = (total + dx_ring[around - 1]).astype(bf16)
    sent_gate = total_gate + gate_grad_ring[around - 1]
    moved, moved_gate = hop(sent), hop(sent_gate)
    gate_keep, gate_send = moe_grad_split(
        normed2_ring, held_until(grad_gpre, sent), "dp", own_side
    )
    moved, moved_gate, gate_keep, gate_send = together(moved, moved_gate, gate_keep, gate_send)
    gate_moved = swap(gate_send, "dp", 1)
    normed2_grad = moved.astype(f32) + dx_ring[0].astype(f32)
    prob_grad = (moved_gate + gate_grad_ring[0]).reshape(EXPERTS, rows_here).T
    probs_here = probs_ring[0]
    grad_logits = probs_here * (prob_grad - jnp.sum(probs_here * prob_grad, axis=1, keepdims=True))
    normed2_grad = normed2_grad + jnp.dot(
        grad_logits, router_f.T, precision=PRECISE, preferred_element_type=f32
    )
    resid_norm_grad, grad_expert_part = norm_back(normed2_grad, gain_expert, unit2, scale2)
    grad_resid = own_final + resid_norm_grad

    def reduce_rows(value):
        return lax.psum_scatter(
            value.reshape(value.shape[0], -1, value.shape[-1]),
            "dp",
            scatter_dimension=1,
            tiled=True,
            axis_index_groups=same_core("dp"),
        )

    resid_ring = [grad_resid.astype(bf16)]
    moved = hop(resid_ring[0])
    up_keep, up_send, gate_sum = moe_grad_split(
        normed2_ring, held_until(grad_upre, resid_ring[0]), "dp", own_side, (gate_keep, gate_moved)
    )
    moved, up_keep, up_send, gate_sum = together(moved, up_keep, up_send, gate_sum)
    resid_ring.append(moved)
    reduced_gate = reduce_rows(gate_sum)
    up_moved = swap(up_send, "dp", 1)
    moved = hop(resid_ring[1])
    moe_part = moe_out(held_until(weighted_hidden, up_keep), down_all)
    moved, moe_part, up_moved = together(moved, moe_part, up_moved)
    resid_ring.append(moved)
    for step in range(3, around):
        resid_ring.append(hop(resid_ring[-1]))
    down_keep, down_send, up_sum = moe_grad_split(
        final_ring, held_until(weighted_hidden, moe_part), "dp", 0, (up_keep, up_moved)
    )
    resid_ring[-1], down_keep, down_send, up_sum = together(
        resid_ring[-1], down_keep, down_send, up_sum
    )
    reduced_up = reduce_rows(up_sum)
    down_moved = swap(down_send, "dp", 1)
    resid_full = in_order(resid_ring, "tensor")
    grad_mixed = dot32(resid_full, output_w).astype(bf16)
    moe_local = moe_part[rows_here : 2 * rows_here].astype(f32)
    moe_moved = hop(held_until(moe_local.astype(bf16), resid_full))
    tn = (((0,), (0,)), ((), ()))
    query_gained, key_gained, value_low, inner_part, gain_grads, *down_split = attention_backward(
        query_rot,
        key_rot,
        value_heads,
        grad_mixed,
        query_raw,
        key_raw,
        norm_scales,
        norm_gains,
        tables,
        marks,
        (down_keep, down_moved),
        "dp",
    )
    query_gained, key_gained, inner_part, reduced_gate, moe_moved, *down_split = together(
        query_gained, key_gained, inner_part, reduced_gate, moe_moved, *down_split
    )
    down_cube = CubeScatter(down_split[:2], "dp")
    down_flying = [
        swap(sent, "dp", order[0]) for sent, order in zip(down_split[2:], cube_orders("dp"))
    ]
    moe_local = moe_moved.astype(f32) + moe_part[2 * rows_here : 3 * rows_here].astype(f32)
    moe_moved = hop(moe_local.astype(bf16))
    inner_sums = all_sum(inner_part[:, 0], ("tensor",)).T / model_width
    back_order = [(here - 1 - step) % around for step in range(around)]
    query_raw_low, key_raw_low, normed1_parts = projection_back(
        (query_raw, key_raw),
        (query_gained, key_gained),
        value_low,
        norm_scales,
        inner_sums,
        attn_all,
        back_order,
    )
    first = normed1_parts[0]
    moved = hop(first)
    attn_keep, attn_send = projection_grads(
        normed1_ring,
        ring_chunks,
        resid_ring,
        [query_raw_low, key_raw_low, value_low, held_until(mixed_heads, first)],
        "dp",
    )
    moved, attn_keep, attn_send, moe_moved, *down_flying = together(
        moved, attn_keep, attn_send, moe_moved, *down_flying
    )
    attn_moved = swap(attn_send, "dp", 1)
    down_cube.finish(down_flying)
    while down_cube.orders[0]:
        down_cube.finish(down_cube.start())
    for step in range(1, around):
        normed1_grad = moved.astype(f32) + normed1_parts[step].astype(f32)
        if step + 1 < around:
            moved = hop(normed1_grad.astype(bf16))
        if step == 1:
            attn_sum = pair_sum(attn_keep, attn_moved)
            moved, attn_sum = together(moved, attn_sum)
            reduced_attn = reduce_rows(attn_sum)
    normed1_grad, reduced_up = together(normed1_grad, reduced_up)
    moe_local = moe_moved.astype(f32) + moe_part[3 * rows_here :].astype(f32)
    moe_moved = hop(held_until(moe_local.astype(bf16), normed1_grad))
    layer_local = resid + xor_blocks(moe_moved.astype(f32) + moe_part[:rows_here].astype(f32), "dp")
    layer_local = layer_local.astype(bf16)
    reduced_down = down_cube.result()
    grad_router_part = lax.dot_general(
        normed2_ring[0].astype(f32), grad_logits, tn, precision=PRECISE, preferred_element_type=f32
    )
    input_norm_grad, grad_attn_part = norm_back(normed1_grad, gain_attn, unit1, scale1)
    grad_input = grad_resid + input_norm_grad
    gains_full = lax.dynamic_update_slice(
        jnp.zeros((2, model_width), f32), gain_grads, (0, head_offset)
    )
    sums = all_sum(
        jnp.concatenate(
            [grad_router_part.T, grad_expert_part[None], gains_full, grad_attn_part[None]]
        ),
        ("tensor", "dp"),
    )
    return (
        layer_local[None],
        grad_input[None],
        reduced_attn[0].astype(f32),
        reduced_attn[1].astype(f32),
        reduced_attn[2].astype(f32),
        reduced_attn[3].astype(f32),
        reduced_gate.astype(f32),
        reduced_up.astype(f32),
        reduced_down,
        sums[:EXPERTS].T,
        sums[EXPERTS + 3],
        sums[EXPERTS],
        sums[EXPERTS + 1],
        sums[EXPERTS + 2],
    )


def solution(mesh):
    in_specs = (
        P("dp", "tensor", None),
        P("dp", None),
        P("dp", None),
        P("dp", None, None),
        P("dp", "tensor", None),
        P("dp", "tensor"),
        P("dp", "tensor"),
        P("dp", "tensor"),
        P("dp", "tensor"),
        P(),
        P(),
        P(),
        P(),
        P(),
        P(None, "dp", "tensor"),
        P(None, "dp", "tensor"),
        P(None, "dp", "tensor"),
    )
    out_specs = (
        P("dp", "tensor", None),
        P("dp", "tensor", None),
        P("dp", "tensor"),
        P("dp", "tensor"),
        P("dp", "tensor"),
        P("dp", "tensor"),
        P(None, "dp", "tensor"),
        P(None, "dp", "tensor"),
        P(None, "dp", "tensor"),
        P(),
        P(),
        P(),
        P(),
        P(),
    )
    return jax.shard_map(
        on_device, mesh=mesh, in_specs=in_specs, out_specs=out_specs, check_vma=False
    )
```

time: 1260 us -> 949 us (0.75)
  waiting for transfers between devices: 675 us -> 351 us
  Pallas kernels: 200 us -> 386 us
  matrix products: 114 us -> 28 us
  local copies, waits for them, and re-layouts: 107 us -> 26.8 us
  starting transfers between devices: 20.6 us -> 49.1 us
  blocking collectives: 17.2 us -> 0 us
    pallas_call x2 -> x15, Pallas kernels: 200 us -> 386 us  [the longest x4 169 us: moe_first(): pl.pallas_call(kernel, grid_spec=pltpu.PrefetchScalarGridSpec(num_scalar_...]
    reduce_scatter x6 -> x3, waiting for transfers between devices: 185 us -> 0.02 us  [reduce_rows(): lax.psum_scatter(value.reshape(value.shape[0], -1, value.shape[-1]), 'dp'...]
    ppermute x34 -> x58, waiting for transfers between devices: 488 us -> 319 us  [the longest x31 182 us: swap(): return lax.ppermute(value, axis, [(i, i ^ bit) for i in range(n)])]
    dot_general x24 -> x1, matrix products: 85.2 us -> 1.37 us  [on_device(): lax.dot_general(normed2_ring[0].astype(f32), grad_logits, tn, precision=P...]
    dynamic_update_slice x14 -> x3, local copies, waits for them, and re-layouts: 36.7 us -> 3.13 us  [in_order(): lax.dynamic_update_slice_in_dim(full, chunk, (here - step) % n * rows, 0)]
    all_gather x1, waiting for transfers between devices: 0.01 us -> 31.2 us  [on_device(): lax.all_gather(jnp.stack([query_weight, key_weight, value_weight, output_...]
    ppermute x34 -> x58, starting transfers between devices: 20 us -> 48.9 us  [the longest x31 26.9 us: swap(): return lax.ppermute(value, axis, [(i, i ^ bit) for i in range(n)])]
    unnamed x153 -> x110, local copies, waits for them, and re-layouts: 23.5 us -> 4.53 us
  transfers between devices with their start and end apart: 44 -> 62, of which waited for: 27 -> 31; matrix products, arithmetic and copies ran while one was open for 16% -> 13% of each run, Pallas kernels for 7% -> 40%
where the time goes in v2:
time: 949 us; the launch traced here: 939 us
  Pallas kernels  386 us (41%)
  waiting for transfers between devices  351 us (37%)
  other arithmetic  84.1 us (9%)
  starting transfers between devices  49.1 us (5%)
  matrix products  28 us (3%)
  local copies, waits for them, and re-layouts  26.8 us (3%)
  between operations  15 us (2%)
    ppermute x31, waiting for transfers between devices, swap(): return lax.ppermute(value, axis, [(i, i ^ bit) for i in range(n)])  182 us
    pallas_call x4, Pallas kernels, moe_first(): pl.pallas_call(kernel, grid_spec=pltpu.PrefetchScalarGridSpec(num_scalar_...  169 us
    ppermute x27, waiting for transfers between devices, ring_hop(): return lax.ppermute(total, axis, [(i, (i + 1) % n) for i in range(n)])  137 us
    pallas_call x3, Pallas kernels, moe_grad_split(): pl.pallas_call(kernel, grid_spec=pltpu.PrefetchScalarGridSpec(num_scalar_...  90 us
    all_gather x1, waiting for transfers between devices, on_device(): lax.all_gather(jnp.stack([query_weight, key_weight, value_weight, output_...  31.2 us
    pallas_call x1, Pallas kernels, attention_backward(): pl.pallas_call(kernel, grid=(heads,), in_specs=[head, head, head, head, h...  29.4 us
    pallas_call x1, Pallas kernels, moe_out(): pl.pallas_call(kernel, grid=(experts,), in_specs=[pl.BlockSpec((1, tokens...  27 us
    ppermute x31, starting transfers between devices, swap(): return lax.ppermute(value, axis, [(i, i ^ bit) for i in range(n)])  26.9 us
  transfers between devices with their start and end apart: 62, of which 31 were waited for; matrix products, arithmetic and copies ran while one was open for 13% of the time, Pallas kernels for 40%

profile of v2, /device:TPU:0, one launch (start us, length us, event | category | flops | bytes accessed | tf_op | source)
XLA Modules:
  0.0 939.5 jit_solution(2789052870583066320)
XLA Ops:
  22.9 17.1 %collective-permute-done.refs_1_ = bf16[256,2048]{1,0:T(8,128)(2,1)} collective-permute-done((bf16[256,2048]{1,0:T(8,128)(2,1)}, bf16[256,2048]{1,0:T(8,128)(2,1)}, u32[]{:S(2)}, u32[]{:S(2)}) %collective-permute-start) | collective-permute-done | bytes 1048608 | tf_op jit(solution)/shard_map/ppermute | solution.py:108
  46.4 20.0 %collective-permute-done.1.refs_2_ = bf16[256,2048]{1,0:T(8,128)(2,1)} collective-permute-done((bf16[256,2048]{1,0:T(8,128)(2,1)}, bf16[256,2048]{1,0:T(8,128)(2,1)}, u32[]{:S(2)}, u32[]{:S(2)}) %collective-permute-start.1) | collective-permute-done | bytes 1048608 | tf_op jit(solution)/shard_map/ppermute | solution.py:108
  70.4 31.2 %all-gather.2.cloned.1.call-done.refs_3_.refs_1_.w_ref = bf16[4,2048,512]{2,1,0:T(8,128)(2,1)} async-done(((bf16[4,256,512]{2,1,0:T(8,128)(2,1)}), bf16[4,2048,512]{2,1,0:T(8,128)(2,1)}) %all-gather.2.cloned.1.call-update) | async-done | bytes 8388624 | tf_op jit(solution)/shard_map/all_gather | solution.py:797
  101.6 11.1 %projections.2 = (f32[1024,512]{1,0:T(8,128)}, f32[1024,512]{1,0:T(8,128)}, bf16[1024,512]{1,0:T(8,128)(2,1)}, f32[2,8,1024]{2,1,0:T(8,128)}) custom-call(s32[3]{0:T(128)} %pad_add_fusion.1.place_ref, bf16[256,2048]{1,0:T(8,128)(2,1)} %fusion.4.refs_0_, bf16[256,2048]{1,0:T(8,128)(2,1)} %collective-permute-done.refs_1_, ...), custom_call_target="tpu_custom_call" | custom-call | flops 4831838208 | bytes 13369344 | tf_op jit(solution)/shard_map/projections/pallas_call | solution.py:184
  150.8 14.9 %attention_forward.1 = (bf16[1024,512]{1,0:T(8,128)(2,1)}, bf16[1024,512]{1,0:T(8,128)(2,1)}, bf16[1024,512]{1,0:T(8,128)(2,1)}) custom-call(f32[1024,512]{1,0:T(8,128)} %get-tuple-element.190.q_ref.qr_ref.qr, f32[1024,512]{1,0:T(8,128)} %get-tuple-element.191.k_ref.kr_ref.kr, bf16[1024,512]{1,0:T(8,128)(2,1)} %get-tuple-element.192.v_ref, ...), custom_call_target="tpu_custom_call" | custom-call | flops 1610612736 | bytes 8388608 | tf_op jit(solution)/shard_map/attention_forward/pallas_call | solution.py:376
  170.8 20.9 %collective-permute-done.8 = bf16[256,2048]{1,0:T(8,128)(2,1)} collective-permute-done((bf16[256,2048]{1,0:T(8,128)(2,1)}, bf16[256,2048]{1,0:T(8,128)(2,1)}, u32[]{:S(2)}, u32[]{:S(2)}) %collective-permute-start.8) | collective-permute-done | bytes 1048608 | tf_op jit(solution)/shard_map/ppermute | solution.py:108
  195.5 18.9 %collective-permute-done.13.refs_7_.refs_23_.refs_39_ = bf16[24,256,256]{2,1,0:T(8,128)(2,1)} collective-permute-done((bf16[24,256,256]{2,1,0:T(8,128)(2,1)S(1)}, bf16[24,256,256]{2,1,0:T(8,128)(2,1)}, u32[]{:S(2)}, u32[]{:S(2)}) %collective-permute-start.13) | collective-permute-done | bytes 3145760 | tf_op jit(solution)/shard_map/ppermute | solution.py:65
  214.4 62.5 %collective-permute-done.14.refs_9_.refs_25_.refs_41_ = bf16[24,256,256]{2,1,0:T(8,128)(2,1)} collective-permute-done((bf16[24,256,256]{2,1,0:T(8,128)(2,1)}, bf16[24,256,256]{2,1,0:T(8,128)(2,1)}, u32[]{:S(2)}, u32[]{:S(2)}) %collective-permute-start.14) | collective-permute-done | bytes 3145760 | tf_op jit(solution)/shard_map/ppermute | solution.py:65
  291.9 15.8 %collective-permute-done.10 = bf16[256,2048]{1,0:T(8,128)(2,1)} collective-permute-done((bf16[256,2048]{1,0:T(8,128)(2,1)S(1)}, bf16[256,2048]{1,0:T(8,128)(2,1)}, u32[]{:S(2)}, u32[]{:S(2)}) %collective-permute-start.10) | collective-permute-done | bytes 1048608 | tf_op jit(solution)/shard_map/ppermute | solution.py:108
  327.2 51.0 %moe_first.4 = (bf16[256,2048]{1,0:T(8,128)(2,1)}, f32[256,16]{1,0:T(8,128)}, bf16[16,1024,256]{2,1,0:T(8,128)(2,1)}, bf16[16,1024,256]{2,1,0:T(8,128)(2,1)}, bf...) custom-call(s32[3]{0:T(128)} %pad_add_fusion.3.side_ref, ...), custom_call_target="tpu_custom_call" | custom-call | flops 21474836480 | bytes 62914560 | tf_op jit(solution)/shard_map/moe_first/pallas_call | solution.py:626
  382.6 39.3 %moe_first.5 = (bf16[256,2048]{1,0:T(8,128)(2,1)}, f32[256,16]{1,0:T(8,128)}, bf16[16,1024,256]{2,1,0:T(8,128)(2,1)}, bf16[16,1024,256]{2,1,0:T(8,128)(2,1)}, bf16[16,1024,256]{2,1,0:T(8,128)(2,1)}) custom-call(s32[3]{0:T(128)} %pad_add_fusion.3.side_ref, ...), custom_call_target="tpu_custom_call", output_to_operand_aliasing={{2}: (7, {}), {3}: (8, {}), {4}: (9, {})} | custom-call | flops 21474836480 | bytes 62914560 | tf_op jit(solution)/shard_map/moe_first/pallas_call | solution.py:626
  434.6 39.4 %moe_first.6 = (bf16[256,2048]{1,0:T(8,128)(2,1)}, f32[256,16]{1,0:T(8,128)}, bf16[16,1024,256]{2,1,0:T(8,128)(2,1)}, bf16[16,1024,256]{2,1,0:T(8,128)(2,1)}, bf16[16,1024,256]{2,1,0:T(8,128)(2,1)}) custom-call(s32[3]{0:T(128)} %pad_add_fusion.3.side_ref, ...), custom_call_target="tpu_custom_call", output_to_operand_aliasing={{2}: (7, {}), {3}: (8, {}), {4}: (9, {})} | custom-call | flops 21474836480 | bytes 62914560 | tf_op jit(solution)/shard_map/moe_first/pallas_call | solution.py:626
  487.6 39.3 %moe_first.7 = (bf16[256,2048]{1,0:T(8,128)(2,1)}, f32[256,16]{1,0:T(8,128)}, bf16[16,1024,256]{2,1,0:T(8,128)(2,1)}, bf16[16,1024,256]{2,1,0:T(8,128)(2,1)}, bf16[16,1024,256]{2,1,0:T(8,128)(2,1)}) custom-call(s32[3]{0:T(128)} %pad_add_fusion.3.side_ref, ...), custom_call_target="tpu_custom_call", output_to_operand_aliasing={{2}: (7, {}), {3}: (8, {}), {4}: (9, {})} | custom-call | flops 21474836480 | bytes 62914560 | tf_op jit(solution)/shard_map/moe_first/pallas_call | solution.py:626
  535.1 26.2 %moe_grad_split.3 = (bf16[16,4,256,256]{3,2,1,0:T(8,128)(2,1)}, bf16[16,4,256,256]{3,2,1,0:T(8,128)(2,1)}) custom-call(s32[1]{0:T(128)} %bitcast.27.side_ref, bf16[256,2048]{1,0:T(8,128)(2,1)} %copy-done.4, bf16[256,2048]{1,0:T(8,128)(2,1)} %collective-permute-done.23.refs_0_.refs_1_, bf16[256,2048]{1,0:T(8,128)(2,1)} %collective-permute-done.25.refs_0_.refs_2_, ...), custom_call_target="tpu_custom_call" | custom-call | flops 17179869184 | bytes 29360128 | tf_op jit(solution)/shard_map/moe_grad_split/pallas_call | solution.py:697
  574.9 31.7 %moe_grad_split.4 = (bf16[16,4,256,256]{3,2,1,0:T(8,128)(2,1)}, bf16[16,4,256,256]{3,2,1,0:T(8,128)(2,1)}, bf16[16,4,256,256]{3,2,1,0:T(8,128)(2,1)}) custom-call(s32[1]{0:T(128)} %bitcast.27.side_ref, bf16[256,2048]{1,0:T(8,128)(2,1)} %copy-done.4, bf16[256,2048]{1,0:T(8,128)(2,1)} %collective-permute-done.23.refs_0_.refs_1_, ...), custom_call_target="tpu_custom_call" | custom-call | flops 17179869184 | bytes 29360128 | tf_op jit(solution)/shard_map/moe_grad_split/pallas_call | solution.py:697
  607.0 27.0 %moe_out.1 = bf16[1024,2048]{1,0:T(8,128)(2,1)} custom-call(bf16[16,1024,256]{2,1,0:T(8,128)(2,1)} %get-tuple-element.298.h_ref.refs_4_, bf16[16,2048,256]{2,1,0:T(8,128)(2,1)} %get-tuple-element.233.refs_5_.d_ref), custom_call_target="tpu_custom_call" | custom-call | flops 17179869184 | bytes 29360128 | tf_op jit(solution)/shard_map/moe_out/pallas_call | solution.py:739
  634.6 32.1 %moe_grad_split.5 = (bf16[16,4,256,256]{3,2,1,0:T(8,128)(2,1)}, bf16[16,4,256,256]{3,2,1,0:T(8,128)(2,1)}, bf16[16,4,256,256]{3,2,1,0:T(8,128)(2,1)}) custom-call(s32[1]{0:T(128)} %constant.184.clone.1.side_ref, bf16[256,2048]{1,0:T(8,128)(2,1)} %select_dynamic-update-slice_fusion.8.refs_1_.refs_0_, bf16[256,2048]{1,0:T(8,128)(2,1)} %collective-permute-done.7.refs_1_, ...), custom_call_target="tpu_custom_call" | custom-call | flops 17179869184 | bytes 29360128 | tf_op jit(solution)/shard_map/moe_grad_split/pallas_call | solution.py:697
  681.3 29.4 %attention_backward.1 = (f32[1024,512]{1,0:T(8,128)}, f32[1024,512]{1,0:T(8,128)}, bf16[1024,512]{1,0:T(8,128)(2,1)}, f32[2,8,1024]{2,1,0:T(8,128)}, f32[2,512]{...) custom-call(bf16[1024,512]{1,0:T(8,128)(2,1)} %get-tuple-element.206, ...), custom_call_target="tpu_custom_call" | custom-call | flops 4026531840 | bytes 13631488 | tf_op jit(solution)/shard_map/attention_backward/pallas_call | solution.py:485
  727.6 13.8 %projection_back.1 = (bf16[1024,512]{1,0:T(8,128)(2,1)}, bf16[1024,512]{1,0:T(8,128)(2,1)}, bf16[4,256,2048]{2,1,0:T(8,128)(2,1)}) custom-call(s32[4]{0:T(128)} %pad_add_fusion.2.place_ref, f32[1024,512]{1,0:T(8,128)} %get-tuple-element.190.q_ref.qr_ref.qr, f32[1024,512]{1,0:T(8,128)} %get-tuple-element.191.k_ref.kr_ref.kr, ...), custom_call_target="tpu_custom_call" | custom-call | flops 6442450944 | bytes 22020096 | tf_op jit(solution)/shard_map/projection_back/pallas_call | solution.py:237
  744.4 19.0 %projection_grads.1 = (bf16[4,4,256,512]{3,2,1,0:T(8,128)(2,1)}, bf16[4,4,256,512]{3,2,1,0:T(8,128)(2,1)}) custom-call(s32[5]{0:T(128)} %stack.84.place_ref, bf16[256,2048]{1,0:T(8,128)(2,1)} %fusion.4.refs_0_, bf16[256,2048]{1,0:T(8,128)(2,1)} %collective-permute-done.refs_1_, bf16[256,2048]{1,0:T(8,128)(2,1)} %collective-permute-done.1.refs_2_, ...), custom_call_target="tpu_custom_call" | custom-call | flops 8589934592 | bytes 20971520 | tf_op jit(solution)/shard_map/projection_grads/pallas_call | solution.py:316
  771.3 35.9 %collective-permute-done.45 = bf16[8,2,256,256]{3,2,0,1:T(8,128)(2,1)} collective-permute-done((bf16[8,2,256,256]{3,2,0,1:T(8,128)(2,1)}, bf16[8,2,256,256]{3,2,0,1:T(8,128)(2,1)}, u32[]{:S(2)}, u32[]{:S(2)}) %collective-permute-start.45) | collective-permute-done | bytes 2097184 | tf_op jit(solution)/shard_map/ppermute | solution.py:65
  825.3 11.9 %collective-permute-done.47 = bf16[256,2048]{1,0:T(8,128)(2,1)} collective-permute-done((bf16[256,2048]{1,0:T(8,128)(2,1)S(1)}, bf16[256,2048]{1,0:T(8,128)(2,1)}, u32[]{:S(2)}, u32[]{:S(2)}) %collective-permute-start.47) | collective-permute-done | bytes 1048608 | tf_op jit(solution)/shard_map/ppermute | solution.py:108
  850.3 19.2 %collective-permute-done.49 = bf16[256,2048]{1,0:T(8,128)(2,1)S(1)} collective-permute-done((bf16[256,2048]{1,0:T(8,128)(2,1)S(1)}, bf16[256,2048]{1,0:T(8,128)(2,1)S(1)}, u32[]{:S(2)}, u32[]{:S(2)}) %collective-permute-start.49) | collective-permute-done | bytes 1048608 | tf_op jit(solution)/shard_map/ppermute | solution.py:108
  875.5 11.9 %collective-permute-done.51 = bf16[8,256,256]{2,1,0:T(8,128)(2,1)} collective-permute-done((bf16[8,256,256]{2,1,0:T(8,128)(2,1)}, bf16[8,256,256]{2,1,0:T(8,128)(2,1)}, u32[]{:S(2)}, u32[]{:S(2)}) %collective-permute-start.51) | collective-permute-done | bytes 1048608 | tf_op jit(solution)/shard_map/ppermute | solution.py:65
  (370 shorter events, 284.9 us)
Async XLA Ops:
  7.2 94.4 %all-gather.2.cloned.1.call-start = ((), (), s32[]{:S(2)}) async-start(), calls=%async_computation.3 | async-start | bytes 9437184 | tf_op jit(solution)/shard_map/all_gather | solution.py:797
  9.7 701.0 %reduce-scatter.4.cloned.1.call-start = ((), (), s32[]{:S(2)}) async-start(), calls=%async_computation.4 | async-start | bytes 10485760 | tf_op jit(solution)/shard_map/reduce_scatter | solution.py:952
  15.5 103.9 %collective-permute-start.3 = (bf16[24,256,256]{2,1,0:T(8,128)(2,1)S(1)}, bf16[24,256,256]{2,1,0:T(8,128)(2,1)}, u32[]{:S(2)}, u32[]{:S(2)}) collective-permute-start(bf16[24,256,256]{2,1,0:T(8,128)(2,1)S(1)} %pad_maximum_fusion.1.refs_3_.refs_19_.refs_35_), channel_id=1, source_target_pairs={{0,8},{4,12},{8,0},{12,4},{16,24},{20,28},{24,16},{28,20},{1,9},{5... | collective-permute-start | bytes 9437192 | tf_op jit(solution)/shard_map/ppermute | solution.py:65
  19.3 103.6 %collective-permute-start.4 = (bf16[24,256,256]{2,1,0:T(8,128)(2,1)}, bf16[24,256,256]{2,1,0:T(8,128)(2,1)}, u32[]{:S(2)}, u32[]{:S(2)}) collective-permute-start(bf16[24,256,256]{2,1,0:T(8,128)(2,1)} %pad_maximum_fusion.2.refs_11_.refs_27_.refs_43_), channel_id=1, source_target_pairs={{0,16},{4,20},{8,24},{12,28},{16,0},{20,4},{24,8},{28,12},{1,17},{... | collective-permute-start | bytes 9437192 | tf_op jit(solution)/shard_map/ppermute | solution.py:65
  66.4 46.3 %collective-permute-start.2 = (bf16[256,2048]{1,0:T(8,128)(2,1)}, bf16[256,2048]{1,0:T(8,128)(2,1)}, u32[]{:S(2)}, u32[]{:S(2)}) collective-permute-start(bf16[256,2048]{1,0:T(8,128)(2,1)} %collective-permute-done.1.refs_2_), channel_id=1, source_target_pairs={{0,1},{1,2},{2,3},{3,0},{4,5},{5,6},{6,7},{7,4},{8,9},{9,10},{10,1... | collective-permute-start | bytes 3145736 | tf_op jit(solution)/shard_map/ppermute | solution.py:108
  143.3 71.1 %collective-permute-start.13 = (bf16[24,256,256]{2,1,0:T(8,128)(2,1)S(1)}, bf16[24,256,256]{2,1,0:T(8,128)(2,1)}, u32[]{:S(2)}, u32[]{:S(2)}) collective-permute-start(bf16[24,256,256]{2,1,0:T(8,128)(2,1)S(1)} %pad_maximum_fusion.1.refs_3_.refs_19_.refs_35_), channel_id=1, source_target_pairs={{0,16},{4,20},{8,24},{12,28},{16,0},{20,4},{24,8},{28,12},{1,17},{... | collective-permute-start | bytes 9437192 | tf_op jit(solution)/shard_map/ppermute | solution.py:65
  144.8 132.1 %collective-permute-start.14 = (bf16[24,256,256]{2,1,0:T(8,128)(2,1)}, bf16[24,256,256]{2,1,0:T(8,128)(2,1)}, u32[]{:S(2)}, u32[]{:S(2)}) collective-permute-start(bf16[24,256,256]{2,1,0:T(8,128)(2,1)} %collective-permute-done.3.refs_5_.refs_21_.refs_37_), channel_id=1, source_target_pairs={{0,16},{4,20},{8,24},{12,28},{16,0},{20,4},{24,8},{28,12},{1,17},{... | collective-permute-start | bytes 9437192 | tf_op jit(solution)/shard_map/ppermute | solution.py:65
  145.3 131.6 %collective-permute-start.16 = (bf16[24,256,256]{2,1,0:T(8,128)(2,1)}, bf16[24,256,256]{2,1,0:T(8,128)(2,1)}, u32[]{:S(2)}, u32[]{:S(2)}) collective-permute-start(bf16[24,256,256]{2,1,0:T(8,128)(2,1)} %pad_maximum_fusion.2.refs_11_.refs_27_.refs_43_), channel_id=1, source_target_pairs={{0,8},{4,12},{8,0},{12,4},{16,24},{20,28},{24,16},{28,20},{1,9},{5... | collective-permute-start | bytes 9437192 | tf_op jit(solution)/shard_map/ppermute | solution.py:65
  194.3 83.1 %collective-permute-start.9 = (bf16[256,2048]{1,0:T(8,128)(2,1)S(1)}, bf16[256,2048]{1,0:T(8,128)(2,1)}, u32[]{:S(2)}, u32[]{:S(2)}) collective-permute-start(bf16[256,2048]{1,0:T(8,128)(2,1)S(1)} %add_convert_fusion.6), channel_id=1, source_target_pairs={{0,1},{1,2},{2,3},{3,0},{4,5},{5,6},{6,7},{7,4},{8,9},{9,10},{10,1... | collective-permute-start | bytes 3145736 | tf_op jit(solution)/shard_map/ppermute | solution.py:108
  194.4 85.8 %collective-permute-start.18 = (bf16[24,256,256]{2,1,0:T(8,128)(2,1)}, bf16[24,256,256]{2,1,0:T(8,128)(2,1)}, u32[]{:S(2)}, u32[]{:S(2)}) collective-permute-start(bf16[24,256,256]{2,1,0:T(8,128)(2,1)} %collective-permute-done.4.refs_15_.refs_31_.refs_47_), channel_id=1, source_target_pairs={{0,8},{4,12},{8,0},{12,4},{16,24},{20,28},{24,16},{28,20},{1,9},{5... | collective-permute-start | bytes 9437192 | tf_op jit(solution)/shard_map/ppermute | solution.py:65
  214.4 67.4 %collective-permute-start.17 = (bf16[24,256,256]{2,1,0:T(8,128)(2,1)}, bf16[24,256,256]{2,1,0:T(8,128)(2,1)}, u32[]{:S(2)}, u32[]{:S(2)}) collective-permute-start(bf16[24,256,256]{2,1,0:T(8,128)(2,1)} %collective-permute-done.4.refs_15_.refs_31_.refs_47_), channel_id=1, source_target_pairs={{0,4},{4,0},{8,12},{12,8},{16,20},{20,16},{24,28},{28,24},{1,5},{5... | collective-permute-start | bytes 9437192 | tf_op jit(solution)/shard_map/ppermute | solution.py:65
  313.4 64.8 %collective-permute-start.23 = (bf16[256,2048]{1,0:T(8,128)(2,1)S(1)}, bf16[256,2048]{1,0:T(8,128)(2,1)}, u32[]{:S(2)}, u32[]{:S(2)}) collective-permute-start(bf16[256,2048]{1,0:T(8,128)(2,1)S(1)} %multiply_convert_fusion.refs_0_), channel_id=1, source_target_pairs={{0,1},{1,2},{2,3},{3,0},{4,5},{5,6},{6,7},{7,4},{8,9},{9,10},{10,1... | collective-permute-start | bytes 3145736 | tf_op jit(solution)/shard_map/ppermute | solution.py:108
  315.0 63.2 %collective-permute-start.24 = (bf16[256,2048]{1,0:T(8,128)(2,1)}, bf16[256,2048]{1,0:T(8,128)(2,1)}, u32[]{:S(2)}, u32[]{:S(2)}) collective-permute-start(bf16[256,2048]{1,0:T(8,128)(2,1)} %collective-permute-done.7.refs_1_), channel_id=1, source_target_pairs={{0,1},{1,2},{2,3},{3,0},{4,5},{5,6},{6,7},{7,4},{8,9},{9,10},{10,1... | collective-permute-start | bytes 3145736 | tf_op jit(solution)/shard_map/ppermute | solution.py:108
  379.9 49.8 %collective-permute-start.25 = (bf16[256,2048]{1,0:T(8,128)(2,1)}, bf16[256,2048]{1,0:T(8,128)(2,1)}, u32[]{:S(2)}, u32[]{:S(2)}) collective-permute-start(bf16[256,2048]{1,0:T(8,128)(2,1)} %collective-permute-done.23.refs_0_.refs_1_), channel_id=1, source_target_pairs={{0,1},{1,2},{2,3},{3,0},{4,5},{5,6},{6,7},{7,4},{8,9},{9,10},{10,1... | collective-permute-start | bytes 3145736 | tf_op jit(solution)/shard_map/ppermute | solution.py:108
  379.9 49.8 %collective-permute-start.26 = (bf16[256,2048]{1,0:T(8,128)(2,1)}, bf16[256,2048]{1,0:T(8,128)(2,1)}, u32[]{:S(2)}, u32[]{:S(2)}) collective-permute-start(bf16[256,2048]{1,0:T(8,128)(2,1)} %collective-permute-done.24.refs_1_.refs_2_), channel_id=1, source_target_pairs={{0,1},{1,2},{2,3},{3,0},{4,5},{5,6},{6,7},{7,4},{8,9},{9,10},{10,1... | collective-permute-start | bytes 3145736 | tf_op jit(solution)/shard_map/ppermute | solution.py:108
  431.3 42.8 %collective-permute-start.27 = (bf16[256,2048]{1,0:T(8,128)(2,1)}, bf16[256,2048]{1,0:T(8,128)(2,1)}, u32[]{:S(2)}, u32[]{:S(2)}) collective-permute-start(bf16[256,2048]{1,0:T(8,128)(2,1)} %collective-permute-done.25.refs_0_.refs_2_), channel_id=1, source_target_pairs={{0,1},{1,2},{2,3},{3,0},{4,5},{5,6},{6,7},{7,4},{8,9},{9,10},{10,1... | collective-permute-start | bytes 3145736 | tf_op jit(solution)/shard_map/ppermute | solution.py:108
  432.6 48.1 %collective-permute-start.28 = (bf16[256,2048]{1,0:T(8,128)(2,1)}, bf16[256,2048]{1,0:T(8,128)(2,1)}, u32[]{:S(2)}, u32[]{:S(2)}) collective-permute-start(bf16[256,2048]{1,0:T(8,128)(2,1)} %get-tuple-element.254), channel_id=1, source_target_pairs={{0,1},{1,2},{2,3},{3,0},{4,5},{5,6},{6,7},{7,4},{8,9},{9,10},{10,1... | collective-permute-start | bytes 3145736 | tf_op jit(solution)/shard_map/ppermute | solution.py:108
  481.7 45.1 %collective-permute-start.31 = (f32[4096]{0:T(1024)S(1)}, f32[4096]{0:T(1024)S(1)}, u32[]{:S(2)}, u32[]{:S(2)}) collective-permute-start(f32[4096]{0:T(1024)S(1)} %add.239), channel_id=1, source_target_pairs={{0,1},{1,2},{2,3},{3,0},{4,5},{5,6},{6,7},{7,4},{8,9},{9,10},{10,1... | collective-permute-start | bytes 49160 | tf_op jit(solution)/shard_map/ppermute | solution.py:108
  606.7 265.8 %reduce-scatter.6.cloned.1.call-start = ((), (), s32[]{:S(2)}) async-start(), calls=%async_computation.5 | async-start | bytes 10485760 | tf_op jit(solution)/shard_map/reduce_scatter | solution.py:952
  667.7 262.5 %reduce-scatter.8.cloned.1.call-start = ((), (), s32[]{:S(2)}) async-start(), calls=%async_computation.6 | async-start | bytes 5242880 | tf_op jit(solution)/shard_map/reduce_scatter | solution.py:952
  724.2 83.0 %collective-permute-start.45 = (bf16[8,2,256,256]{3,2,0,1:T(8,128)(2,1)}, bf16[8,2,256,256]{3,2,0,1:T(8,128)(2,1)}, u32[]{:S(2)}, u32[]{:S(2)}) collective-permute-start(bf16[8,2,256,256]{3,2,0,1:T(8,128)(2,1)} %copy.119), channel_id=1, source_target_pairs={{0,8},{4,12},{8,0},{12,4},{16,24},{20,28},{24,16},{28,20},{1,9},{5... | collective-permute-start | bytes 6291464 | tf_op jit(solution)/shard_map/ppermute | solution.py:65
  725.4 82.2 %collective-permute-start.46 = (bf16[8,2,256,256]{3,2,1,0:T(8,128)(2,1)}, bf16[8,2,256,256]{3,2,1,0:T(8,128)(2,1)}, u32[]{:S(2)}, u32[]{:S(2)}) collective-permute-start(bf16[8,2,256,256]{3,2,1,0:T(8,128)(2,1)} %get-tuple-element.327), channel_id=1, source_target_pairs={{0,16},{4,20},{8,24},{12,28},{16,0},{20,4},{24,8},{28,12},{1,17},{... | collective-permute-start | bytes 6291464 | tf_op jit(solution)/shard_map/ppermute | solution.py:65
  840.2 47.3 %collective-permute-start.51 = (bf16[8,256,256]{2,1,0:T(8,128)(2,1)}, bf16[8,256,256]{2,1,0:T(8,128)(2,1)}, u32[]{:S(2)}, u32[]{:S(2)}) collective-permute-start(bf16[8,256,256]{2,1,0:T(8,128)(2,1)} %fusion.22), channel_id=1, source_target_pairs={{0,16},{4,20},{8,24},{12,28},{16,0},{20,4},{24,8},{28,12},{1,17},{... | collective-permute-start | bytes 3145736 | tf_op jit(solution)/shard_map/ppermute | solution.py:65
  847.2 42.6 %collective-permute-start.52 = (bf16[8,256,256]{2,1,0:T(8,128)(2,1)}, bf16[8,256,256]{2,1,0:T(8,128)(2,1)}, u32[]{:S(2)}, u32[]{:S(2)}) collective-permute-start(bf16[8,256,256]{2,1,0:T(8,128)(2,1)} %fusion.23), channel_id=1, source_target_pairs={{0,8},{4,12},{8,0},{12,4},{16,24},{20,28},{24,16},{28,20},{1,9},{5... | collective-permute-start | bytes 3145736 | tf_op jit(solution)/shard_map/ppermute | solution.py:65
  (91 other events, 1926.7 us)
Sparse Core Ops, SparseCore 0:
  10.5 91.0 all-gather.1
  606.8 84.2 reduce-scatter.3
  694.5 122.4 reduce-scatter.5
  837.3 73.1 reduce-scatter.7

commit v3 on v2

--- a/solution.py
+++ b/solution.py
@@ -260,21 +260,23 @@
     )(jnp.stack(order).astype(jnp.int32), *raws, *gaineds, value_low, scales, inner, weights)
 
 
-def pair_sum(first, second):
+def pair_split(first, second, axis):
     block = pl.BlockSpec((1,) + first.shape[1:], lambda i: (i, 0, 0, 0))
-
-    def kernel(a_ref, b_ref, out_ref):
-        add_pair((a_ref, b_ref), (out_ref,))
+    steps = first.shape[0]
+    specs, shapes = split_outs(first, steps)
+
+    def kernel(a_ref, b_ref, *outs):
+        add_split((a_ref, b_ref), outs, pl.program_id(0) >= steps // 2, cube_orders(axis))
 
     return pl.pallas_call(
         kernel,
-        grid=(first.shape[0],),
+        grid=(steps,),
         in_specs=[block, block],
-        out_specs=block,
-        out_shape=jax.ShapeDtypeStruct(first.shape, first.dtype),
+        out_specs=specs,
+        out_shape=shapes,
         compiler_params=pltpu.CompilerParams(vmem_limit_bytes=58 << 20),
         cost_estimate=pl.CostEstimate(flops=first.size, transcendentals=0, bytes_accessed=6 * first.size),
-        name="pair_sum",
+        name="pair_split",
     )(first, second)
 
 
@@ -305,8 +307,8 @@
             @pl.when(i == j)
             def _(j=j):
                 for q in range(n // 2):
-                    for out, side in ((keep_ref, place_ref[count]), (send_ref, 1 - place_ref[count])):
-                        at = pl.multiple_of((2 * q + side) * block, block)
+                    for out, side in ((keep_ref, 0), (send_ref, 1)):
+                        at = pl.multiple_of(((2 * q + side) ^ place_ref[count]) * block, block)
                         product = dot32(turned[pl.ds(at, block), :], low_refs[j][...])
                         out[0, q] = product.astype(jnp.bfloat16)
 
@@ -330,7 +332,7 @@
             bytes_accessed=4 * rows * width + 2 * arrays * columns * (width + rows),
         ),
         name="projection_grads",
-    )(jnp.stack([*places, lax.axis_index(axis) % 2]).astype(jnp.int32), *firsts, *seconds, *lows)
+    )(jnp.stack([*places, lax.axis_index(axis)]).astype(jnp.int32), *firsts, *seconds, *lows)
 
 
 def attention_forward(query_raw, key_raw, values, scales, gains, tables, marks):
@@ -409,31 +411,17 @@
     f32, bf16 = jnp.float32, jnp.bfloat16
     widest = max(key_span(t)[1] for t in range(tiles))
     tn = (((0,), (0,)), ((), ()))
-    experts, blocks = addends[0].shape[:2]
-    each = experts // heads
-    part = pl.BlockSpec((each,) + addends[0].shape[1:], lambda h: (h, 0, 0, 0))
-    fewer = (blocks // 2,) + addends[0].shape[2:]
-    split_specs = [
-        pl.BlockSpec((each,) + fewer, lambda h: (jnp.minimum(h, heads // 2 - 1), 0, 0, 0)),
-        pl.BlockSpec((each,) + fewer, lambda h: (jnp.maximum(h - heads // 2, 0), 0, 0, 0)),
-    ]
-    firsts = [order[0] // 2 for order in cube_orders(axis)]
+    part = pl.BlockSpec(
+        (addends[0].shape[0] // heads,) + addends[0].shape[1:], lambda h: (h, 0, 0, 0)
+    )
+    sum_specs, sum_shapes = split_outs(addends[0], heads)
 
     def kernel(
         q_ref, k_ref, v_ref, m_ref, qr_ref, kr_ref, s_ref, g_ref, cos_ref, sin_ref, col_ref, row_ref, a_ref, b_ref,
         dq_out, dk_out, dv_out, inner_out, gain_out, stay_0, stay_1, send_0, send_1, bias, dq, dk, dv,
     ):
         h = pl.program_id(0)
-        for p, (stay, send) in enumerate(((stay_0, send_0), (stay_1, send_1))):
-
-            @pl.when((h >= heads // 2) == bool(p))
-            def _(p=p, stay=stay, send=send):
-                at = [0, 0]
-                for m in range(blocks):
-                    out = 1 if m & firsts[p] else 0
-                    total = a_ref[:, m].astype(f32) + b_ref[:, m].astype(f32)
-                    (stay, send)[out][:, at[out]] = total.astype(bf16)
-                    at[out] += 1
+        add_split((a_ref, b_ref), (stay_0, stay_1, send_0, send_1), h >= heads // 2, cube_orders(axis))
 
         @pl.when(h == 0)
         def _():
@@ -502,7 +490,7 @@
             part,
         ],
         out_specs=[head, head, head, pl.BlockSpec((2, 8, length), lambda h: (0, 0, 0)), pair]
-        + split_specs * 2,
+        + sum_specs,
         out_shape=[
             wide,
             wide,
@@ -510,7 +498,7 @@
             jax.ShapeDtypeStruct((2, 8, length), f32),
             jax.ShapeDtypeStruct((2, columns), f32),
         ]
-        + [jax.ShapeDtypeStruct((experts // 2,) + fewer, bf16)] * 4,
+        + sum_shapes,
         scratch_shapes=[
             pltpu.VMEM((widest, length), f32),
             pltpu.VMEM((length, HEAD), f32),
@@ -529,19 +517,21 @@
     )
 
 
-def moe_first(xs, fs, weight, arrays, filled, first, total, side):
+def moe_first(xs, fs, weight, arrays, span, filled, made, before, first, total, side):
     count = len(xs)
     chunk, width = xs[0].shape
-    rows = count * chunk
-    parted = [isinstance(a, list) for a in arrays]
+    parted = isinstance(arrays[0], list)
     experts = weight.shape[1]
-    pieces = [a if p else [(0, experts, 0, [a])] for a, p in zip(arrays, parted)]
-    hidden = pieces[0][0][3][0].shape[-1]
-    step = 2 if any(parted) else (4 if count == 1 else 1)
+    pieces = arrays if parted else [[(0, experts, [(a, 0)])] for a in arrays]
+    hidden = pieces[0][0][2][0][0].shape[-1]
+    step = 2
+    low, high = span
     bf16 = jnp.bfloat16
-    before = [] if filled is None else list(filled)
     flat = [(i, *group) for i, groups in enumerate(pieces) for group in groups]
     sizes = [len(entry[-1]) for entry in flat]
+    aliased = list(filled or []) + list(made or [])
+    before = [pair[i] for i in range(2) for pair in before or []]
+    makes = 3 if parted else 0
 
     def kernel(side_ref, *refs):
         x_refs, f_refs, w_ref = refs[:count], refs[count : 2 * count], refs[2 * count]
@@ -550,42 +540,46 @@
         for size in sizes:
             groups.append(refs[at : at + size])
             at += size
-        outs = refs[at + len(before) :]
-        dx_ref, gp_ref, wh_ref, dg_ref, du_ref, acc = *outs[:5], outs[-1]
-        made = list(outs[5:-1])
+        earlier = refs[at : at + len(before)]
+        outs = refs[at + len(before) + len(aliased) :]
+        dx_refs, gp_refs = outs[:count], outs[count : 2 * count]
+        wh_ref, dg_ref, du_ref = outs[2 * count : 2 * count + 3]
+        target_refs = outs[2 * count + 3 : 2 * count + 3 + makes]
+        acc = outs[-1]
         s = pl.program_id(0)
-        ready = []
-        for i in range(3):
-            if not parted[i]:
-                ready.append(next(g[0] for g, entry in zip(groups, flat) if entry[0] == i))
-                continue
-            target = made.pop(0)
-            ready.append(target)
-            mine = [(g, *entry[1:]) for g, entry in zip(groups, flat) if entry[0] == i]
-            for refs_in, begin, held, _, blocks in mine:
-
-                @pl.when((s * step >= begin) & (s * step < begin + held))
+        for i, target in enumerate(target_refs):
+            for refs_in, entry in zip(groups, flat):
+                if entry[0] != i:
+                    continue
+                begin, held, blocks = entry[1:]
+
+                @pl.when((low + s * step >= begin) & (low + s * step < begin + held))
                 def _(refs_in=refs_in, blocks=blocks, target=target, i=i):
-                    high = blocks[0].shape[1]
+                    tall = blocks[0][0].shape[1]
                     for m in range(len(blocks)):
-                        place = 0 if len(blocks) == 1 else (side_ref[i] ^ m) * high
-                        place = 0 if len(blocks) == 1 else pl.multiple_of(place, high)
-                        target[:, pl.ds(place, high), :] = refs_in[m][...]
-
-        g_ref, u_ref, d_ref = ready
+                        place = pl.multiple_of((side_ref[i] ^ m) * tall, tall)
+                        target[:, pl.ds(place, tall), :] = refs_in[m][...]
+
+        g_ref, u_ref, d_ref = target_refs if parted else [group[0] for group in groups]
 
         @pl.when(s == 0)
         def _():
-            acc[...] = jnp.zeros_like(acc)
-            gp_ref[...] = jnp.zeros_like(gp_ref)
+            for r in range(count):
+                rs = pl.ds(r * chunk, chunk)
+                if before:
+                    acc[rs, :] = earlier[r][...].astype(jnp.float32)
+                    gp_refs[r][...] = earlier[count + r][...]
+                else:
+                    acc[rs, :] = jnp.zeros((chunk, width), jnp.float32)
+                    gp_refs[r][...] = jnp.zeros((chunk, experts), jnp.float32)
 
         lane = lax.broadcasted_iota(jnp.int32, (chunk, experts), 1)
         for r in range(count):
             rs = pl.ds(r * chunk, chunk)
             x, f = x_refs[r][...], f_refs[r][...]
-            dx = None
+            grads, rows_w = [], []
             for j in range(step):
-                e = s * step + j
+                e = low + s * step + j
                 w = jnp.sum(jnp.where(lane == e, w_ref[rs, :], 0.0), axis=1, keepdims=True)
                 gate_pre = dot32(x, g_ref[j])
                 up_pre = dot32(x, u_ref[j])
@@ -595,72 +589,74 @@
                 hidden_f = act * up_pre
                 wh_ref[j, rs, :] = (w * hidden_f).astype(bf16)
                 inner = jnp.sum(hidden_f * projected, axis=1, keepdims=True)
-                gp_ref[rs, :] = jnp.where(lane == e, inner, gp_ref[rs, :])
+                gp_refs[r][...] = jnp.where(lane == e, inner, gp_refs[r][...])
                 grad_hidden = w * projected
                 dg = (grad_hidden * up_pre * (sig + act * (1.0 - sig))).astype(bf16)
                 du = (grad_hidden * act).astype(bf16)
                 dg_ref[j, rs, :] = dg
                 du_ref[j, rs, :] = du
-                term = dot32(dg, g_ref[j], NT) + dot32(du, u_ref[j], NT)
-                dx = term if dx is None else dx + term
-            acc[rs, :] += dx
-
-        @pl.when(s == experts // step - 1)
+                grads += [dg, du]
+                rows_w += [g_ref[j], u_ref[j]]
+            acc[rs, :] += dot32(jnp.concatenate(grads, axis=1), jnp.concatenate(rows_w, axis=1), NT)
+
+        @pl.when(s == (high - low) // step - 1)
         def _():
-            dx_ref[...] = acc[...].astype(bf16)
+            for r in range(count):
+                dx_refs[r][...] = acc[pl.ds(r * chunk, chunk), :].astype(bf16)
 
     def whole(shape):
         return pl.BlockSpec(shape, lambda s, side: (0, 0), pipeline_mode=pl.Buffered(1))
+
+    def out_whole(shape):
+        return pl.BlockSpec(shape, lambda s, side: (0, 0))
 
     def block_of(block, begin, held, base):
         return pl.BlockSpec(
             (step,) + block.shape[1:],
-            lambda s, side: (base // step + jnp.clip(s - begin // step, 0, held // step - 1), 0, 0),
+            lambda s, side: (
+                base // step + jnp.clip(s + low // step - begin // step, 0, held // step - 1),
+                0,
+                0,
+            ),
         )
 
-    w_spec = pl.BlockSpec((step, width, hidden), lambda s, side: (s, 0, 0))
-    h_spec = pl.BlockSpec((step, rows, hidden), lambda s, side: (s, first // count, 0))
+    w_spec = pl.BlockSpec((step, width, hidden), lambda s, side: (s + low // step, 0, 0))
+    h_spec = pl.BlockSpec(
+        (step, count * chunk, hidden), lambda s, side: (s + low // step, first // count, 0)
+    )
     kept = jax.ShapeDtypeStruct((experts, total, hidden), bf16)
-    blocks_in = [block for entry in flat for block in entry[-1]]
-    made_count = sum(parted)
+    blocks_in = [block for entry in flat for block, _ in entry[-1]]
+    rows = count * chunk
+    ahead = 2 + 2 * count + len(blocks_in) + len(before)
     return pl.pallas_call(
         kernel,
         grid_spec=pltpu.PrefetchScalarGridSpec(
             num_scalar_prefetch=1,
-            grid=(experts // step,),
+            grid=((high - low) // step,),
             in_specs=[whole((chunk, width))] * (2 * count)
             + [whole((rows, experts))]
-            + [block_of(block, *entry[1:-1]) for entry in flat for block in entry[-1]]
-            + [pl.BlockSpec(memory_space=pl.ANY)] * len(before),
-            out_specs=[
-                pl.BlockSpec((rows, width), lambda s, side: (0, 0)),
-                pl.BlockSpec((rows, experts), lambda s, side: (0, 0)),
-                h_spec,
-                h_spec,
-                h_spec,
-            ]
-            + [w_spec] * made_count,
+            + [block_of(block, *entry[1:-1], base) for entry in flat for block, base in entry[-1]]
+            + [whole(value.shape) for value in before]
+            + [pl.BlockSpec(memory_space=pl.ANY)] * len(aliased),
+            out_specs=[out_whole((chunk, width))] * count
+            + [out_whole((chunk, experts))] * count
+            + [h_spec] * 3
+            + [w_spec] * makes,
             scratch_shapes=[pltpu.VMEM((rows, width), jnp.float32)],
         ),
-        out_shape=[
-            jax.ShapeDtypeStruct((rows, width), bf16),
-            jax.ShapeDtypeStruct((rows, experts), jnp.float32),
-            kept,
-            kept,
-            kept,
-        ]
-        + [jax.ShapeDtypeStruct((experts, width, hidden), bf16)] * made_count,
-        input_output_aliases={
-            2 + 2 * count + len(blocks_in) + i: 2 + i for i in range(len(before))
-        },
+        out_shape=[jax.ShapeDtypeStruct((chunk, width), bf16)] * count
+        + [jax.ShapeDtypeStruct((chunk, experts), jnp.float32)] * count
+        + [kept] * 3
+        + [jax.ShapeDtypeStruct((experts, width, hidden), bf16)] * makes,
+        input_output_aliases={ahead + i: 2 * count + i for i in range(len(aliased))},
         compiler_params=pltpu.CompilerParams(vmem_limit_bytes=58 << 20),
         cost_estimate=pl.CostEstimate(
-            flops=10 * rows * width * hidden * experts,
-            transcendentals=rows * hidden * experts,
-            bytes_accessed=6 * experts * hidden * (width + rows) + 12 * rows * width,
+            flops=10 * rows * width * hidden * (high - low),
+            transcendentals=rows * hidden * (high - low),
+            bytes_accessed=6 * (high - low) * hidden * (width + rows) + 12 * rows * width,
         ),
         name="moe_first",
-    )(side, *xs, *fs, weight, *blocks_in, *before)
+    )(side, *xs, *fs, weight, *blocks_in, *before, *aliased)
 
 
 def add_pair(adds, sums):
@@ -669,7 +665,32 @@
         out[...] = total.astype(out.dtype)
 
 
-def moe_grad_split(xs, kept, axis, side, addends=()):
+def add_split(adds, outs, late, orders):
+    for p in range(2):
+        targets = (outs[p], outs[2 + p])
+
+        @pl.when(late == bool(p))
+        def _(p=p, targets=targets):
+            at = [0, 0]
+            for m in range(adds[0].shape[1]):
+                sent = 1 if m & (orders[p][0] // 2) else 0
+                total = adds[0][:, m].astype(jnp.float32) + adds[1][:, m].astype(jnp.float32)
+                targets[sent][:, at[sent]] = total.astype(jnp.bfloat16)
+                at[sent] += 1
+
+
+def split_outs(addend, steps):
+    experts, blocks = addend.shape[:2]
+    fewer = (blocks // 2,) + addend.shape[2:]
+    each = (experts // steps,) + fewer
+    specs = [
+        pl.BlockSpec(each, lambda h, *_: (jnp.minimum(h, steps // 2 - 1), 0, 0, 0)),
+        pl.BlockSpec(each, lambda h, *_: (jnp.maximum(h - steps // 2, 0), 0, 0, 0)),
+    ]
+    return specs * 2, [jax.ShapeDtypeStruct((experts // 2,) + fewer, jnp.bfloat16)] * 4
+
+
+def moe_grad_split(xs, kept, axis, side, flip, addends=(), split=False):
     chunk, width = xs[0].shape
     experts, tokens, hidden = kept.shape
     n = lax.axis_size(axis)
@@ -679,21 +700,33 @@
     def kernel(side_ref, *refs):
         h_ref, *adds = refs[count : count + 1 + len(addends)]
         keep_ref, send_ref, *sums, turned = refs[count + 1 + len(addends) :]
-        add_pair(adds, sums)
+        if split:
+            add_split(adds, sums, pl.program_id(0) >= experts // 2, cube_orders(axis))
+        else:
+            add_pair(adds, sums)
 
         @pl.when(pl.program_id(0) == 0)
         def _():
             for r in range(count):
-                turned[:, r * chunk : (r + 1) * chunk] = refs[r][...].T
-
-        mine = side_ref[0]
-        for q in range(n // 2):
-            for out, side in ((keep_ref, mine), (send_ref, 1 - mine)):
-                at = pl.multiple_of((2 * q + side) * block, block)
-                out[0, q] = dot32(turned[pl.ds(at, block), :], h_ref[0]).astype(jnp.bfloat16)
+                columns = refs[r][...].T
+                for j in range(n):
+                    place = j ^ side_ref[1]
+                    at = ((place ^ side_ref[0]) % 2) * (n // 2) + place // 2
+                    at = pl.multiple_of(at * block, block)
+                    turned[pl.ds(at, block), r * chunk : (r + 1) * chunk] = columns[
+                        j * block : (j + 1) * block
+                    ]
+
+        product = dot32(turned[...], h_ref[0]).astype(jnp.bfloat16)
+        product = product.reshape(n, block, hidden)
+        keep_ref[0] = product[: n // 2]
+        send_ref[0] = product[n // 2 :]
 
     half = pl.BlockSpec((1, n // 2, block, hidden), lambda e, side: (e, 0, 0, 0))
     shape = jax.ShapeDtypeStruct((experts, n // 2, block, hidden), jnp.bfloat16)
+    sum_specs, sum_shapes = [half] * (len(addends) // 2), [shape] * (len(addends) // 2)
+    if split:
+        sum_specs, sum_shapes = split_outs(addends[0], experts)
     return pl.pallas_call(
         kernel,
         grid_spec=pltpu.PrefetchScalarGridSpec(
@@ -705,10 +738,10 @@
             * count
             + [pl.BlockSpec((1, tokens, hidden), lambda e, side: (e, 0, 0))]
             + [half] * len(addends),
-            out_specs=[half, half] + [half] * (len(addends) // 2),
+            out_specs=[half, half] + sum_specs,
             scratch_shapes=[pltpu.VMEM((width, tokens), jnp.bfloat16)],
         ),
-        out_shape=[shape, shape] + [shape] * (len(addends) // 2),
+        out_shape=[shape, shape] + sum_shapes,
         compiler_params=pltpu.CompilerParams(vmem_limit_bytes=58 << 20),
         cost_estimate=pl.CostEstimate(
             flops=2 * tokens * width * hidden * experts,
@@ -716,7 +749,7 @@
             bytes_accessed=2 * experts * hidden * (width + tokens) + 2 * tokens * width,
         ),
         name="moe_grad_split",
-    )(jnp.asarray(side, jnp.int32).reshape(1), *xs, kept, *addends)
+    )(jnp.stack([jnp.asarray(side, jnp.int32), jnp.asarray(flip, jnp.int32)]), *xs, kept, *addends)
 
 
 def moe_out(wh, down_all):
@@ -801,28 +834,42 @@
     experts = down_weight.shape[0]
     half = experts // 2
     bits = bits_of(lax.axis_size("dp"))
+    quarter = experts // 4
     exchanged = [
-        {0: jnp.concatenate([w[at : at + half] for w in (gate_weight, up_weight, down_weight)])}
-        for at in (0, half)
+        jnp.concatenate([w[at : at + quarter] for w in (gate_weight, up_weight, down_weight)])
+        for at in range(0, experts, quarter)
     ]
+    masks = [[0] for _ in exchanged]
+    arriving = [None] * len(exchanged)
     far_orders = cube_orders("dp")
-
-    def exchange_far(stage):
-        for pieces, order in zip(exchanged, far_orders):
-            for mask in list(pieces):
-                pieces[mask ^ order[stage]] = swap(pieces[mask], "dp", order[stage])
-
-    def exchange_near():
-        for pieces in exchanged:
-            for mask in list(pieces):
-                if mask ^ 1 not in pieces and not mask & 1:
-                    pieces[mask ^ 1] = swap(pieces[mask], "dp", 1)
-
-    def exchange_with(*values):
-        leaves, tree = jax.tree.flatten(exchanged)
-        out = together(*values, *leaves)
-        exchanged[:] = jax.tree.unflatten(tree, out[len(values) :])
+    early, late = (0, 1), (2, 3)
+
+    def exchange_far(stage, sets):
+        for i in sets:
+            arriving[i] = swap(exchanged[i], "dp", far_orders[i % 2][stage])
+
+    def exchange_near(sets):
+        for i in sets:
+            arriving[i] = swap(exchanged[i], "dp", 1)
+
+    def arrived(sets, stage, *values):
+        out = together(*values, *(arriving[i] for i in sets))
+        for i, value in zip(sets, out[len(values) :]):
+            arriving[i] = value
+        for i in sets:
+            if stage is not None:
+                bit = far_orders[i % 2][stage]
+                exchanged[i] = jnp.concatenate([exchanged[i], arriving[i]])
+                masks[i] = masks[i] + [mask ^ bit for mask in masks[i]]
         return out[: len(values)]
+
+    def far_rest(sets):
+        for stage in range(1, len(far_orders[0])):
+            if stage > 1:
+                arrived(sets, stage - 1)
+            exchange_far(stage, sets)
+
+    last_far = len(far_orders[0]) - 1
 
     head_offset = here * query_w.shape[1]
     gain_attn = attn_norm_gain.astype(f32)
@@ -835,15 +882,13 @@
     )
     normed1, unit1, scale1 = rows_norm(local_x, gain_attn)
     normed1_ring = [normed1.astype(bf16)]
-    exchange_far(0)
+    exchange_far(0, early + late)
     for _ in range(1, around):
         normed1_ring.append(hop(normed1_ring[-1]))
     normed1_ring[-2], attn_all = together(normed1_ring[-2], attn_all)
     projected = projections(normed1_ring[:-1], attn_all, ring_chunks[:-1], around, None)
-    normed1_ring[-1], *projected = exchange_with(normed1_ring[-1], *projected)
-    first_pieces = [dict(pieces) for pieces in exchanged]
-    for stage in range(1, len(far_orders[0])):
-        exchange_far(stage)
+    normed1_ring[-1], *projected = arrived(early + late, 0, normed1_ring[-1], *projected)
+    far_rest(early)
     query_raw, key_raw, value_heads, squares = projections(
         normed1_ring[-1:], attn_all, ring_chunks[-1:], around, projected
     )
@@ -857,15 +902,15 @@
         query_raw, key_raw, value_heads, norm_scales, norm_gains, tables, marks
     )
     mixed_heads, final_ring[-1] = together(mixed_heads, final_ring[-1])
-    for pieces, early in zip(exchanged, first_pieces):
-        for mask, piece in early.items():
-            pieces[mask ^ 1] = swap(held_until(piece, mixed_heads), "dp", 1)
+    for i in late:
+        exchanged[i] = held_until(exchanged[i], mixed_heads)
+    far_rest(late)
     attn_local = dot32(rows_of(mixed_heads, (here - 1) % around), output_w, NT)
     for step in range(1, around):
         moved = hop(attn_local.astype(bf16))
-        if step + 1 == around:
-            (moved,) = exchange_with(moved)
-            exchange_near()
+        if step + 2 == around:
+            (moved,) = arrived(early, last_far, moved)
+            exchange_near(early)
         attn_local = moved.astype(f32) + dot32(
             rows_of(mixed_heads, (here - 1 - step) % around), output_w, NT
         )
@@ -874,72 +919,98 @@
 
     normed2_ring = [normed2.astype(bf16)]
     router_f = router_weight.astype(f32)
-    probs_ring, routed_ring, dx_ring, gate_grad_ring = [], [], [], []
+    probs_ring, routed_ring = [], []
     kept = None
     total = total_gate = None
-    arrays = [
-        [
-            (part * half, half, i * half, [pieces[mask] for mask in sorted(pieces)])
-            for part, pieces in enumerate(exchanged)
-        ]
-        for i in range(3)
-    ]
+
+    def gate_grad_of(s):
+        return jnp.where(routed_ring[s], gate_part[s], 0.0).T.reshape(-1)
+
+    late_far, late_far_near = {}, {}
+
+    def parts_of(sets):
+        groups = [[], [], []]
+        for j in sets:
+            places = {}
+            for at, mask in enumerate(masks[j]):
+                places[mask], places[mask ^ 1] = (exchanged[j], at), (arriving[j], at)
+                if j in late_far:
+                    turned = mask ^ far_orders[j % 2][last_far]
+                    places[turned], places[turned ^ 1] = (late_far[j], at), (late_far_near[j], at)
+            for i in range(3):
+                blocks = [
+                    (places[m][0], (3 * places[m][1] + i) * quarter) for m in sorted(places)
+                ]
+                groups[i].append((j * quarter, quarter, blocks))
+        return groups
+
     here_dp = lax.axis_index("dp")
     sides = jnp.stack([here_dp, here_dp, jnp.zeros_like(here_dp)]).astype(jnp.int32)
-    for call in [[s] for s in range(around)]:
-        last = call[-1]
-        if last + 1 < around:
-            normed2_ring.append(hop(normed2_ring[last]))
-        if len(final_ring) < around:
-            final_ring.append(hop(held_until(final_ring[-1], normed2_ring[last])))
+    dx_ring, gate_part = {}, {}
+    arrays = made = None
+    calls = [((0,), early), ((1,), early), ((0, 1), late)] + [((s,), None) for s in range(2, around)]
+    for number, (call, sets) in enumerate(calls):
+        if number + 1 < around:
+            normed2_ring.append(hop(normed2_ring[number]))
+        if len(final_ring) < around and number >= 2:
+            final_ring.append(hop(final_ring[-1]))
         for s in call:
+            if s < len(probs_ring):
+                continue
             probs_ring.append(jax.nn.softmax(dot32(normed2_ring[s], router_weight), axis=-1))
             route = rows_of(route_all, ring_chunks[s])
             routed_ring.append(
                 jnp.any(route[:, :, None] == jnp.arange(EXPERTS, dtype=jnp.int32), axis=1)
             )
-        weights = jnp.concatenate(
-            [jnp.where(routed_ring[s], probs_ring[s], 0.0) for s in call]
-        )
-        if last >= 2:
-            sent = dx_ring[last - 1] if total is None else (total + dx_ring[last - 1]).astype(bf16)
-            sent_gate = gate_grad_ring[last - 1] if total is None else total_gate + gate_grad_ring[last - 1]
-            moved, moved_gate = hop(sent), hop(sent_gate)
+        weights = jnp.concatenate([jnp.where(routed_ring[s], probs_ring[s], 0.0) for s in call])
+        flying = []
+        if sets is None:
+            s = call[0] - 1
+            sent = dx_ring[s] if total is None else (total + dx_ring[s]).astype(bf16)
+            sent_gate = gate_grad_of(s) if total is None else total_gate + gate_grad_of(s)
+            flying = [hop(sent), hop(sent_gate)]
         outs = moe_first(
             [normed2_ring[s] for s in call],
             [final_ring[s] for s in call],
             weights,
-            arrays,
+            arrays if sets != late and arrays is not None and number > 0 else parts_of(sets),
+            (0, experts) if sets is None else (half * (sets == late), half * (1 + (sets == late))),
             kept,
+            made if sets == late else None,
+            [(dx_ring[s], gate_part[s]) for s in call] if sets == late else None,
             call[0],
             length,
             sides,
         )
-        waiting = [normed2_ring[-1], final_ring[-1]] + ([moved, moved_gate] if last >= 2 else [])
+        waiting = [normed2_ring[-1], final_ring[-1], *flying]
         held = together(*outs, *waiting)
         outs, waiting = held[: len(outs)], held[len(outs) :]
         normed2_ring[-1], final_ring[-1] = waiting[:2]
-        if last >= 2:
+        if number == 0:
+            (normed2_ring[-1],) = arrived(late, None, normed2_ring[-1])
+            late_far = {i: arriving[i] for i in late}
+            late_far_near = {i: swap(late_far[i], "dp", 1) for i in late}
+            exchange_near(late)
+        if flying:
             total, total_gate = waiting[2].astype(f32), waiting[3]
+        count = len(call)
         for i, s in enumerate(call):
-            dx_ring.append(outs[0][i * rows_here : (i + 1) * rows_here])
-            grads = jnp.where(routed_ring[s], outs[1][i * rows_here : (i + 1) * rows_here], 0.0)
-            gate_grad_ring.append(grads.T.reshape(-1))
-        kept = outs[2:5]
-        if len(outs) > 5:
-            arrays = outs[5:]
+            dx_ring[s], gate_part[s] = outs[i], outs[count + i]
+        kept = outs[2 * count : 2 * count + 3]
+        if len(outs) > 2 * count + 3:
+            arrays = made = outs[2 * count + 3 :]
     weighted_hidden, grad_gpre, grad_upre = kept
     down_all = arrays[2]
     sent = (total + dx_ring[around - 1]).astype(bf16)
-    sent_gate = total_gate + gate_grad_ring[around - 1]
+    sent_gate = total_gate + gate_grad_of(around - 1)
     moved, moved_gate = hop(sent), hop(sent_gate)
     gate_keep, gate_send = moe_grad_split(
-        normed2_ring, held_until(grad_gpre, sent), "dp", own_side
+        normed2_ring, held_until(grad_gpre, sent), "dp", own_side, 0
     )
     moved, moved_gate, gate_keep, gate_send = together(moved, moved_gate, gate_keep, gate_send)
     gate_moved = swap(gate_send, "dp", 1)
     normed2_grad = moved.astype(f32) + dx_ring[0].astype(f32)
-    prob_grad = (moved_gate + gate_grad_ring[0]).reshape(EXPERTS, rows_here).T
+    prob_grad = (moved_gate + gate_grad_of(0)).reshape(EXPERTS, rows_here).T
     probs_here = probs_ring[0]
     grad_logits = probs_here * (prob_grad - jnp.sum(probs_here * prob_grad, axis=1, keepdims=True))
     normed2_grad = normed2_grad + jnp.dot(
@@ -960,7 +1031,7 @@
     resid_ring = [grad_resid.astype(bf16)]
     moved = hop(resid_ring[0])
     up_keep, up_send, gate_sum = moe_grad_split(
-        normed2_ring, held_until(grad_upre, resid_ring[0]), "dp", own_side, (gate_keep, gate_moved)
+        normed2_ring, held_until(grad_upre, resid_ring[0]), "dp", 0, here_dp, (gate_keep, gate_moved)
     )
     moved, up_keep, up_send, gate_sum = together(moved, up_keep, up_send, gate_sum)
     resid_ring.append(moved)
@@ -972,13 +1043,18 @@
     resid_ring.append(moved)
     for step in range(3, around):
         resid_ring.append(hop(resid_ring[-1]))
-    down_keep, down_send, up_sum = moe_grad_split(
-        final_ring, held_until(weighted_hidden, moe_part), "dp", 0, (up_keep, up_moved)
-    )
-    resid_ring[-1], down_keep, down_send, up_sum = together(
-        resid_ring[-1], down_keep, down_send, up_sum
-    )
-    reduced_up = reduce_rows(up_sum)
+    down_keep, down_send, *up_split = moe_grad_split(
+        final_ring, held_until(weighted_hidden, moe_part), "dp", 0, 0, (up_keep, up_moved), True
+    )
+    resid_ring[-1], down_keep, down_send, *up_split = together(
+        resid_ring[-1], down_keep, down_send, *up_split
+    )
+
+    def cube_begin(split):
+        flying = [swap(sent, "dp", order[0]) for sent, order in zip(split[2:], cube_orders("dp"))]
+        return CubeScatter(split[:2], "dp"), flying
+
+    up_cube, up_flying = cube_begin(up_split)
     down_moved = swap(down_send, "dp", 1)
     resid_full = in_order(resid_ring, "tensor")
     grad_mixed = dot32(resid_full, output_w).astype(bf16)
@@ -1002,13 +1078,13 @@
     query_gained, key_gained, inner_part, reduced_gate, moe_moved, *down_split = together(
         query_gained, key_gained, inner_part, reduced_gate, moe_moved, *down_split
     )
-    down_cube = CubeScatter(down_split[:2], "dp")
-    down_flying = [
-        swap(sent, "dp", order[0]) for sent, order in zip(down_split[2:], cube_orders("dp"))
-    ]
+    down_cube, down_flying = cube_begin(down_split)
     moe_local = moe_moved.astype(f32) + moe_part[2 * rows_here : 3 * rows_here].astype(f32)
     moe_moved = hop(moe_local.astype(bf16))
     inner_sums = all_sum(inner_part[:, 0], ("tensor",)).T / model_width
+    inner_sums, *up_flying = together(inner_sums, *up_flying)
+    up_cube.finish(up_flying)
+    up_flying = up_cube.start()
     back_order = [(here - 1 - step) % around for step in range(around)]
     query_raw_low, key_raw_low, normed1_parts = projection_back(
         (query_raw, key_raw),
@@ -1028,9 +1104,13 @@
         [query_raw_low, key_raw_low, value_low, held_until(mixed_heads, first)],
         "dp",
     )
-    moved, attn_keep, attn_send, moe_moved, *down_flying = together(
-        moved, attn_keep, attn_send, moe_moved, *down_flying
-    )
+    moved, attn_keep, attn_send, moe_moved, up_flying, down_flying = jax.tree.unflatten(
+        jax.tree.structure((0, 0, 0, 0, [0, 0], [0, 0])),
+        together(moved, attn_keep, attn_send, moe_moved, *up_flying, *down_flying),
+    )
+    up_cube.finish(up_flying)
+    while up_cube.orders[0]:
+        up_cube.finish(up_cube.start())
     attn_moved = swap(attn_send, "dp", 1)
     down_cube.finish(down_flying)
     while down_cube.orders[0]:
@@ -1040,12 +1120,16 @@
         if step + 1 < around:
             moved = hop(normed1_grad.astype(bf16))
         if step == 1:
-            attn_sum = pair_sum(attn_keep, attn_moved)
-            moved, attn_sum = together(moved, attn_sum)
-            reduced_attn = reduce_rows(attn_sum)
-    normed1_grad, reduced_up = together(normed1_grad, reduced_up)
+            attn_split = pair_split(attn_keep, attn_moved, "dp")
+            attn_cube, attn_flying = cube_begin(attn_split)
+    normed1_grad, moe_moved, *attn_flying = together(normed1_grad, moe_moved, *attn_flying)
+    attn_cube.finish(attn_flying)
+    while attn_cube.orders[0]:
+        attn_cube.finish(attn_cube.start())
+    reduced_up = up_cube.result()
+    reduced_attn = attn_cube.result()
     moe_local = moe_moved.astype(f32) + moe_part[3 * rows_here :].astype(f32)
-    moe_moved = hop(held_until(moe_local.astype(bf16), normed1_grad))
+    moe_moved = hop(moe_local.astype(bf16))
     layer_local = resid + xor_blocks(moe_moved.astype(f32) + moe_part[:rows_here].astype(f32), "dp")
     layer_local = layer_local.astype(bf16)
     reduced_down = down_cube.result()
@@ -1061,17 +1145,17 @@
         jnp.concatenate(
             [grad_router_part.T, grad_expert_part[None], gains_full, grad_attn_part[None]]
         ),
-        ("tensor", "dp"),
+        ("dp", "tensor"),
     )
     return (
         layer_local[None],
         grad_input[None],
-        reduced_attn[0].astype(f32),
-        reduced_attn[1].astype(f32),
-        reduced_attn[2].astype(f32),
-        reduced_attn[3].astype(f32),
+        reduced_attn[0],
+        reduced_attn[1],
+        reduced_attn[2],
+        reduced_attn[3],
         reduced_gate.astype(f32),
-        reduced_up.astype(f32),
+        reduced_up,
         reduced_down,
         sums[:EXPERTS].T,
         sums[EXPERTS + 3],

time: 949 us -> 886 us (0.934)
  waiting for transfers between devices: 351 us -> 268 us
  Pallas kernels: 386 us -> 356 us
  local copies, waits for them, and re-layouts: 26.8 us -> 50.8 us
  other arithmetic: 84.1 us -> 97.5 us
  starting transfers between devices: 49.1 us -> 59.9 us
    ppermute x31 -> x39, waiting for transfers between devices: 182 us -> 110 us  [swap(): return lax.ppermute(value, axis, [(i, i ^ bit) for i in range(n)])]
    pallas_call x4 -> x5, Pallas kernels: 169 us -> 144 us  [moe_first(): pl.pallas_call(kernel, grid_spec=pltpu.PrefetchScalarGridSpec(num_scalar_...]
    unnamed x110 -> x205, local copies, waits for them, and re-layouts: 4.53 us -> 16.8 us
    concatenate x2 -> x8, other arithmetic: 2.22 us -> 14.3 us  [the longest x3 8.16 us: arrived(): exchanged[i] = jnp.concatenate([exchanged[i], arriving[i]])]
    ppermute x27, waiting for transfers between devices: 137 us -> 127 us  [ring_hop(): return lax.ppermute(total, axis, [(i, (i + 1) % n) for i in range(n)])]
    ppermute x31 -> x39, starting transfers between devices: 26.9 us -> 37 us  [swap(): return lax.ppermute(value, axis, [(i, i ^ bit) for i in range(n)])]
  transfers between devices with their start and end apart: 62 -> 68, of which waited for: 31 -> 30; matrix products, arithmetic and copies ran while one was open for 13% -> 17% of each run, Pallas kernels for 40% -> 40%
where the time goes in v3:
time: 886 us; the launch traced here: 878 us
  Pallas kernels  356 us (40%)
  waiting for transfers between devices  268 us (30%)
  other arithmetic  97.5 us (11%)
  starting transfers between devices  59.9 us (7%)
  local copies, waits for them, and re-layouts  50.8 us (6%)
  matrix products  30.1 us (3%)
  between operations  15.7 us (2%)
    pallas_call x5, Pallas kernels, moe_first(): pl.pallas_call(kernel, grid_spec=pltpu.PrefetchScalarGridSpec(num_scalar_...  144 us
    ppermute x27, waiting for transfers between devices, ring_hop(): return lax.ppermute(total, axis, [(i, (i + 1) % n) for i in range(n)])  127 us
    ppermute x39, waiting for transfers between devices, swap(): return lax.ppermute(value, axis, [(i, i ^ bit) for i in range(n)])  110 us
    pallas_call x3, Pallas kernels, moe_grad_split(): pl.pallas_call(kernel, grid_spec=pltpu.PrefetchScalarGridSpec(num_scalar_...  86.4 us
    ppermute x39, starting transfers between devices, swap(): return lax.ppermute(value, axis, [(i, i ^ bit) for i in range(n)])  37 us
    all_gather x1, waiting for transfers between devices, on_device(): lax.all_gather(jnp.stack([query_weight, key_weight, value_weight, output_...  30.7 us
    pallas_call x1, Pallas kernels, attention_backward(): pl.pallas_call(kernel, grid=(heads,), in_specs=[head, head, head, head, h...  29.5 us
    pallas_call x1, Pallas kernels, moe_out(): pl.pallas_call(kernel, grid=(experts,), in_specs=[pl.BlockSpec((1, tokens...  26.2 us
  transfers between devices with their start and end apart: 68, of which 30 were waited for; matrix products, arithmetic and copies ran while one was open for 17% of the time, Pallas kernels for 40%

profile of v3, /device:TPU:0, one launch (start us, length us, event | category | flops | bytes accessed | tf_op | source)
XLA Modules:
  0.0 878.0 jit_solution(2755348481491843399)
XLA Ops:
  47.3 19.0 %collective-permute-done.1.refs_2_ = bf16[256,2048]{1,0:T(8,128)(2,1)} collective-permute-done((bf16[256,2048]{1,0:T(8,128)(2,1)}, bf16[256,2048]{1,0:T(8,128)(2,1)}, u32[]{:S(2)}, u32[]{:S(2)}) %collective-permute-start.1) | collective-permute-done | bytes 1048608 | tf_op jit(solution)/shard_map/ppermute | solution.py:108
  70.8 30.7 %all-gather.2.cloned.1.call-done.refs_3_.refs_1_.w_ref = bf16[4,2048,512]{2,1,0:T(8,128)(2,1)} async-done(((bf16[4,256,512]{2,1,0:T(8,128)(2,1)}), bf16[4,2048,512]{2,1,0:T(8,128)(2,1)}) %all-gather.2.cloned.1.call-update) | async-done | bytes 8388624 | tf_op jit(solution)/shard_map/all_gather | solution.py:830
  101.5 11.1 %projections.2 = (f32[1024,512]{1,0:T(8,128)}, f32[1024,512]{1,0:T(8,128)}, bf16[1024,512]{1,0:T(8,128)(2,1)}, f32[2,8,1024]{2,1,0:T(8,128)}) custom-call(s32[3]{0:T(128)} %pad_add_fusion.1.place_ref, bf16[256,2048]{1,0:T(8,128)(2,1)} %fusion.4.refs_0_, bf16[256,2048]{1,0:T(8,128)(2,1)} %collective-permute-done.refs_1_, ...), custom_call_target="tpu_custom_call" | custom-call | flops 4831838208 | bytes 13369344 | tf_op jit(solution)/shard_map/projections/pallas_call | solution.py:184
  112.6 12.5 %collective-permute-done.4 = bf16[12,256,256]{2,1,0:T(8,128)(2,1)S(1)} collective-permute-done((bf16[12,256,256]{2,1,0:T(8,128)(2,1)}, bf16[12,256,256]{2,1,0:T(8,128)(2,1)S(1)}, u32[]{:S(2)}, u32[]{:S(2)}) %collective-permute-start.4) | collective-permute-done | bytes 1572896 | tf_op jit(solution)/shard_map/ppermute | solution.py:65
  153.1 14.9 %attention_forward.1 = (bf16[1024,512]{1,0:T(8,128)(2,1)}, bf16[1024,512]{1,0:T(8,128)(2,1)}, bf16[1024,512]{1,0:T(8,128)(2,1)}) custom-call(f32[1024,512]{1,0:T(8,128)} %get-tuple-element.215.q_ref.qr_ref.qr, f32[1024,512]{1,0:T(8,128)} %get-tuple-element.216.k_ref.kr_ref.kr, bf16[1024,512]{1,0:T(8,128)(2,1)} %get-tuple-element.217.v_ref, ...), custom_call_target="tpu_custom_call" | custom-call | flops 1610612736 | bytes 8388608 | tf_op jit(solution)/shard_map/attention_forward/pallas_call | solution.py:378
  172.9 22.1 %collective-permute-done.10 = bf16[256,2048]{1,0:T(8,128)(2,1)} collective-permute-done((bf16[256,2048]{1,0:T(8,128)(2,1)}, bf16[256,2048]{1,0:T(8,128)(2,1)}, u32[]{:S(2)}, u32[]{:S(2)}) %collective-permute-start.10) | collective-permute-done | bytes 1048608 | tf_op jit(solution)/shard_map/ppermute | solution.py:108
  200.2 11.5 %collective-permute-done.13 = bf16[24,256,256]{2,1,0:T(8,128)(2,1)} collective-permute-done((bf16[24,256,256]{2,1,0:T(8,128)(2,1)}, bf16[24,256,256]{2,1,0:T(8,128)(2,1)}, u32[]{:S(2)}, u32[]{:S(2)}) %collective-permute-start.13) | collective-permute-done | bytes 3145760 | tf_op jit(solution)/shard_map/ppermute | solution.py:65
  238.6 21.0 %collective-permute-done.14 = bf16[256,2048]{1,0:T(8,128)(2,1)} collective-permute-done((bf16[256,2048]{1,0:T(8,128)(2,1)}, bf16[256,2048]{1,0:T(8,128)(2,1)}, u32[]{:S(2)}, u32[]{:S(2)}) %collective-permute-start.14) | collective-permute-done | bytes 1048608 | tf_op jit(solution)/shard_map/ppermute | solution.py:108
  268.4 27.0 %moe_first.5 = (bf16[256,2048]{1,0:T(8,128)(2,1)}, f32[256,16]{1,0:T(8,128)}, bf16[16,1024,256]{2,1,0:T(8,128)(2,1)}, bf16[16,1024,256]{2,1,0:T(8,128)(2,1)}, bf...) custom-call(s32[3]{0:T(128)} %pad_add_fusion.3.side_ref, ...), custom_call_target="tpu_custom_call" | custom-call | flops 10737418240 | bytes 34603008 | tf_op jit(solution)/shard_map/moe_first/pallas_call | solution.py:631
  314.5 18.3 %moe_first.6 = (bf16[256,2048]{1,0:T(8,128)(2,1)}, f32[256,16]{1,0:T(8,128)}, bf16[16,1024,256]{2,1,0:T(8,128)(2,1)}, bf16[16,1024,256]{2,1,0:T(8,128)(2,1)}, bf16[16,1024,256]{2,1,0:T(8,128)(2,1)}) custom-call(s32[3]{0:T(128)} %pad_add_fusion.3.side_ref, ...), custom_call_target="tpu_custom_call", output_to_operand_aliasing={{2}: (7, {}), {3}: (8, {}), {4}: (9, {})} | custom-call | flops 10737418240 | bytes 34603008 | tf_op jit(solution)/shard_map/moe_first/pallas_call | solution.py:631
  340.4 37.4 %moe_first.7 = (bf16[256,2048]{1,0:T(8,128)(2,1)}, bf16[256,2048]{1,0:T(8,128)(2,1)}, f32[256,16]{1,0:T(8,128)}, f32[256,16]{1,0:T(8,128)}, bf16[16,1024,256]{2,...) custom-call(s32[3]{0:T(128)} %pad_add_fusion.3.side_ref, ...), custom_call_target="tpu_custom_call", output_to_operand_aliasing={{4}: (58, {}), {5}: (59, {}), {6}: (60, {}), {7}: (61, {}),... | custom-call | flops 21474836480 | bytes 44040192 | tf_op jit(solution)/shard_map/moe_first/pallas_call | solution.py:631
  387.8 30.6 %moe_first.8 = (bf16[256,2048]{1,0:T(8,128)(2,1)}, f32[256,16]{1,0:T(8,128)}, bf16[16,1024,256]{2,1,0:T(8,128)(2,1)}, bf16[16,1024,256]{2,1,0:T(8,128)(2,1)}, bf16[16,1024,256]{2,1,0:T(8,128)(2,1)}) custom-call(s32[3]{0:T(128)} %pad_add_fusion.3.side_ref, ...), custom_call_target="tpu_custom_call", output_to_operand_aliasing={{2}: (7, {}), {3}: (8, {}), {4}: (9, {})} | custom-call | flops 21474836480 | bytes 62914560 | tf_op jit(solution)/shard_map/moe_first/pallas_call | solution.py:631
  418.4 16.3 %collective-permute-done.28 = bf16[256,2048]{1,0:T(8,128)(2,1)S(1)} collective-permute-done((bf16[256,2048]{1,0:T(8,128)(2,1)}, bf16[256,2048]{1,0:T(8,128)(2,1)S(1)}, u32[]{:S(2)}, u32[]{:S(2)}) %collective-permute-start.28) | collective-permute-done | bytes 1048608 | tf_op jit(solution)/shard_map/ppermute | solution.py:108
  441.0 30.4 %moe_first.9 = (bf16[256,2048]{1,0:T(8,128)(2,1)}, f32[256,16]{1,0:T(8,128)}, bf16[16,1024,256]{2,1,0:T(8,128)(2,1)}, bf16[16,1024,256]{2,1,0:T(8,128)(2,1)}, bf16[16,1024,256]{2,1,0:T(8,128)(2,1)}) custom-call(s32[3]{0:T(128)} %pad_add_fusion.3.side_ref, ...), custom_call_target="tpu_custom_call", output_to_operand_aliasing={{2}: (7, {}), {3}: (8, {}), {4}: (9, {})} | custom-call | flops 21474836480 | bytes 62914560 | tf_op jit(solution)/shard_map/moe_first/pallas_call | solution.py:631
  479.0 25.6 %moe_grad_split.3 = (bf16[16,4,256,256]{3,2,1,0:T(8,128)(2,1)}, bf16[16,4,256,256]{3,2,1,0:T(8,128)(2,1)}) custom-call(s32[2]{0:T(128)} %pad_add_fusion.4.side_ref, bf16[256,2048]{1,0:T(8,128)(2,1)} %multiply_convert_fusion.refs_0_, bf16[256,2048]{1,0:T(8,128)(2,1)} %collective-permute-done.17.refs_0_.refs_1_, ...), custom_call_target="tpu_custom_call" | custom-call | flops 17179869184 | bytes 29360128 | tf_op jit(solution)/shard_map/moe_grad_split/pallas_call | solution.py:730
  518.1 30.8 %moe_grad_split.4 = (bf16[16,4,256,256]{3,2,1,0:T(8,128)(2,1)}, bf16[16,4,256,256]{3,2,1,0:T(8,128)(2,1)}, bf16[16,4,256,256]{3,2,1,0:T(8,128)(2,1)}) custom-call(s32[2]{0:T(128)} %pad_add_fusion.5.side_ref, bf16[256,2048]{1,0:T(8,128)(2,1)} %multiply_convert_fusion.refs_0_, bf16[256,2048]{1,0:T(8,128)(2,1)} %collective-permute-done.17.refs_0_.refs_1_, ...), custom_call_target="tpu_custom_call" | custom-call | flops 17179869184 | bytes 29360128 | tf_op jit(solution)/shard_map/moe_grad_split/pallas_call | solution.py:730
  549.7 26.2 %moe_out.1 = bf16[1024,2048]{1,0:T(8,128)(2,1)} custom-call(bf16[16,1024,256]{2,1,0:T(8,128)(2,1)} %get-tuple-element.334.h_ref.refs_4_, bf16[16,2048,256]{2,1,0:T(8,128)(2,1)} %get-tuple-element.280.refs_5_.d_ref), custom_call_target="tpu_custom_call" | custom-call | flops 17179869184 | bytes 29360128 | tf_op jit(solution)/shard_map/moe_out/pallas_call | solution.py:772
  577.5 30.1 %moe_grad_split.5 = (bf16[16,4,256,256]{3,2,1,0:T(8,128)(2,1)}, bf16[16,4,256,256]{3,2,1,0:T(8,128)(2,1)}, bf16[8,2,256,256]{3,2,1,0:T(8,128)(2,1)}, bf16[8,2,25...) custom-call(s32[2]{0:T(128)} %broadcast_4_side_ref.2.side_ref, ...), custom_call_target="tpu_custom_call" | custom-call | flops 17179869184 | bytes 29360128 | tf_op jit(solution)/shard_map/moe_grad_split/pallas_call | solution.py:730
  623.6 29.5 %attention_backward.1 = (f32[1024,512]{1,0:T(8,128)}, f32[1024,512]{1,0:T(8,128)}, bf16[1024,512]{1,0:T(8,128)(2,1)}, f32[2,8,1024]{2,1,0:T(8,128)}, f32[2,512]{...) custom-call(bf16[1024,512]{1,0:T(8,128)(2,1)} %get-tuple-element.225, ...), custom_call_target="tpu_custom_call" | custom-call | flops 4026531840 | bytes 13631488 | tf_op jit(solution)/shard_map/attention_backward/pallas_call | solution.py:473
  690.0 13.6 %projection_back.1 = (bf16[1024,512]{1,0:T(8,128)(2,1)}, bf16[1024,512]{1,0:T(8,128)(2,1)}, bf16[4,256,2048]{2,1,0:T(8,128)(2,1)}) custom-call(s32[4]{0:T(128)} %pad_add_fusion.2.place_ref, f32[1024,512]{1,0:T(8,128)} %get-tuple-element.215.q_ref.qr_ref.qr, f32[1024,512]{1,0:T(8,128)} %get-tuple-element.216.k_ref.kr_ref.kr, ...), custom_call_target="tpu_custom_call" | custom-call | flops 6442450944 | bytes 22020096 | tf_op jit(solution)/shard_map/projection_back/pallas_call | solution.py:237
  708.3 18.8 %projection_grads.1 = (bf16[4,4,256,512]{3,2,1,0:T(8,128)(2,1)}, bf16[4,4,256,512]{3,2,1,0:T(8,128)(2,1)}) custom-call(s32[5]{0:T(128)} %stack.97.place_ref, bf16[256,2048]{1,0:T(8,128)(2,1)} %fusion.4.refs_0_, bf16[256,2048]{1,0:T(8,128)(2,1)} %collective-permute-done.refs_1_, bf16[256,2048]{1,0:T(8,128)(2,1)} %collective-permute-done.1.refs_2_, ...), custom_call_target="tpu_custom_call" | custom-call | flops 8589934592 | bytes 20971520 | tf_op jit(solution)/shard_map/projection_grads/pallas_call | solution.py:318
  727.1 18.2 %collective-permute-done.48 = bf16[8,256,256]{2,1,0:T(8,128)(2,1)} collective-permute-done((bf16[8,256,256]{2,1,0:T(8,128)(2,1)}, bf16[8,256,256]{2,1,0:T(8,128)(2,1)}, u32[]{:S(2)}, u32[]{:S(2)}) %collective-permute-start.48) | collective-permute-done | bytes 1048608 | tf_op jit(solution)/shard_map/ppermute | solution.py:65
  766.4 13.8 %collective-permute-done.51 = bf16[256,2048]{1,0:T(8,128)(2,1)S(1)} collective-permute-done((bf16[256,2048]{1,0:T(8,128)(2,1)S(1)}, bf16[256,2048]{1,0:T(8,128)(2,1)S(1)}, u32[]{:S(2)}, u32[]{:S(2)}) %collective-permute-start.51) | collective-permute-done | bytes 1048608 | tf_op jit(solution)/shard_map/ppermute | solution.py:108
  796.4 12.2 %collective-permute-done.52 = bf16[256,2048]{1,0:T(8,128)(2,1)} collective-permute-done((bf16[256,2048]{1,0:T(8,128)(2,1)}, bf16[256,2048]{1,0:T(8,128)(2,1)}, u32[]{:S(2)}, u32[]{:S(2)}) %collective-permute-start.52) | collective-permute-done | bytes 1048608 | tf_op jit(solution)/shard_map/ppermute | solution.py:108
  (498 shorter events, 340.8 us)
Async XLA Ops:
  7.2 94.3 %all-gather.2.cloned.1.call-start = ((), (), s32[]{:S(2)}) async-start(), calls=%async_computation.1 | async-start | bytes 9437184 | tf_op jit(solution)/shard_map/all_gather | solution.py:830
  9.7 643.5 %reduce-scatter.2.cloned.1.call-start = ((), (), s32[]{:S(2)}) async-start(), calls=%async_computation.2 | async-start | bytes 10485760 | tf_op jit(solution)/shard_map/reduce_scatter | solution.py:1023
  21.6 91.0 %collective-permute-start.6 = (bf16[12,256,256]{2,1,0:T(8,128)(2,1)}, bf16[12,256,256]{2,1,0:T(8,128)(2,1)}, u32[]{:S(2)}, u32[]{:S(2)}) collective-permute-start(bf16[12,256,256]{2,1,0:T(8,128)(2,1)} %pad_maximum_fusion.9), channel_id=1, source_target_pairs={{0,16},{4,20},{8,24},{12,28},{16,0},{20,4},{24,8},{28,12},{1,17},{... | collective-permute-start | bytes 4718600 | tf_op jit(solution)/shard_map/ppermute | solution.py:65
  24.4 88.2 %collective-permute-start.5 = (bf16[12,256,256]{2,1,0:T(8,128)(2,1)}, bf16[12,256,256]{2,1,0:T(8,128)(2,1)}, u32[]{:S(2)}, u32[]{:S(2)}) collective-permute-start(bf16[12,256,256]{2,1,0:T(8,128)(2,1)} %pad_maximum_fusion.8), channel_id=1, source_target_pairs={{0,8},{4,12},{8,0},{12,4},{16,24},{20,28},{24,16},{28,20},{1,9},{5... | collective-permute-start | bytes 4718600 | tf_op jit(solution)/shard_map/ppermute | solution.py:65
  27.3 97.8 %collective-permute-start.4 = (bf16[12,256,256]{2,1,0:T(8,128)(2,1)}, bf16[12,256,256]{2,1,0:T(8,128)(2,1)S(1)}, u32[]{:S(2)}, u32[]{:S(2)}) collective-permute-start(bf16[12,256,256]{2,1,0:T(8,128)(2,1)} %pad_maximum_fusion.7), channel_id=1, source_target_pairs={{0,16},{4,20},{8,24},{12,28},{16,0},{20,4},{24,8},{28,12},{1,17},{... | collective-permute-start | bytes 4718600 | tf_op jit(solution)/shard_map/ppermute | solution.py:65
  29.1 96.0 %collective-permute-start.3 = (bf16[12,256,256]{2,1,0:T(8,128)(2,1)}, bf16[12,256,256]{2,1,0:T(8,128)(2,1)S(1)}, u32[]{:S(2)}, u32[]{:S(2)}) collective-permute-start(bf16[12,256,256]{2,1,0:T(8,128)(2,1)} %pad_maximum_fusion.6), channel_id=1, source_target_pairs={{0,8},{4,12},{8,0},{12,4},{16,24},{20,28},{24,16},{28,20},{1,9},{5... | collective-permute-start | bytes 4718600 | tf_op jit(solution)/shard_map/ppermute | solution.py:65
  66.4 58.7 %collective-permute-start.2 = (bf16[256,2048]{1,0:T(8,128)(2,1)}, bf16[256,2048]{1,0:T(8,128)(2,1)}, u32[]{:S(2)}, u32[]{:S(2)}) collective-permute-start(bf16[256,2048]{1,0:T(8,128)(2,1)} %collective-permute-done.1.refs_2_), channel_id=1, source_target_pairs={{0,1},{1,2},{2,3},{3,0},{4,5},{5,6},{6,7},{7,4},{8,9},{9,10},{10,1... | collective-permute-start | bytes 3145736 | tf_op jit(solution)/shard_map/ppermute | solution.py:108
  144.4 67.3 %collective-permute-start.13 = (bf16[24,256,256]{2,1,0:T(8,128)(2,1)}, bf16[24,256,256]{2,1,0:T(8,128)(2,1)}, u32[]{:S(2)}, u32[]{:S(2)}) collective-permute-start(bf16[24,256,256]{2,1,0:T(8,128)(2,1)} %pad_maximum_fusion.3), channel_id=1, source_target_pairs={{0,8},{4,12},{8,0},{12,4},{16,24},{20,28},{24,16},{28,20},{1,9},{5... | collective-permute-start | bytes 9437192 | tf_op jit(solution)/shard_map/ppermute | solution.py:65
  147.7 67.1 %collective-permute-start.12 = (bf16[24,256,256]{2,1,0:T(8,128)(2,1)}, bf16[24,256,256]{2,1,0:T(8,128)(2,1)}, u32[]{:S(2)}, u32[]{:S(2)}) collective-permute-start(bf16[24,256,256]{2,1,0:T(8,128)(2,1)} %pad_maximum_fusion.2), channel_id=1, source_target_pairs={{0,16},{4,20},{8,24},{12,28},{16,0},{20,4},{24,8},{28,12},{1,17},{... | collective-permute-start | bytes 9437192 | tf_op jit(solution)/shard_map/ppermute | solution.py:65
  224.0 43.9 %collective-permute-start.16 = (bf16[48,256,256]{2,1,0:T(8,128)(2,1)}, bf16[48,256,256]{2,1,0:T(8,128)(2,1)}, u32[]{:S(2)}, u32[]{:S(2)}) collective-permute-start(bf16[48,256,256]{2,1,0:T(8,128)(2,1)} %constant_dynamic-update-slice_fusion.5.refs_11_.refs_13_.refs_15_.refs_17_.refs_27_.refs_29_.refs_31_.refs_, ...), channel_id=1, source_target_pairs={{0,4},{4,0},{8,12},{12,8},{16,20},{20,16},{24,28},{28,24},{1,5},{5... | collective-permute-start | bytes 18874376 | tf_op jit(solution)/shard_map/ppermute | solution.py:65
  235.8 70.3 %collective-permute-start.19 = (bf16[24,256,256]{2,1,0:T(8,128)(2,1)}, bf16[24,256,256]{2,1,0:T(8,128)(2,1)}, u32[]{:S(2)}, u32[]{:S(2)}) collective-permute-start(bf16[24,256,256]{2,1,0:T(8,128)(2,1)} %get-tuple-element.242.refs_13_.refs_17_.refs_29_.refs_33_.refs_45_.refs_49_), channel_id=1, source_target_pairs={{0,8},{4,12},{8,0},{12,4},{16,24},{20,28},{24,16},{28,20},{1,9},{5... | collective-permute-start | bytes 9437192 | tf_op jit(solution)/shard_map/ppermute | solution.py:65
  236.8 69.8 %collective-permute-start.18 = (bf16[24,256,256]{2,1,0:T(8,128)(2,1)S(1)}, bf16[24,256,256]{2,1,0:T(8,128)(2,1)}, u32[]{:S(2)}, u32[]{:S(2)}) collective-permute-start(bf16[24,256,256]{2,1,0:T(8,128)(2,1)S(1)} %get-tuple-element.240.refs_5_.refs_7_.refs_21_.refs_23_.refs_37_.refs_39_), channel_id=1, source_target_pairs={{0,16},{4,20},{8,24},{12,28},{16,0},{20,4},{24,8},{28,12},{1,17},{... | collective-permute-start | bytes 9437192 | tf_op jit(solution)/shard_map/ppermute | solution.py:65
  267.9 70.8 %collective-permute-start.23 = (bf16[24,256,256]{2,1,0:T(8,128)(2,1)}, bf16[24,256,256]{2,1,0:T(8,128)(2,1)}, u32[]{:S(2)}, u32[]{:S(2)}) collective-permute-start(bf16[24,256,256]{2,1,0:T(8,128)(2,1)} %get-tuple-element.242.refs_13_.refs_17_.refs_29_.refs_33_.refs_45_.refs_49_), channel_id=1, source_target_pairs={{0,4},{4,0},{8,12},{12,8},{16,20},{20,16},{24,28},{28,24},{1,5},{5... | collective-permute-start | bytes 9437192 | tf_op jit(solution)/shard_map/ppermute | solution.py:65
  267.9 72.4 %collective-permute-start.21 = (bf16[24,256,256]{2,1,0:T(8,128)(2,1)S(1)}, bf16[24,256,256]{2,1,0:T(8,128)(2,1)}, u32[]{:S(2)}, u32[]{:S(2)}) collective-permute-start(bf16[24,256,256]{2,1,0:T(8,128)(2,1)S(1)} %get-tuple-element.240.refs_5_.refs_7_.refs_21_.refs_23_.refs_37_.refs_39_), channel_id=1, source_target_pairs={{0,4},{4,0},{8,12},{12,8},{16,20},{20,16},{24,28},{28,24},{1,5},{5... | collective-permute-start | bytes 9437192 | tf_op jit(solution)/shard_map/ppermute | solution.py:65
  336.0 41.8 %collective-permute-start.25 = (bf16[256,2048]{1,0:T(8,128)(2,1)}, bf16[256,2048]{1,0:T(8,128)(2,1)}, u32[]{:S(2)}, u32[]{:S(2)}) collective-permute-start(bf16[256,2048]{1,0:T(8,128)(2,1)} %collective-permute-done.20.refs_0_.refs_2_), channel_id=1, source_target_pairs={{0,1},{1,2},{2,3},{3,0},{4,5},{5,6},{6,7},{7,4},{8,9},{9,10},{10,1... | collective-permute-start | bytes 3145736 | tf_op jit(solution)/shard_map/ppermute | solution.py:108
  338.8 45.9 %collective-permute-start.26 = (bf16[256,2048]{1,0:T(8,128)(2,1)}, bf16[256,2048]{1,0:T(8,128)(2,1)S(1)}, u32[]{:S(2)}, u32[]{:S(2)}) collective-permute-start(bf16[256,2048]{1,0:T(8,128)(2,1)} %collective-permute-done.9.refs_1_.refs_3_), channel_id=1, source_target_pairs={{0,1},{1,2},{2,3},{3,0},{4,5},{5,6},{6,7},{7,4},{8,9},{9,10},{10,1... | collective-permute-start | bytes 3145736 | tf_op jit(solution)/shard_map/ppermute | solution.py:108
  387.0 47.8 %collective-permute-start.28 = (bf16[256,2048]{1,0:T(8,128)(2,1)}, bf16[256,2048]{1,0:T(8,128)(2,1)S(1)}, u32[]{:S(2)}, u32[]{:S(2)}) collective-permute-start(bf16[256,2048]{1,0:T(8,128)(2,1)} %get-tuple-element.290), channel_id=1, source_target_pairs={{0,1},{1,2},{2,3},{3,0},{4,5},{5,6},{6,7},{7,4},{8,9},{9,10},{10,1... | collective-permute-start | bytes 3145736 | tf_op jit(solution)/shard_map/ppermute | solution.py:108
  613.9 64.2 %collective-permute-start.43 = (bf16[8,2,256,256]{3,2,0,1:T(8,128)(2,1)}, bf16[8,2,256,256]{3,2,0,1:T(8,128)(2,1)}, u32[]{:S(2)}, u32[]{:S(2)}) collective-permute-start(bf16[8,2,256,256]{3,2,0,1:T(8,128)(2,1)} %copy.168), channel_id=1, source_target_pairs={{0,8},{4,12},{8,0},{12,4},{16,24},{20,28},{24,16},{28,20},{1,9},{5... | collective-permute-start | bytes 6291464 | tf_op jit(solution)/shard_map/ppermute | solution.py:65
  615.1 63.2 %collective-permute-start.44 = (bf16[8,2,256,256]{3,2,1,0:T(8,128)(2,1)}, bf16[8,2,256,256]{3,2,1,0:T(8,128)(2,1)}, u32[]{:S(2)}, u32[]{:S(2)}) collective-permute-start(bf16[8,2,256,256]{3,2,1,0:T(8,128)(2,1)} %get-tuple-element.359), channel_id=1, source_target_pairs={{0,16},{4,20},{8,24},{12,28},{16,0},{20,4},{24,8},{28,12},{1,17},{... | collective-permute-start | bytes 6291464 | tf_op jit(solution)/shard_map/ppermute | solution.py:65
  662.9 43.0 %collective-permute-start.46 = (bf16[256,2048]{1,0:T(8,128)(2,1)}, bf16[256,2048]{1,0:T(8,128)(2,1)S(1)}, u32[]{:S(2)}, u32[]{:S(2)}) collective-permute-start(bf16[256,2048]{1,0:T(8,128)(2,1)} %add_convert_fusion.2), channel_id=1, source_target_pairs={{0,1},{1,2},{2,3},{3,0},{4,5},{5,6},{6,7},{7,4},{8,9},{9,10},{10,1... | collective-permute-start | bytes 3145736 | tf_op jit(solution)/shard_map/ppermute | solution.py:108
  664.5 80.9 %collective-permute-start.49 = (bf16[8,2,256,256]{3,2,0,1:T(8,128)(2,1)}, bf16[8,2,256,256]{3,2,0,1:T(8,128)(2,1)}, u32[]{:S(2)}, u32[]{:S(2)}) collective-permute-start(bf16[8,2,256,256]{3,2,0,1:T(8,128)(2,1)} %copy.171), channel_id=1, source_target_pairs={{0,8},{4,12},{8,0},{12,4},{16,24},{20,28},{24,16},{28,20},{1,9},{5... | collective-permute-start | bytes 6291464 | tf_op jit(solution)/shard_map/ppermute | solution.py:65
  664.8 80.6 %collective-permute-start.50 = (bf16[8,2,256,256]{3,2,1,0:T(8,128)(2,1)}, bf16[8,2,256,256]{3,2,1,0:T(8,128)(2,1)}, u32[]{:S(2)}, u32[]{:S(2)}) collective-permute-start(bf16[8,2,256,256]{3,2,1,0:T(8,128)(2,1)} %get-tuple-element.373), channel_id=1, source_target_pairs={{0,16},{4,20},{8,24},{12,28},{16,0},{20,4},{24,8},{28,12},{1,17},{... | collective-permute-start | bytes 6291464 | tf_op jit(solution)/shard_map/ppermute | solution.py:65
  682.2 63.1 %collective-permute-start.48 = (bf16[8,256,256]{2,1,0:T(8,128)(2,1)}, bf16[8,256,256]{2,1,0:T(8,128)(2,1)}, u32[]{:S(2)}, u32[]{:S(2)}) collective-permute-start(bf16[8,256,256]{2,1,0:T(8,128)(2,1)} %fusion.27), channel_id=1, source_target_pairs={{0,8},{4,12},{8,0},{12,4},{16,24},{20,28},{24,16},{28,20},{1,9},{5... | collective-permute-start | bytes 3145736 | tf_op jit(solution)/shard_map/ppermute | solution.py:65
  688.6 56.7 %collective-permute-start.47 = (bf16[8,256,256]{2,1,0:T(8,128)(2,1)}, bf16[8,256,256]{2,1,0:T(8,128)(2,1)}, u32[]{:S(2)}, u32[]{:S(2)}) collective-permute-start(bf16[8,256,256]{2,1,0:T(8,128)(2,1)} %fusion.24), channel_id=1, source_target_pairs={{0,16},{4,20},{8,24},{12,28},{16,0},{20,4},{24,8},{28,12},{1,17},{... | collective-permute-start | bytes 3145736 | tf_op jit(solution)/shard_map/ppermute | solution.py:65
  (142 other events, 2457.7 us)
Sparse Core Ops, SparseCore 0:
  10.5 90.9 all-gather.1
  549.3 100.8 reduce-scatter.1

commit v4 on v3

--- a/solution.py
+++ b/solution.py
@@ -882,12 +882,15 @@
     )
     normed1, unit1, scale1 = rows_norm(local_x, gain_attn)
     normed1_ring = [normed1.astype(bf16)]
-    exchange_far(0, early + late)
+    exchange_far(0, early)
     for _ in range(1, around):
         normed1_ring.append(hop(normed1_ring[-1]))
-    normed1_ring[-2], attn_all = together(normed1_ring[-2], attn_all)
+    normed1_ring[-2], attn_all, exchanged[2], exchanged[3] = together(
+        normed1_ring[-2], attn_all, exchanged[2], exchanged[3]
+    )
+    exchange_far(0, late)
     projected = projections(normed1_ring[:-1], attn_all, ring_chunks[:-1], around, None)
-    normed1_ring[-1], *projected = arrived(early + late, 0, normed1_ring[-1], *projected)
+    normed1_ring[-1], *projected = arrived(early, 0, normed1_ring[-1], *projected)
     far_rest(early)
     query_raw, key_raw, value_heads, squares = projections(
         normed1_ring[-1:], attn_all, ring_chunks[-1:], around, projected
@@ -901,9 +904,7 @@
     query_rot, key_rot, mixed_heads = attention_forward(
         query_raw, key_raw, value_heads, norm_scales, norm_gains, tables, marks
     )
-    mixed_heads, final_ring[-1] = together(mixed_heads, final_ring[-1])
-    for i in late:
-        exchanged[i] = held_until(exchanged[i], mixed_heads)
+    mixed_heads, final_ring[-1] = arrived(late, 0, mixed_heads, final_ring[-1])
     far_rest(late)
     attn_local = dot32(rows_of(mixed_heads, (here - 1) % around), output_w, NT)
     for step in range(1, around):
@@ -952,7 +953,7 @@
     for number, (call, sets) in enumerate(calls):
         if number + 1 < around:
             normed2_ring.append(hop(normed2_ring[number]))
-        if len(final_ring) < around and number >= 2:
+        if len(final_ring) < around and number != 1:
             final_ring.append(hop(final_ring[-1]))
         for s in call:
             if s < len(probs_ring):
@@ -1017,6 +1018,17 @@
         grad_logits, router_f.T, precision=PRECISE, preferred_element_type=f32
     )
     resid_norm_grad, grad_expert_part = norm_back(normed2_grad, gain_expert, unit2, scale2)
+    tn = (((0,), (0,)), ((), ()))
+    grad_router_part = lax.dot_general(
+        normed2_ring[0].astype(f32), grad_logits, tn, precision=PRECISE, preferred_element_type=f32
+    )
+    first_sums = jnp.concatenate([grad_router_part.T, grad_expert_part[None]]).reshape(-1)
+    sum_steps = [(axis, bit) for axis in ("dp", "tensor") for bit in bits_of(lax.axis_size(axis))]
+
+    def sum_hop():
+        axis, bit = sum_steps.pop(0)
+        return swap(first_sums, axis, bit)
+
     grad_resid = own_final + resid_norm_grad
 
     def reduce_rows(value):
@@ -1033,22 +1045,27 @@
     up_keep, up_send, gate_sum = moe_grad_split(
         normed2_ring, held_until(grad_upre, resid_ring[0]), "dp", 0, here_dp, (gate_keep, gate_moved)
     )
-    moved, up_keep, up_send, gate_sum = together(moved, up_keep, up_send, gate_sum)
+    moved, up_keep, up_send, gate_sum, hopped = together(
+        moved, up_keep, up_send, gate_sum, sum_hop()
+    )
+    first_sums = first_sums + hopped
     resid_ring.append(moved)
     reduced_gate = reduce_rows(gate_sum)
     up_moved = swap(up_send, "dp", 1)
     moved = hop(resid_ring[1])
     moe_part = moe_out(held_until(weighted_hidden, up_keep), down_all)
-    moved, moe_part, up_moved = together(moved, moe_part, up_moved)
+    moved, moe_part, up_moved, hopped = together(moved, moe_part, up_moved, sum_hop())
+    first_sums = first_sums + hopped
     resid_ring.append(moved)
     for step in range(3, around):
         resid_ring.append(hop(resid_ring[-1]))
     down_keep, down_send, *up_split = moe_grad_split(
         final_ring, held_until(weighted_hidden, moe_part), "dp", 0, 0, (up_keep, up_moved), True
     )
-    resid_ring[-1], down_keep, down_send, *up_split = together(
-        resid_ring[-1], down_keep, down_send, *up_split
-    )
+    resid_ring[-1], down_keep, down_send, hopped, *up_split = together(
+        resid_ring[-1], down_keep, down_send, sum_hop(), *up_split
+    )
+    first_sums = first_sums + hopped
 
     def cube_begin(split):
         flying = [swap(sent, "dp", order[0]) for sent, order in zip(split[2:], cube_orders("dp"))]
@@ -1060,7 +1077,6 @@
     grad_mixed = dot32(resid_full, output_w).astype(bf16)
     moe_local = moe_part[rows_here : 2 * rows_here].astype(f32)
     moe_moved = hop(held_until(moe_local.astype(bf16), resid_full))
-    tn = (((0,), (0,)), ((), ()))
     query_gained, key_gained, value_low, inner_part, gain_grads, *down_split = attention_backward(
         query_rot,
         key_rot,
@@ -1075,16 +1091,18 @@
         (down_keep, down_moved),
         "dp",
     )
-    query_gained, key_gained, inner_part, reduced_gate, moe_moved, *down_split = together(
-        query_gained, key_gained, inner_part, reduced_gate, moe_moved, *down_split
-    )
+    query_gained, key_gained, inner_part, reduced_gate, moe_moved, hopped, *down_split = together(
+        query_gained, key_gained, inner_part, reduced_gate, moe_moved, sum_hop(), *down_split
+    )
+    first_sums = first_sums + hopped
     down_cube, down_flying = cube_begin(down_split)
     moe_local = moe_moved.astype(f32) + moe_part[2 * rows_here : 3 * rows_here].astype(f32)
-    moe_moved = hop(moe_local.astype(bf16))
-    inner_sums = all_sum(inner_part[:, 0], ("tensor",)).T / model_width
-    inner_sums, *up_flying = together(inner_sums, *up_flying)
+    inner_sums = all_sum(inner_part[:, 0], ("tensor",))
+    inner_sums, moe_low = together(inner_sums, moe_local.astype(bf16))
+    moe_moved = hop(moe_low)
+    inner_sums = inner_sums.T / model_width
+    inner_sums, moe_moved, *up_flying = together(inner_sums, moe_moved, *up_flying)
     up_cube.finish(up_flying)
-    up_flying = up_cube.start()
     back_order = [(here - 1 - step) % around for step in range(around)]
     query_raw_low, key_raw_low, normed1_parts = projection_back(
         (query_raw, key_raw),
@@ -1104,49 +1122,54 @@
         [query_raw_low, key_raw_low, value_low, held_until(mixed_heads, first)],
         "dp",
     )
-    moved, attn_keep, attn_send, moe_moved, up_flying, down_flying = jax.tree.unflatten(
-        jax.tree.structure((0, 0, 0, 0, [0, 0], [0, 0])),
-        together(moved, attn_keep, attn_send, moe_moved, *up_flying, *down_flying),
-    )
-    up_cube.finish(up_flying)
-    while up_cube.orders[0]:
-        up_cube.finish(up_cube.start())
+    moved, attn_keep, attn_send, *down_flying = together(moved, attn_keep, attn_send, *down_flying)
     attn_moved = swap(attn_send, "dp", 1)
     down_cube.finish(down_flying)
-    while down_cube.orders[0]:
-        down_cube.finish(down_cube.start())
+    up_cube.pieces = [
+        jnp.concatenate(pair) for pair in zip(up_cube.pieces, down_cube.pieces)
+    ]
+    while len(up_cube.orders[0]) > 1:
+        up_cube.finish(up_cube.start())
+    up_flying = up_cube.start()
     for step in range(1, around):
         normed1_grad = moved.astype(f32) + normed1_parts[step].astype(f32)
         if step + 1 < around:
             moved = hop(normed1_grad.astype(bf16))
         if step == 1:
             attn_split = pair_split(attn_keep, attn_moved, "dp")
+            moved, *attn_split = together(moved, *attn_split)
             attn_cube, attn_flying = cube_begin(attn_split)
-    normed1_grad, moe_moved, *attn_flying = together(normed1_grad, moe_moved, *attn_flying)
-    attn_cube.finish(attn_flying)
-    while attn_cube.orders[0]:
-        attn_cube.finish(attn_cube.start())
-    reduced_up = up_cube.result()
-    reduced_attn = attn_cube.result()
+    normed1_grad, *up_flying = together(normed1_grad, *up_flying)
+    up_cube.finish(up_flying)
+    reduced_up = jnp.concatenate([piece[:half] for piece in up_cube.pieces])
+    reduced_down = jnp.concatenate([piece[half:] for piece in up_cube.pieces])
     moe_local = moe_moved.astype(f32) + moe_part[3 * rows_here :].astype(f32)
     moe_moved = hop(moe_local.astype(bf16))
-    layer_local = resid + xor_blocks(moe_moved.astype(f32) + moe_part[:rows_here].astype(f32), "dp")
-    layer_local = layer_local.astype(bf16)
-    reduced_down = down_cube.result()
-    grad_router_part = lax.dot_general(
-        normed2_ring[0].astype(f32), grad_logits, tn, precision=PRECISE, preferred_element_type=f32
-    )
     input_norm_grad, grad_attn_part = norm_back(normed1_grad, gain_attn, unit1, scale1)
     grad_input = grad_resid + input_norm_grad
     gains_full = lax.dynamic_update_slice(
         jnp.zeros((2, model_width), f32), gain_grads, (0, head_offset)
     )
-    sums = all_sum(
-        jnp.concatenate(
-            [grad_router_part.T, grad_expert_part[None], gains_full, grad_attn_part[None]]
-        ),
-        ("dp", "tensor"),
-    )
+    while len(sum_steps) > 1:
+        first_sums = first_sums + sum_hop()
+    last_sums = jnp.concatenate([gains_full.reshape(-1), grad_attn_part])
+    last_sums = last_sums + swap(last_sums, "dp", 1)
+    last_sums, *attn_flying = together(last_sums, *attn_flying)
+    attn_cube.finish(attn_flying)
+    while attn_cube.orders[0]:
+        attn_cube.finish(attn_cube.start())
+    reduced_attn = attn_cube.result()
+    for bit in bits_of(lax.axis_size("dp"))[1:]:
+        last_sums = last_sums + swap(last_sums, "dp", bit)
+    last_sums, moe_moved = together(last_sums, moe_moved)
+    layer_local = resid + xor_blocks(moe_moved.astype(f32) + moe_part[:rows_here].astype(f32), "dp")
+    layer_local = layer_local.astype(bf16)
+    axis, bit = sum_steps.pop()
+    for early_bit in bits_of(lax.axis_size(axis)):
+        if early_bit != bit:
+            last_sums = last_sums + swap(last_sums, axis, early_bit)
+    sums = jnp.concatenate([first_sums, last_sums])
+    sums = (sums + swap(sums, axis, bit)).reshape(EXPERTS + 4, model_width)
     return (
         layer_local[None],
         grad_input[None],

time: 886 us -> 846 us (0.955)
  waiting for transfers between devices: 268 us -> 214 us
  local copies, waits for them, and re-layouts: 50.8 us -> 63.5 us
    ppermute x39 -> x41, waiting for transfers between devices: 110 us -> 50.5 us  [swap(): return lax.ppermute(value, axis, [(i, i ^ bit) for i in range(n)])]
    ppermute x27, waiting for transfers between devices: 127 us -> 141 us  [ring_hop(): return lax.ppermute(total, axis, [(i, (i + 1) % n) for i in range(n)])]
    unnamed x205 -> x194, local copies, waits for them, and re-layouts: 16.8 us -> 23.3 us
    add x12 -> x10, other arithmetic: 17.3 us -> 19.4 us  [finish(): stay.astype(jnp.float32) + came.reshape(stay.shape).astype(jnp.float32)]
    ppermute x39 -> x41, starting transfers between devices: 37 us -> 37.8 us  [swap(): return lax.ppermute(value, axis, [(i, i ^ bit) for i in range(n)])]
  transfers between devices with their start and end apart: 68 -> 70, of which waited for: 30 -> 26; matrix products, arithmetic and copies ran while one was open for 17% -> 19% of each run, Pallas kernels for 40% -> 43%
where the time goes in v4:
time: 846 us; the launch traced here: 838 us
  Pallas kernels  357 us (42%)
  waiting for transfers between devices  214 us (25%)
  other arithmetic  98.6 us (12%)
  local copies, waits for them, and re-layouts  63.5 us (8%)
  starting transfers between devices  59.1 us (7%)
  matrix products  29.1 us (3%)
  between operations  16.2 us (2%)
    pallas_call x5, Pallas kernels, moe_first(): pl.pallas_call(kernel, grid_spec=pltpu.PrefetchScalarGridSpec(num_scalar_...  144 us
    ppermute x27, waiting for transfers between devices, ring_hop(): return lax.ppermute(total, axis, [(i, (i + 1) % n) for i in range(n)])  141 us
    pallas_call x3, Pallas kernels, moe_grad_split(): pl.pallas_call(kernel, grid_spec=pltpu.PrefetchScalarGridSpec(num_scalar_...  87.5 us
    ppermute x41, waiting for transfers between devices, swap(): return lax.ppermute(value, axis, [(i, i ^ bit) for i in range(n)])  50.5 us
    ppermute x41, starting transfers between devices, swap(): return lax.ppermute(value, axis, [(i, i ^ bit) for i in range(n)])  37.8 us
    pallas_call x1, Pallas kernels, attention_backward(): pl.pallas_call(kernel, grid=(heads,), in_specs=[head, head, head, head, h...  29.6 us
    pallas_call x1, Pallas kernels, moe_out(): pl.pallas_call(kernel, grid=(experts,), in_specs=[pl.BlockSpec((1, tokens...  26 us
    dot_general x9, matrix products, dot32(): lax.dot_general(left, right, dims, preferred_element_type=jnp.float32)  23.9 us
  transfers between devices with their start and end apart: 70, of which 26 were waited for; matrix products, arithmetic and copies ran while one was open for 19% of the time, Pallas kernels for 43%

profile of v4, /device:TPU:0, one launch (start us, length us, event | category | flops | bytes accessed | tf_op | source)
XLA Modules:
  0.0 837.7 jit_solution(1805022807791081406)
XLA Ops:
  30.9 9.0 %collective-permute-done.refs_1_ = bf16[256,2048]{1,0:T(8,128)(2,1)} collective-permute-done((bf16[256,2048]{1,0:T(8,128)(2,1)}, bf16[256,2048]{1,0:T(8,128)(2,1)}, u32[]{:S(2)}, u32[]{:S(2)}) %collective-permute-start) | collective-permute-done | bytes 1048608 | tf_op jit(solution)/shard_map/ppermute | solution.py:108
  48.6 17.8 %collective-permute-done.1.refs_2_ = bf16[256,2048]{1,0:T(8,128)(2,1)} collective-permute-done((bf16[256,2048]{1,0:T(8,128)(2,1)}, bf16[256,2048]{1,0:T(8,128)(2,1)}, u32[]{:S(2)}, u32[]{:S(2)}) %collective-permute-start.1) | collective-permute-done | bytes 1048608 | tf_op jit(solution)/shard_map/ppermute | solution.py:108
  70.5 23.0 %all-gather.2.cloned.1.call-done.refs_3_.refs_1_.w_ref = bf16[4,2048,512]{2,1,0:T(8,128)(2,1)} async-done(((bf16[4,256,512]{2,1,0:T(8,128)(2,1)}), bf16[4,2048,512]{2,1,0:T(8,128)(2,1)}) %all-gather.2.cloned.1.call-update) | async-done | bytes 8388624 | tf_op jit(solution)/shard_map/all_gather | solution.py:830
  95.7 11.1 %projections.2 = (f32[1024,512]{1,0:T(8,128)}, f32[1024,512]{1,0:T(8,128)}, bf16[1024,512]{1,0:T(8,128)(2,1)}, f32[2,8,1024]{2,1,0:T(8,128)}) custom-call(s32[3]{0:T(128)} %pad_add_fusion.1.place_ref, bf16[256,2048]{1,0:T(8,128)(2,1)} %fusion.11.refs_0_, bf16[256,2048]{1,0:T(8,128)(2,1)} %collective-permute-done.refs_1_, ...), custom_call_target="tpu_custom_call" | custom-call | flops 4831838208 | bytes 13369344 | tf_op jit(solution)/shard_map/projections/pallas_call | solution.py:184
  134.4 14.9 %attention_forward.1 = (bf16[1024,512]{1,0:T(8,128)(2,1)}, bf16[1024,512]{1,0:T(8,128)(2,1)}, bf16[1024,512]{1,0:T(8,128)(2,1)}) custom-call(f32[1024,512]{1,0:T(8,128)} %get-tuple-element.228.q_ref.qr_ref.qr, f32[1024,512]{1,0:T(8,128)} %get-tuple-element.229.k_ref.kr_ref.kr, bf16[1024,512]{1,0:T(8,128)(2,1)} %get-tuple-element.230.v_ref, ...), custom_call_target="tpu_custom_call" | custom-call | flops 1610612736 | bytes 8388608 | tf_op jit(solution)/shard_map/attention_forward/pallas_call | solution.py:378
  154.4 22.6 %collective-permute-done.10 = bf16[256,2048]{1,0:T(8,128)(2,1)} collective-permute-done((bf16[256,2048]{1,0:T(8,128)(2,1)}, bf16[256,2048]{1,0:T(8,128)(2,1)}, u32[]{:S(2)}, u32[]{:S(2)}) %collective-permute-start.10) | collective-permute-done | bytes 1048608 | tf_op jit(solution)/shard_map/ppermute | solution.py:108
  181.0 16.9 %collective-permute-done.13 = bf16[24,256,256]{2,1,0:T(8,128)(2,1)} collective-permute-done((bf16[24,256,256]{2,1,0:T(8,128)(2,1)}, bf16[24,256,256]{2,1,0:T(8,128)(2,1)}, u32[]{:S(2)}, u32[]{:S(2)}) %collective-permute-start.13) | collective-permute-done | bytes 3145760 | tf_op jit(solution)/shard_map/ppermute | solution.py:65
  225.0 18.5 %collective-permute-done.14 = bf16[256,2048]{1,0:T(8,128)(2,1)} collective-permute-done((bf16[256,2048]{1,0:T(8,128)(2,1)}, bf16[256,2048]{1,0:T(8,128)(2,1)}, u32[]{:S(2)}, u32[]{:S(2)}) %collective-permute-start.14) | collective-permute-done | bytes 1048608 | tf_op jit(solution)/shard_map/ppermute | solution.py:108
  251.3 27.0 %moe_first.5 = (bf16[256,2048]{1,0:T(8,128)(2,1)}, f32[256,16]{1,0:T(8,128)}, bf16[16,1024,256]{2,1,0:T(8,128)(2,1)}, bf16[16,1024,256]{2,1,0:T(8,128)(2,1)}, bf...) custom-call(s32[3]{0:T(128)} %pad_add_fusion.2.side_ref, ...), custom_call_target="tpu_custom_call" | custom-call | flops 10737418240 | bytes 34603008 | tf_op jit(solution)/shard_map/moe_first/pallas_call | solution.py:631
  278.8 13.5 %collective-permute-done.17.refs_0_.refs_1_ = bf16[256,2048]{1,0:T(8,128)(2,1)S(1)} collective-permute-done((bf16[256,2048]{1,0:T(8,128)(2,1)}, bf16[256,2048]{1,0:T(8,128)(2,1)S(1)}, u32[]{:S(2)}, u32[]{:S(2)}) %collective-permute-start.17) | collective-permute-done | bytes 1048608 | tf_op jit(solution)/shard_map/ppermute | solution.py:108
  301.0 18.5 %moe_first.6 = (bf16[256,2048]{1,0:T(8,128)(2,1)}, f32[256,16]{1,0:T(8,128)}, bf16[16,1024,256]{2,1,0:T(8,128)(2,1)}, bf16[16,1024,256]{2,1,0:T(8,128)(2,1)}, bf16[16,1024,256]{2,1,0:T(8,128)(2,1)}) custom-call(s32[3]{0:T(128)} %pad_add_fusion.2.side_ref, bf16[256,2048]{1,0:T(8,128)(2,1)} %copy-done.15, ...), custom_call_target="tpu_custom_call", output_to_operand_aliasing={{2}: (7, {}), {3}: (8, {}), {4}: (9, {})} | custom-call | flops 10737418240 | bytes 34603008 | tf_op jit(solution)/shard_map/moe_first/pallas_call | solution.py:631
  326.3 37.5 %moe_first.7 = (bf16[256,2048]{1,0:T(8,128)(2,1)}, bf16[256,2048]{1,0:T(8,128)(2,1)}, f32[256,16]{1,0:T(8,128)}, f32[256,16]{1,0:T(8,128)}, bf16[16,1024,256]{2,...) custom-call(s32[3]{0:T(128)} %pad_add_fusion.2.side_ref, ...), custom_call_target="tpu_custom_call", output_to_operand_aliasing={{4}: (58, {}), {5}: (59, {}), {6}: (60, {}), {7}: (61, {}),... | custom-call | flops 21474836480 | bytes 44040192 | tf_op jit(solution)/shard_map/moe_first/pallas_call | solution.py:631
  363.8 7.5 collective-permute-done.27.refs_1_.refs_3_
  373.4 30.5 %moe_first.8 = (bf16[256,2048]{1,0:T(8,128)(2,1)}, f32[256,16]{1,0:T(8,128)}, bf16[16,1024,256]{2,1,0:T(8,128)(2,1)}, bf16[16,1024,256]{2,1,0:T(8,128)(2,1)}, bf16[16,1024,256]{2,1,0:T(8,128)(2,1)}) custom-call(s32[3]{0:T(128)} %pad_add_fusion.2.side_ref, ...), custom_call_target="tpu_custom_call", output_to_operand_aliasing={{2}: (7, {}), {3}: (8, {}), {4}: (9, {})} | custom-call | flops 21474836480 | bytes 62914560 | tf_op jit(solution)/shard_map/moe_first/pallas_call | solution.py:631
  414.5 30.5 %moe_first.9 = (bf16[256,2048]{1,0:T(8,128)(2,1)}, f32[256,16]{1,0:T(8,128)}, bf16[16,1024,256]{2,1,0:T(8,128)(2,1)}, bf16[16,1024,256]{2,1,0:T(8,128)(2,1)}, bf16[16,1024,256]{2,1,0:T(8,128)(2,1)}) custom-call(s32[3]{0:T(128)} %pad_add_fusion.2.side_ref, ...), custom_call_target="tpu_custom_call", output_to_operand_aliasing={{2}: (7, {}), {3}: (8, {}), {4}: (9, {})} | custom-call | flops 21474836480 | bytes 62914560 | tf_op jit(solution)/shard_map/moe_first/pallas_call | solution.py:631
  448.0 25.7 %moe_grad_split.3 = (bf16[16,4,256,256]{3,2,1,0:T(8,128)(2,1)}, bf16[16,4,256,256]{3,2,1,0:T(8,128)(2,1)}) custom-call(s32[2]{0:T(128)} %pad_add_fusion.3.side_ref, bf16[256,2048]{1,0:T(8,128)(2,1)} %copy-done.11, bf16[256,2048]{1,0:T(8,128)(2,1)} %copy-done.15, bf16[256,2048]{1,0:T(8,128)(2,1)} %collective-permute-done.21.refs_0_.refs_2_, ...), custom_call_target="tpu_custom_call" | custom-call | flops 17179869184 | bytes 29360128 | tf_op jit(solution)/shard_map/moe_grad_split/pallas_call | solution.py:730
  489.4 30.8 %moe_grad_split.4 = (bf16[16,4,256,256]{3,2,1,0:T(8,128)(2,1)}, bf16[16,4,256,256]{3,2,1,0:T(8,128)(2,1)}, bf16[16,4,256,256]{3,2,1,0:T(8,128)(2,1)}) custom-call(s32[2]{0:T(128)} %pad_add_fusion.4.side_ref, bf16[256,2048]{1,0:T(8,128)(2,1)} %copy-done.11, bf16[256,2048]{1,0:T(8,128)(2,1)} %copy-done.15, ...), custom_call_target="tpu_custom_call" | custom-call | flops 17179869184 | bytes 29360128 | tf_op jit(solution)/shard_map/moe_grad_split/pallas_call | solution.py:730
  526.1 26.0 %moe_out.1 = bf16[1024,2048]{1,0:T(8,128)(2,1)} custom-call(bf16[16,1024,256]{2,1,0:T(8,128)(2,1)} %get-tuple-element.348.h_ref.refs_4_, bf16[16,2048,256]{2,1,0:T(8,128)(2,1)} %get-tuple-element.292.refs_5_.d_ref), custom_call_target="tpu_custom_call" | custom-call | flops 17179869184 | bytes 29360128 | tf_op jit(solution)/shard_map/moe_out/pallas_call | solution.py:772
  554.2 31.1 %moe_grad_split.5 = (bf16[16,4,256,256]{3,2,1,0:T(8,128)(2,1)}, bf16[16,4,256,256]{3,2,1,0:T(8,128)(2,1)}, bf16[8,2,256,256]{3,2,1,0:T(8,128)(2,1)}, bf16[8,2,25...) custom-call(s32[2]{0:T(128)} %broadcast_4_side_ref.2.side_ref, ...), custom_call_target="tpu_custom_call" | custom-call | flops 17179869184 | bytes 29360128 | tf_op jit(solution)/shard_map/moe_grad_split/pallas_call | solution.py:730
  600.5 29.6 %attention_backward.1 = (f32[1024,512]{1,0:T(8,128)}, f32[1024,512]{1,0:T(8,128)}, bf16[1024,512]{1,0:T(8,128)(2,1)}, f32[2,8,1024]{2,1,0:T(8,128)}, f32[2,512]{...) custom-call(bf16[1024,512]{1,0:T(8,128)(2,1)} %get-tuple-element.240, ...), custom_call_target="tpu_custom_call" | custom-call | flops 4026531840 | bytes 13631488 | tf_op jit(solution)/shard_map/attention_backward/pallas_call | solution.py:473
  654.8 11.5 %collective-permute-done.47 = bf16[256,2048]{1,0:T(8,128)(2,1)S(1)} collective-permute-done((bf16[256,2048]{1,0:T(8,128)(2,1)}, bf16[256,2048]{1,0:T(8,128)(2,1)S(1)}, u32[]{:S(2)}, u32[]{:S(2)}) %collective-permute-start.47) | collective-permute-done | bytes 1048608 | tf_op jit(solution)/shard_map/ppermute | solution.py:108
  666.2 13.6 %projection_back.1 = (bf16[1024,512]{1,0:T(8,128)(2,1)}, bf16[1024,512]{1,0:T(8,128)(2,1)}, bf16[4,256,2048]{2,1,0:T(8,128)(2,1)}) custom-call(s32[4]{0:T(128)} %pad_add_fusion.5.place_ref, f32[1024,512]{1,0:T(8,128)} %get-tuple-element.228.q_ref.qr_ref.qr, f32[1024,512]{1,0:T(8,128)} %get-tuple-element.229.k_ref.kr_ref.kr, ...), custom_call_target="tpu_custom_call" | custom-call | flops 6442450944 | bytes 22020096 | tf_op jit(solution)/shard_map/projection_back/pallas_call | solution.py:237
  682.9 18.7 %projection_grads.1 = (bf16[4,4,256,512]{3,2,1,0:T(8,128)(2,1)}, bf16[4,4,256,512]{3,2,1,0:T(8,128)(2,1)}) custom-call(s32[5]{0:T(128)} %stack.97.place_ref, bf16[256,2048]{1,0:T(8,128)(2,1)} %fusion.11.refs_0_, bf16[256,2048]{1,0:T(8,128)(2,1)} %collective-permute-done.refs_1_, bf16[256,2048]{1,0:T(8,128)(2,1)} %collective-permute-done.1.refs_2_, ...), custom_call_target="tpu_custom_call" | custom-call | flops 8589934592 | bytes 20971520 | tf_op jit(solution)/shard_map/projection_grads/pallas_call | solution.py:318
  752.0 22.2 %collective-permute-done.55 = bf16[256,2048]{1,0:T(8,128)(2,1)S(1)} collective-permute-done((bf16[256,2048]{1,0:T(8,128)(2,1)S(1)}, bf16[256,2048]{1,0:T(8,128)(2,1)S(1)}, u32[]{:S(2)}, u32[]{:S(2)}) %collective-permute-start.55) | collective-permute-done | bytes 1048608 | tf_op jit(solution)/shard_map/ppermute | solution.py:108
  (497 shorter events, 313.9 us)
Async XLA Ops:
  7.2 86.3 %all-gather.2.cloned.1.call-start = ((), (), s32[]{:S(2)}) async-start(), calls=%async_computation.1 | async-start | bytes 9437184 | tf_op jit(solution)/shard_map/all_gather | solution.py:830
  9.7 620.5 %reduce-scatter.2.cloned.1.call-start = ((), (), s32[]{:S(2)}) async-start(), calls=%async_computation.2 | async-start | bytes 10485760 | tf_op jit(solution)/shard_map/reduce_scatter | solution.py:1035
  21.8 85.1 %collective-permute-start.4 = (bf16[12,256,256]{2,1,0:T(8,128)(2,1)}, bf16[12,256,256]{2,1,0:T(8,128)(2,1)S(1)}, u32[]{:S(2)}, u32[]{:S(2)}) collective-permute-start(bf16[12,256,256]{2,1,0:T(8,128)(2,1)} %pad_maximum_fusion.9), channel_id=1, source_target_pairs={{0,16},{4,20},{8,24},{12,28},{16,0},{20,4},{24,8},{28,12},{1,17},{... | collective-permute-start | bytes 4718600 | tf_op jit(solution)/shard_map/ppermute | solution.py:65
  24.6 82.3 %collective-permute-start.3 = (bf16[12,256,256]{2,1,0:T(8,128)(2,1)}, bf16[12,256,256]{2,1,0:T(8,128)(2,1)S(1)}, u32[]{:S(2)}, u32[]{:S(2)}) collective-permute-start(bf16[12,256,256]{2,1,0:T(8,128)(2,1)} %pad_maximum_fusion.8), channel_id=1, source_target_pairs={{0,8},{4,12},{8,0},{12,4},{16,24},{20,28},{24,16},{28,20},{1,9},{5... | collective-permute-start | bytes 4718600 | tf_op jit(solution)/shard_map/ppermute | solution.py:65
  93.5 55.8 %collective-permute-start.8 = (bf16[12,256,256]{2,1,0:T(8,128)(2,1)}, bf16[12,256,256]{2,1,0:T(8,128)(2,1)}, u32[]{:S(2)}, u32[]{:S(2)}) collective-permute-start(bf16[12,256,256]{2,1,0:T(8,128)(2,1)} %get-tuple-element.234), channel_id=1, source_target_pairs={{0,8},{4,12},{8,0},{12,4},{16,24},{20,28},{24,16},{28,20},{1,9},{5... | collective-permute-start | bytes 4718600 | tf_op jit(solution)/shard_map/ppermute | solution.py:65
  95.0 54.3 %collective-permute-start.9 = (bf16[12,256,256]{2,1,0:T(8,128)(2,1)}, bf16[12,256,256]{2,1,0:T(8,128)(2,1)}, u32[]{:S(2)}, u32[]{:S(2)}) collective-permute-start(bf16[12,256,256]{2,1,0:T(8,128)(2,1)} %get-tuple-element.235), channel_id=1, source_target_pairs={{0,16},{4,20},{8,24},{12,28},{16,0},{20,4},{24,8},{28,12},{1,17},{... | collective-permute-start | bytes 4718600 | tf_op jit(solution)/shard_map/ppermute | solution.py:65
  126.1 71.8 %collective-permute-start.13 = (bf16[24,256,256]{2,1,0:T(8,128)(2,1)}, bf16[24,256,256]{2,1,0:T(8,128)(2,1)}, u32[]{:S(2)}, u32[]{:S(2)}) collective-permute-start(bf16[24,256,256]{2,1,0:T(8,128)(2,1)} %pad_maximum_fusion.5), channel_id=1, source_target_pairs={{0,8},{4,12},{8,0},{12,4},{16,24},{20,28},{24,16},{28,20},{1,9},{5... | collective-permute-start | bytes 9437192 | tf_op jit(solution)/shard_map/ppermute | solution.py:65
  128.5 70.5 %collective-permute-start.12 = (bf16[24,256,256]{2,1,0:T(8,128)(2,1)}, bf16[24,256,256]{2,1,0:T(8,128)(2,1)}, u32[]{:S(2)}, u32[]{:S(2)}) collective-permute-start(bf16[24,256,256]{2,1,0:T(8,128)(2,1)} %pad_maximum_fusion.4), channel_id=1, source_target_pairs={{0,16},{4,20},{8,24},{12,28},{16,0},{20,4},{24,8},{28,12},{1,17},{... | collective-permute-start | bytes 9437192 | tf_op jit(solution)/shard_map/ppermute | solution.py:65
  206.5 43.4 %collective-permute-start.16 = (bf16[48,256,256]{2,1,0:T(8,128)(2,1)}, bf16[48,256,256]{2,1,0:T(8,128)(2,1)}, u32[]{:S(2)}, u32[]{:S(2)}) collective-permute-start(bf16[48,256,256]{2,1,0:T(8,128)(2,1)} %constant_dynamic-update-slice_fusion.5.refs_11_.refs_13_.refs_15_.refs_17_.refs_27_.refs_29_.refs_31_.refs_, ...), channel_id=1, source_target_pairs={{0,4},{4,0},{8,12},{12,8},{16,20},{20,16},{24,28},{28,24},{1,5},{5... | collective-permute-start | bytes 18874376 | tf_op jit(solution)/shard_map/ppermute | solution.py:65
  220.4 71.8 %collective-permute-start.19 = (bf16[24,256,256]{2,1,0:T(8,128)(2,1)}, bf16[24,256,256]{2,1,0:T(8,128)(2,1)}, u32[]{:S(2)}, u32[]{:S(2)}) collective-permute-start(bf16[24,256,256]{2,1,0:T(8,128)(2,1)} %constant_dynamic-update-slice_fusion.10.refs_5_.refs_7_.refs_21_.refs_23_.refs_37_.refs_39_), channel_id=1, source_target_pairs={{0,16},{4,20},{8,24},{12,28},{16,0},{20,4},{24,8},{28,12},{1,17},{... | collective-permute-start | bytes 9437192 | tf_op jit(solution)/shard_map/ppermute | solution.py:65
  222.6 69.9 %collective-permute-start.20 = (bf16[24,256,256]{2,1,0:T(8,128)(2,1)S(1)}, bf16[24,256,256]{2,1,0:T(8,128)(2,1)}, u32[]{:S(2)}, u32[]{:S(2)}) collective-permute-start(bf16[24,256,256]{2,1,0:T(8,128)(2,1)S(1)} %constant_dynamic-update-slice_fusion.12.refs_13_.refs_17_.refs_29_.refs_33_.refs_45_.refs_49_), channel_id=1, source_target_pairs={{0,8},{4,12},{8,0},{12,4},{16,24},{20,28},{24,16},{28,20},{1,9},{5... | collective-permute-start | bytes 9437192 | tf_op jit(solution)/shard_map/ppermute | solution.py:65
  249.9 42.3 %collective-permute-start.17 = (bf16[256,2048]{1,0:T(8,128)(2,1)}, bf16[256,2048]{1,0:T(8,128)(2,1)S(1)}, u32[]{:S(2)}, u32[]{:S(2)}) collective-permute-start(bf16[256,2048]{1,0:T(8,128)(2,1)} %copy-done.11), channel_id=1, source_target_pairs={{0,1},{1,2},{2,3},{3,0},{4,5},{5,6},{6,7},{7,4},{8,9},{9,10},{10,1... | collective-permute-start | bytes 3145736 | tf_op jit(solution)/shard_map/ppermute | solution.py:108
  251.3 74.1 %collective-permute-start.22 = (bf16[24,256,256]{2,1,0:T(8,128)(2,1)}, bf16[24,256,256]{2,1,0:T(8,128)(2,1)}, u32[]{:S(2)}, u32[]{:S(2)}) collective-permute-start(bf16[24,256,256]{2,1,0:T(8,128)(2,1)} %constant_dynamic-update-slice_fusion.10.refs_5_.refs_7_.refs_21_.refs_23_.refs_37_.refs_39_), channel_id=1, source_target_pairs={{0,4},{4,0},{8,12},{12,8},{16,20},{20,16},{24,28},{28,24},{1,5},{5... | collective-permute-start | bytes 9437192 | tf_op jit(solution)/shard_map/ppermute | solution.py:65
  278.3 48.1 %collective-permute-start.24 = (bf16[24,256,256]{2,1,0:T(8,128)(2,1)S(1)}, bf16[24,256,256]{2,1,0:T(8,128)(2,1)}, u32[]{:S(2)}, u32[]{:S(2)}) collective-permute-start(bf16[24,256,256]{2,1,0:T(8,128)(2,1)S(1)} %constant_dynamic-update-slice_fusion.12.refs_13_.refs_17_.refs_29_.refs_33_.refs_45_.refs_49_), channel_id=1, source_target_pairs={{0,4},{4,0},{8,12},{12,8},{16,20},{20,16},{24,28},{28,24},{1,5},{5... | collective-permute-start | bytes 9437192 | tf_op jit(solution)/shard_map/ppermute | solution.py:65
  322.6 41.2 %collective-permute-start.26 = (bf16[256,2048]{1,0:T(8,128)(2,1)}, bf16[256,2048]{1,0:T(8,128)(2,1)}, u32[]{:S(2)}, u32[]{:S(2)}) collective-permute-start(bf16[256,2048]{1,0:T(8,128)(2,1)} %collective-permute-done.21.refs_0_.refs_2_), channel_id=1, source_target_pairs={{0,1},{1,2},{2,3},{3,0},{4,5},{5,6},{6,7},{7,4},{8,9},{9,10},{10,1... | collective-permute-start | bytes 3145736 | tf_op jit(solution)/shard_map/ppermute | solution.py:108
  325.3 45.9 %collective-permute-start.27 = (bf16[256,2048]{1,0:T(8,128)(2,1)}, bf16[256,2048]{1,0:T(8,128)(2,1)S(1)}, u32[]{:S(2)}, u32[]{:S(2)}) collective-permute-start(bf16[256,2048]{1,0:T(8,128)(2,1)} %collective-permute-done.18.refs_1_.refs_2_), channel_id=1, source_target_pairs={{0,1},{1,2},{2,3},{3,0},{4,5},{5,6},{6,7},{7,4},{8,9},{9,10},{10,1... | collective-permute-start | bytes 3145736 | tf_op jit(solution)/shard_map/ppermute | solution.py:108
  593.4 61.3 %collective-permute-start.48 = (bf16[8,2,256,256]{3,2,0,1:T(8,128)(2,1)}, bf16[8,2,256,256]{3,2,0,1:T(8,128)(2,1)}, u32[]{:S(2)}, u32[]{:S(2)}) collective-permute-start(bf16[8,2,256,256]{3,2,0,1:T(8,128)(2,1)} %copy.167), channel_id=1, source_target_pairs={{0,8},{4,12},{8,0},{12,4},{16,24},{20,28},{24,16},{28,20},{1,9},{5... | collective-permute-start | bytes 6291464 | tf_op jit(solution)/shard_map/ppermute | solution.py:65
  593.7 61.0 %collective-permute-start.49 = (bf16[8,2,256,256]{3,2,1,0:T(8,128)(2,1)}, bf16[8,2,256,256]{3,2,1,0:T(8,128)(2,1)}, u32[]{:S(2)}, u32[]{:S(2)}) collective-permute-start(bf16[8,2,256,256]{3,2,1,0:T(8,128)(2,1)} %get-tuple-element.379), channel_id=1, source_target_pairs={{0,16},{4,20},{8,24},{12,28},{16,0},{20,4},{24,8},{28,12},{1,17},{... | collective-permute-start | bytes 6291464 | tf_op jit(solution)/shard_map/ppermute | solution.py:65
  644.8 56.9 %collective-permute-start.51 = (bf16[8,2,256,256]{3,2,0,1:T(8,128)(2,1)S(1)}, bf16[8,2,256,256]{3,2,0,1:T(8,128)(2,1)}, u32[]{:S(2)}, u32[]{:S(2)}) collective-permute-start(bf16[8,2,256,256]{3,2,0,1:T(8,128)(2,1)S(1)} %copy.168), channel_id=1, source_target_pairs={{0,8},{4,12},{8,0},{12,4},{16,24},{20,28},{24,16},{28,20},{1,9},{5... | collective-permute-start | bytes 6291464 | tf_op jit(solution)/shard_map/ppermute | solution.py:65
  645.6 56.1 %collective-permute-start.52 = (bf16[8,2,256,256]{3,2,1,0:T(8,128)(2,1)}, bf16[8,2,256,256]{3,2,1,0:T(8,128)(2,1)}, u32[]{:S(2)}, u32[]{:S(2)}) collective-permute-start(bf16[8,2,256,256]{3,2,1,0:T(8,128)(2,1)} %get-tuple-element.388), channel_id=1, source_target_pairs={{0,16},{4,20},{8,24},{12,28},{16,0},{20,4},{24,8},{28,12},{1,17},{... | collective-permute-start | bytes 6291464 | tf_op jit(solution)/shard_map/ppermute | solution.py:65
  725.4 50.6 %collective-permute-start.57 = (bf16[16,256,256]{2,1,0:T(8,128)(2,1)}, bf16[16,256,256]{2,1,0:T(8,128)(2,1)}, u32[]{:S(2)}, u32[]{:S(2)}) collective-permute-start(bf16[16,256,256]{2,1,0:T(8,128)(2,1)} %fusion.19), channel_id=1, source_target_pairs={{0,8},{4,12},{8,0},{12,4},{16,24},{20,28},{24,16},{28,20},{1,9},{5... | collective-permute-start | bytes 6291464 | tf_op jit(solution)/shard_map/ppermute | solution.py:65
  731.7 48.8 %collective-permute-start.56 = (bf16[16,256,256]{2,1,0:T(8,128)(2,1)}, bf16[16,256,256]{2,1,0:T(8,128)(2,1)}, u32[]{:S(2)}, u32[]{:S(2)}) collective-permute-start(bf16[16,256,256]{2,1,0:T(8,128)(2,1)} %fusion.20), channel_id=1, source_target_pairs={{0,16},{4,20},{8,24},{12,28},{16,0},{20,4},{24,8},{28,12},{1,17},{... | collective-permute-start | bytes 6291464 | tf_op jit(solution)/shard_map/ppermute | solution.py:65
  750.6 61.7 %collective-permute-start.63 = (bf16[256,2048]{1,0:T(8,128)(2,1)S(1)}, bf16[256,2048]{1,0:T(8,128)(2,1)S(1)}, u32[]{:S(2)}, u32[]{:S(2)}) collective-permute-start(bf16[256,2048]{1,0:T(8,128)(2,1)S(1)} %add_convert_fusion.1), channel_id=1, source_target_pairs={{0,1},{1,2},{2,3},{3,0},{4,5},{5,6},{6,7},{7,4},{8,9},{9,10},{10,1... | collective-permute-start | bytes 3145736 | tf_op jit(solution)/shard_map/ppermute | solution.py:108
  750.6 45.4 %collective-permute-start.59 = (bf16[2,2,256,512]{3,2,1,0:T(8,128)(2,1)}, bf16[2,2,256,512]{3,2,1,0:T(8,128)(2,1)}, u32[]{:S(2)}, u32[]{:S(2)}) collective-permute-start(bf16[2,2,256,512]{3,2,1,0:T(8,128)(2,1)} %get-tuple-element.406), channel_id=1, source_target_pairs={{0,8},{4,12},{8,0},{12,4},{16,24},{20,28},{24,16},{28,20},{1,9},{5... | collective-permute-start | bytes 3145736 | tf_op jit(solution)/shard_map/ppermute | solution.py:65
  (137 other events, 2320.9 us)
Sparse Core Ops, SparseCore 0:
  10.5 82.9 all-gather.1
  520.5 103.2 reduce-scatter.1

commit v5 on v4

--- a/solution.py
+++ b/solution.py
@@ -258,6 +258,25 @@
         ),
         name="projection_back",
     )(jnp.stack(order).astype(jnp.int32), *raws, *gaineds, value_low, scales, inner, weights)
+
+
+def pair_sum(first, second):
+    each = 4
+    block = pl.BlockSpec((each,) + first.shape[1:], lambda i: (i, 0, 0, 0))
+
+    def kernel(a_ref, b_ref, out_ref):
+        add_pair((a_ref, b_ref), (out_ref,))
+
+    return pl.pallas_call(
+        kernel,
+        grid=(first.shape[0] // each,),
+        in_specs=[block, block],
+        out_specs=block,
+        out_shape=jax.ShapeDtypeStruct(first.shape, first.dtype),
+        compiler_params=pltpu.CompilerParams(vmem_limit_bytes=58 << 20),
+        cost_estimate=pl.CostEstimate(flops=first.size, transcendentals=0, bytes_accessed=6 * first.size),
+        name="pair_sum",
+    )(first, second)
 
 
 def pair_split(first, second, axis):
@@ -755,6 +774,7 @@
 def moe_out(wh, down_all):
     experts, tokens, hidden = wh.shape
     width = down_all.shape[1]
+    step, block = 2, min(256, tokens)
 
     def kernel(h_ref, d_ref, out_ref, acc):
         e = pl.program_id(0)
@@ -763,18 +783,22 @@
         def _():
             acc[...] = jnp.zeros_like(acc)
 
-        acc[...] += dot32(h_ref[0], d_ref[0], NT)
-
-        @pl.when(e == experts - 1)
+        down = jnp.concatenate([d_ref[j] for j in range(step)], axis=1)
+        for r in range(tokens // block):
+            rs = pl.ds(r * block, block)
+            rows = jnp.concatenate([h_ref[j, rs, :] for j in range(step)], axis=1)
+            acc[rs, :] += dot32(rows, down, NT)
+
+        @pl.when(e == experts // step - 1)
         def _():
             out_ref[...] = acc[...].astype(jnp.bfloat16)
 
     return pl.pallas_call(
         kernel,
-        grid=(experts,),
+        grid=(experts // step,),
         in_specs=[
-            pl.BlockSpec((1, tokens, hidden), lambda e: (e, 0, 0)),
-            pl.BlockSpec((1, width, hidden), lambda e: (e, 0, 0)),
+            pl.BlockSpec((step, tokens, hidden), lambda e: (e, 0, 0)),
+            pl.BlockSpec((step, width, hidden), lambda e: (e, 0, 0)),
         ],
         out_specs=pl.BlockSpec((tokens, width), lambda e: (0, 0)),
         out_shape=jax.ShapeDtypeStruct((tokens, width), jnp.bfloat16),
@@ -1040,17 +1064,17 @@
             axis_index_groups=same_core("dp"),
         )
 
-    resid_ring = [grad_resid.astype(bf16)]
+    resid_low, gate_moved = together(grad_resid.astype(bf16), gate_moved)
+    resid_ring = [resid_low]
     moved = hop(resid_ring[0])
-    up_keep, up_send, gate_sum = moe_grad_split(
-        normed2_ring, held_until(grad_upre, resid_ring[0]), "dp", 0, here_dp, (gate_keep, gate_moved)
-    )
-    moved, up_keep, up_send, gate_sum, hopped = together(
-        moved, up_keep, up_send, gate_sum, sum_hop()
-    )
+    gate_moved, first_sums = together(gate_moved, first_sums)
+    gate_sum = pair_sum(gate_keep, gate_moved)
+    gate_sum, grad_upre = together(gate_sum, grad_upre)
+    reduced_gate = reduce_rows(gate_sum)
+    up_keep, up_send = moe_grad_split(normed2_ring, grad_upre, "dp", 0, here_dp)
+    moved, up_keep, up_send, hopped = together(moved, up_keep, up_send, sum_hop())
     first_sums = first_sums + hopped
     resid_ring.append(moved)
-    reduced_gate = reduce_rows(gate_sum)
     up_moved = swap(up_send, "dp", 1)
     moved = hop(resid_ring[1])
     moe_part = moe_out(held_until(weighted_hidden, up_keep), down_all)
@@ -1059,11 +1083,12 @@
     resid_ring.append(moved)
     for step in range(3, around):
         resid_ring.append(hop(resid_ring[-1]))
+    moe_moved = hop(moe_part[rows_here : 2 * rows_here])
     down_keep, down_send, *up_split = moe_grad_split(
         final_ring, held_until(weighted_hidden, moe_part), "dp", 0, 0, (up_keep, up_moved), True
     )
-    resid_ring[-1], down_keep, down_send, hopped, *up_split = together(
-        resid_ring[-1], down_keep, down_send, sum_hop(), *up_split
+    resid_ring[-1], down_keep, down_send, reduced_gate, hopped, *up_split = together(
+        resid_ring[-1], down_keep, down_send, reduced_gate, sum_hop(), *up_split
     )
     first_sums = first_sums + hopped
 
@@ -1075,8 +1100,9 @@
     down_moved = swap(down_send, "dp", 1)
     resid_full = in_order(resid_ring, "tensor")
     grad_mixed = dot32(resid_full, output_w).astype(bf16)
-    moe_local = moe_part[rows_here : 2 * rows_here].astype(f32)
-    moe_moved = hop(held_until(moe_local.astype(bf16), resid_full))
+    grad_mixed, moe_moved = together(grad_mixed, moe_moved)
+    moe_local = moe_moved.astype(f32) + moe_part[2 * rows_here : 3 * rows_here].astype(f32)
+    moe_moved = hop(moe_local.astype(bf16))
     query_gained, key_gained, value_low, inner_part, gain_grads, *down_split = attention_backward(
         query_rot,
         key_rot,
@@ -1096,7 +1122,7 @@
     )
     first_sums = first_sums + hopped
     down_cube, down_flying = cube_begin(down_split)
-    moe_local = moe_moved.astype(f32) + moe_part[2 * rows_here : 3 * rows_here].astype(f32)
+    moe_local = moe_moved.astype(f32) + moe_part[3 * rows_here :].astype(f32)
     inner_sums = all_sum(inner_part[:, 0], ("tensor",))
     inner_sums, moe_low = together(inner_sums, moe_local.astype(bf16))
     moe_moved = hop(moe_low)
@@ -1143,8 +1169,6 @@
     up_cube.finish(up_flying)
     reduced_up = jnp.concatenate([piece[:half] for piece in up_cube.pieces])
     reduced_down = jnp.concatenate([piece[half:] for piece in up_cube.pieces])
-    moe_local = moe_moved.astype(f32) + moe_part[3 * rows_here :].astype(f32)
-    moe_moved = hop(moe_local.astype(bf16))
     input_norm_grad, grad_attn_part = norm_back(normed1_grad, gain_attn, unit1, scale1)
     grad_input = grad_resid + input_norm_grad
     gains_full = lax.dynamic_update_slice(

time: 846 us -> 860 us (1.017)
  waiting for transfers between devices: 214 us -> 235 us
    ppermute x27, waiting for transfers between devices: 141 us -> 163 us  [ring_hop(): return lax.ppermute(total, axis, [(i, (i + 1) % n) for i in range(n)])]
    pallas_call x1 -> x2, Pallas kernels: 26 us -> 33.9 us  [the longest x1 24.4 us: moe_out(): pl.pallas_call(kernel, grid=(experts // step,), in_specs=[pl.BlockSpec((s...]
  transfers between devices with their start and end apart: 70 -> 70, of which waited for: 26 -> 34; matrix products, arithmetic and copies ran while one was open for 19% -> 19% of each run, Pallas kernels for 43% -> 41%
where the time goes in v5:
time: 860 us; the launch traced here: 853 us
  Pallas kernels  359 us (42%)
  waiting for transfers between devices  235 us (27%)
  other arithmetic  95.9 us (11%)
  starting transfers between devices  59.3 us (7%)
  local copies, waits for them, and re-layouts  58.3 us (7%)
  matrix products  29.7 us (3%)
  between operations  15.9 us (2%)
    ppermute x27, waiting for transfers between devices, ring_hop(): return lax.ppermute(total, axis, [(i, (i + 1) % n) for i in range(n)])  163 us
    pallas_call x5, Pallas kernels, moe_first(): pl.pallas_call(kernel, grid_spec=pltpu.PrefetchScalarGridSpec(num_scalar_...  144 us
    pallas_call x3, Pallas kernels, moe_grad_split(): pl.pallas_call(kernel, grid_spec=pltpu.PrefetchScalarGridSpec(num_scalar_...  81.6 us
    ppermute x41, waiting for transfers between devices, swap(): return lax.ppermute(value, axis, [(i, i ^ bit) for i in range(n)])  48.1 us
    ppermute x41, starting transfers between devices, swap(): return lax.ppermute(value, axis, [(i, i ^ bit) for i in range(n)])  37.8 us
    pallas_call x1, Pallas kernels, attention_backward(): pl.pallas_call(kernel, grid=(heads,), in_specs=[head, head, head, head, h...  29.3 us
    pallas_call x1, Pallas kernels, moe_out(): pl.pallas_call(kernel, grid=(experts // step,), in_specs=[pl.BlockSpec((s...  24.4 us
    dot_general x9, matrix products, dot32(): lax.dot_general(left, right, dims, preferred_element_type=jnp.float32)  23.9 us
  transfers between devices with their start and end apart: 70, of which 34 were waited for; matrix products, arithmetic and copies ran while one was open for 19% of the time, Pallas kernels for 41%

profile of v5, /device:TPU:0, one launch (start us, length us, event | category | flops | bytes accessed | tf_op | source)
XLA Modules:
  0.0 852.9 jit_solution(9108851799467201996)
XLA Ops:
  48.5 17.9 %collective-permute-done.1.refs_2_ = bf16[256,2048]{1,0:T(8,128)(2,1)} collective-permute-done((bf16[256,2048]{1,0:T(8,128)(2,1)}, bf16[256,2048]{1,0:T(8,128)(2,1)}, u32[]{:S(2)}, u32[]{:S(2)}) %collective-permute-start.1) | collective-permute-done | bytes 1048608 | tf_op jit(solution)/shard_map/ppermute | solution.py:108
  70.5 23.0 %all-gather.2.cloned.1.call-done.refs_3_.refs_1_.w_ref = bf16[4,2048,512]{2,1,0:T(8,128)(2,1)} async-done(((bf16[4,256,512]{2,1,0:T(8,128)(2,1)}), bf16[4,2048,512]{2,1,0:T(8,128)(2,1)}) %all-gather.2.cloned.1.call-update) | async-done | bytes 8388624 | tf_op jit(solution)/shard_map/all_gather | solution.py:854
  95.7 11.1 %projections.2 = (f32[1024,512]{1,0:T(8,128)}, f32[1024,512]{1,0:T(8,128)}, bf16[1024,512]{1,0:T(8,128)(2,1)}, f32[2,8,1024]{2,1,0:T(8,128)}) custom-call(s32[3]{0:T(128)} %pad_add_fusion.1.place_ref, bf16[256,2048]{1,0:T(8,128)(2,1)} %fusion.11.refs_0_, bf16[256,2048]{1,0:T(8,128)(2,1)} %collective-permute-done.refs_1_, ...), custom_call_target="tpu_custom_call" | custom-call | flops 4831838208 | bytes 13369344 | tf_op jit(solution)/shard_map/projections/pallas_call | solution.py:184
  134.4 14.9 %attention_forward.1 = (bf16[1024,512]{1,0:T(8,128)(2,1)}, bf16[1024,512]{1,0:T(8,128)(2,1)}, bf16[1024,512]{1,0:T(8,128)(2,1)}) custom-call(f32[1024,512]{1,0:T(8,128)} %get-tuple-element.233.q_ref.qr_ref.qr, f32[1024,512]{1,0:T(8,128)} %get-tuple-element.234.k_ref.kr_ref.kr, bf16[1024,512]{1,0:T(8,128)(2,1)} %get-tuple-element.235.v_ref, ...), custom_call_target="tpu_custom_call" | custom-call | flops 1610612736 | bytes 8388608 | tf_op jit(solution)/shard_map/attention_forward/pallas_call | solution.py:397
  154.4 22.6 %collective-permute-done.10 = bf16[256,2048]{1,0:T(8,128)(2,1)} collective-permute-done((bf16[256,2048]{1,0:T(8,128)(2,1)}, bf16[256,2048]{1,0:T(8,128)(2,1)}, u32[]{:S(2)}, u32[]{:S(2)}) %collective-permute-start.10) | collective-permute-done | bytes 1048608 | tf_op jit(solution)/shard_map/ppermute | solution.py:108
  181.0 16.9 %collective-permute-done.13 = bf16[24,256,256]{2,1,0:T(8,128)(2,1)} collective-permute-done((bf16[24,256,256]{2,1,0:T(8,128)(2,1)}, bf16[24,256,256]{2,1,0:T(8,128)(2,1)}, u32[]{:S(2)}, u32[]{:S(2)}) %collective-permute-start.13) | collective-permute-done | bytes 3145760 | tf_op jit(solution)/shard_map/ppermute | solution.py:65
  225.0 18.3 %collective-permute-done.14 = bf16[256,2048]{1,0:T(8,128)(2,1)} collective-permute-done((bf16[256,2048]{1,0:T(8,128)(2,1)}, bf16[256,2048]{1,0:T(8,128)(2,1)}, u32[]{:S(2)}, u32[]{:S(2)}) %collective-permute-start.14) | collective-permute-done | bytes 1048608 | tf_op jit(solution)/shard_map/ppermute | solution.py:108
  251.0 27.0 %moe_first.5 = (bf16[256,2048]{1,0:T(8,128)(2,1)}, f32[256,16]{1,0:T(8,128)}, bf16[16,1024,256]{2,1,0:T(8,128)(2,1)}, bf16[16,1024,256]{2,1,0:T(8,128)(2,1)}, bf...) custom-call(s32[3]{0:T(128)} %pad_add_fusion.2.side_ref, ...), custom_call_target="tpu_custom_call" | custom-call | flops 10737418240 | bytes 34603008 | tf_op jit(solution)/shard_map/moe_first/pallas_call | solution.py:650
  278.5 13.5 %collective-permute-done.17.refs_0_.refs_1_ = bf16[256,2048]{1,0:T(8,128)(2,1)S(1)} collective-permute-done((bf16[256,2048]{1,0:T(8,128)(2,1)}, bf16[256,2048]{1,0:T(8,128)(2,1)S(1)}, u32[]{:S(2)}, u32[]{:S(2)}) %collective-permute-start.17) | collective-permute-done | bytes 1048608 | tf_op jit(solution)/shard_map/ppermute | solution.py:108
  300.8 18.5 %moe_first.6 = (bf16[256,2048]{1,0:T(8,128)(2,1)}, f32[256,16]{1,0:T(8,128)}, bf16[16,1024,256]{2,1,0:T(8,128)(2,1)}, bf16[16,1024,256]{2,1,0:T(8,128)(2,1)}, bf16[16,1024,256]{2,1,0:T(8,128)(2,1)}) custom-call(s32[3]{0:T(128)} %pad_add_fusion.2.side_ref, bf16[256,2048]{1,0:T(8,128)(2,1)} %copy-done.15, ...), custom_call_target="tpu_custom_call", output_to_operand_aliasing={{2}: (7, {}), {3}: (8, {}), {4}: (9, {})} | custom-call | flops 10737418240 | bytes 34603008 | tf_op jit(solution)/shard_map/moe_first/pallas_call | solution.py:650
  326.4 37.4 %moe_first.7 = (bf16[256,2048]{1,0:T(8,128)(2,1)}, bf16[256,2048]{1,0:T(8,128)(2,1)}, f32[256,16]{1,0:T(8,128)}, f32[256,16]{1,0:T(8,128)}, bf16[16,1024,256]{2,...) custom-call(s32[3]{0:T(128)} %pad_add_fusion.2.side_ref, ...), custom_call_target="tpu_custom_call", output_to_operand_aliasing={{4}: (58, {}), {5}: (59, {}), {6}: (60, {}), {7}: (61, {}),... | custom-call | flops 21474836480 | bytes 44040192 | tf_op jit(solution)/shard_map/moe_first/pallas_call | solution.py:650
  373.2 30.7 %moe_first.8 = (bf16[256,2048]{1,0:T(8,128)(2,1)}, f32[256,16]{1,0:T(8,128)}, bf16[16,1024,256]{2,1,0:T(8,128)(2,1)}, bf16[16,1024,256]{2,1,0:T(8,128)(2,1)}, bf16[16,1024,256]{2,1,0:T(8,128)(2,1)}) custom-call(s32[3]{0:T(128)} %pad_add_fusion.2.side_ref, ...), custom_call_target="tpu_custom_call", output_to_operand_aliasing={{2}: (7, {}), {3}: (8, {}), {4}: (9, {})} | custom-call | flops 21474836480 | bytes 62914560 | tf_op jit(solution)/shard_map/moe_first/pallas_call | solution.py:650
  414.4 30.6 %moe_first.9 = (bf16[256,2048]{1,0:T(8,128)(2,1)}, f32[256,16]{1,0:T(8,128)}, bf16[16,1024,256]{2,1,0:T(8,128)(2,1)}, bf16[16,1024,256]{2,1,0:T(8,128)(2,1)}, bf16[16,1024,256]{2,1,0:T(8,128)(2,1)}) custom-call(s32[3]{0:T(128)} %pad_add_fusion.2.side_ref, ...), custom_call_target="tpu_custom_call", output_to_operand_aliasing={{2}: (7, {}), {3}: (8, {}), {4}: (9, {})} | custom-call | flops 21474836480 | bytes 62914560 | tf_op jit(solution)/shard_map/moe_first/pallas_call | solution.py:650
  447.9 25.7 %moe_grad_split.3 = (bf16[16,4,256,256]{3,2,1,0:T(8,128)(2,1)}, bf16[16,4,256,256]{3,2,1,0:T(8,128)(2,1)}) custom-call(s32[2]{0:T(128)} %get-tuple-element.506.side_ref, bf16[256,2048]{1,0:T(8,128)(2,1)} %copy-done.11, bf16[256,2048]{1,0:T(8,128)(2,1)} %copy-done.15, bf16[256,2048]{1,0:T(8,128)(2,1)} %collective-permute-done.21.refs_0_.refs_2_, ...), custom_call_target="tpu_custom_call" | custom-call | flops 17179869184 | bytes 29360128 | tf_op jit(solution)/shard_map/moe_grad_split/pallas_call | solution.py:749
  487.2 9.5 %pair_sum.1 = bf16[16,4,256,256]{3,2,1,0:T(8,128)(2,1)} custom-call(bf16[16,4,256,256]{3,2,1,0:T(8,128)(2,1)} %get-tuple-element.339.a_ref, bf16[16,4,256,256]{3,2,1,0:T(8,128)(2,1)} %collective-permute-done.34.b_ref), custom_call_target="tpu_custom_call" | custom-call | flops 4194304 | bytes 25165824 | tf_op jit(solution)/shard_map/pair_sum/pallas_call | solution.py:270
  498.8 25.6 %moe_grad_split.4 = (bf16[16,4,256,256]{3,2,1,0:T(8,128)(2,1)}, bf16[16,4,256,256]{3,2,1,0:T(8,128)(2,1)}) custom-call(s32[2]{0:T(128)} %get-tuple-element.507.side_ref, bf16[256,2048]{1,0:T(8,128)(2,1)} %copy-done.11, bf16[256,2048]{1,0:T(8,128)(2,1)} %copy-done.15, bf16[256,2048]{1,0:T(8,128)(2,1)} %collective-permute-done.21.refs_0_.refs_2_, ...), custom_call_target="tpu_custom_call" | custom-call | flops 17179869184 | bytes 29360128 | tf_op jit(solution)/shard_map/moe_grad_split/pallas_call | solution.py:749
  530.2 24.4 %moe_out.1 = bf16[1024,2048]{1,0:T(8,128)(2,1)} custom-call(bf16[16,1024,256]{2,1,0:T(8,128)(2,1)} %get-tuple-element.356.h_ref.refs_4_, bf16[16,2048,256]{2,1,0:T(8,128)(2,1)} %get-tuple-element.297.refs_5_.d_ref), custom_call_target="tpu_custom_call" | custom-call | flops 17179869184 | bytes 29360128 | tf_op jit(solution)/shard_map/moe_out/pallas_call | solution.py:796
  557.0 30.3 %moe_grad_split.5 = (bf16[16,4,256,256]{3,2,1,0:T(8,128)(2,1)}, bf16[16,4,256,256]{3,2,1,0:T(8,128)(2,1)}, bf16[8,2,256,256]{3,2,1,0:T(8,128)(2,1)}, bf16[8,2,25...) custom-call(s32[2]{0:T(128)} %broadcast_4_side_ref.2.side_ref, ...), custom_call_target="tpu_custom_call" | custom-call | flops 17179869184 | bytes 29360128 | tf_op jit(solution)/shard_map/moe_grad_split/pallas_call | solution.py:749
  598.2 19.6 %collective-permute-done.42 = bf16[256,2048]{1,0:T(8,128)(2,1)S(1)} collective-permute-done((bf16[256,2048]{1,0:T(8,128)(2,1)S(1)}, bf16[256,2048]{1,0:T(8,128)(2,1)S(1)}, u32[]{:S(2)}, u32[]{:S(2)}) %collective-permute-start.42) | collective-permute-done | bytes 1048608 | tf_op jit(solution)/shard_map/ppermute | solution.py:108
  624.3 29.3 %attention_backward.1 = (f32[1024,512]{1,0:T(8,128)}, f32[1024,512]{1,0:T(8,128)}, bf16[1024,512]{1,0:T(8,128)(2,1)}, f32[2,8,1024]{2,1,0:T(8,128)}, f32[2,512]{...) custom-call(bf16[1024,512]{1,0:T(8,128)(2,1)} %get-tuple-element.245, ...), custom_call_target="tpu_custom_call" | custom-call | flops 4026531840 | bytes 13631488 | tf_op jit(solution)/shard_map/attention_backward/pallas_call | solution.py:492
  671.3 16.1 %collective-permute-done.48 = bf16[256,2048]{1,0:T(8,128)(2,1)S(1)} collective-permute-done((bf16[256,2048]{1,0:T(8,128)(2,1)}, bf16[256,2048]{1,0:T(8,128)(2,1)S(1)}, u32[]{:S(2)}, u32[]{:S(2)}) %collective-permute-start.48) | collective-permute-done | bytes 1048608 | tf_op jit(solution)/shard_map/ppermute | solution.py:108
  687.4 13.6 %projection_back.1 = (bf16[1024,512]{1,0:T(8,128)(2,1)}, bf16[1024,512]{1,0:T(8,128)(2,1)}, bf16[4,256,2048]{2,1,0:T(8,128)(2,1)}) custom-call(s32[4]{0:T(128)} %pad_add_fusion.5.place_ref, f32[1024,512]{1,0:T(8,128)} %get-tuple-element.233.q_ref.qr_ref.qr, f32[1024,512]{1,0:T(8,128)} %get-tuple-element.234.k_ref.kr_ref.kr, ...), custom_call_target="tpu_custom_call" | custom-call | flops 6442450944 | bytes 22020096 | tf_op jit(solution)/shard_map/projection_back/pallas_call | solution.py:237
  704.1 18.7 %projection_grads.1 = (bf16[4,4,256,512]{3,2,1,0:T(8,128)(2,1)}, bf16[4,4,256,512]{3,2,1,0:T(8,128)(2,1)}) custom-call(s32[5]{0:T(128)} %stack.97.place_ref, bf16[256,2048]{1,0:T(8,128)(2,1)} %fusion.11.refs_0_, bf16[256,2048]{1,0:T(8,128)(2,1)} %collective-permute-done.refs_1_, bf16[256,2048]{1,0:T(8,128)(2,1)} %collective-permute-done.1.refs_2_, ...), custom_call_target="tpu_custom_call" | custom-call | flops 8589934592 | bytes 20971520 | tf_op jit(solution)/shard_map/projection_grads/pallas_call | solution.py:337
  769.6 21.7 %collective-permute-done.56 = bf16[256,2048]{1,0:T(8,128)(2,1)S(1)} collective-permute-done((bf16[256,2048]{1,0:T(8,128)(2,1)S(1)}, bf16[256,2048]{1,0:T(8,128)(2,1)S(1)}, u32[]{:S(2)}, u32[]{:S(2)}) %collective-permute-start.56) | collective-permute-done | bytes 1048608 | tf_op jit(solution)/shard_map/ppermute | solution.py:108
  (498 shorter events, 320.3 us)
Async XLA Ops:
  7.2 86.3 %all-gather.2.cloned.1.call-start = ((), (), s32[]{:S(2)}) async-start(), calls=%async_computation.1 | async-start | bytes 9437184 | tf_op jit(solution)/shard_map/all_gather | solution.py:854
  9.7 577.8 %reduce-scatter.2.cloned.1.call-start = ((), (), s32[]{:S(2)}) async-start(), calls=%async_computation.2 | async-start | bytes 10485760 | tf_op jit(solution)/shard_map/reduce_scatter | solution.py:1059
  21.7 85.1 %collective-permute-start.4 = (bf16[12,256,256]{2,1,0:T(8,128)(2,1)}, bf16[12,256,256]{2,1,0:T(8,128)(2,1)S(1)}, u32[]{:S(2)}, u32[]{:S(2)}) collective-permute-start(bf16[12,256,256]{2,1,0:T(8,128)(2,1)} %pad_maximum_fusion.9), channel_id=1, source_target_pairs={{0,16},{4,20},{8,24},{12,28},{16,0},{20,4},{24,8},{28,12},{1,17},{... | collective-permute-start | bytes 4718600 | tf_op jit(solution)/shard_map/ppermute | solution.py:65
  24.6 82.3 %collective-permute-start.3 = (bf16[12,256,256]{2,1,0:T(8,128)(2,1)}, bf16[12,256,256]{2,1,0:T(8,128)(2,1)S(1)}, u32[]{:S(2)}, u32[]{:S(2)}) collective-permute-start(bf16[12,256,256]{2,1,0:T(8,128)(2,1)} %pad_maximum_fusion.8), channel_id=1, source_target_pairs={{0,8},{4,12},{8,0},{12,4},{16,24},{20,28},{24,16},{28,20},{1,9},{5... | collective-permute-start | bytes 4718600 | tf_op jit(solution)/shard_map/ppermute | solution.py:65
  93.5 55.8 %collective-permute-start.8 = (bf16[12,256,256]{2,1,0:T(8,128)(2,1)}, bf16[12,256,256]{2,1,0:T(8,128)(2,1)}, u32[]{:S(2)}, u32[]{:S(2)}) collective-permute-start(bf16[12,256,256]{2,1,0:T(8,128)(2,1)} %get-tuple-element.239), channel_id=1, source_target_pairs={{0,8},{4,12},{8,0},{12,4},{16,24},{20,28},{24,16},{28,20},{1,9},{5... | collective-permute-start | bytes 4718600 | tf_op jit(solution)/shard_map/ppermute | solution.py:65
  95.0 54.3 %collective-permute-start.9 = (bf16[12,256,256]{2,1,0:T(8,128)(2,1)}, bf16[12,256,256]{2,1,0:T(8,128)(2,1)}, u32[]{:S(2)}, u32[]{:S(2)}) collective-permute-start(bf16[12,256,256]{2,1,0:T(8,128)(2,1)} %get-tuple-element.240), channel_id=1, source_target_pairs={{0,16},{4,20},{8,24},{12,28},{16,0},{20,4},{24,8},{28,12},{1,17},{... | collective-permute-start | bytes 4718600 | tf_op jit(solution)/shard_map/ppermute | solution.py:65
  126.1 71.7 %collective-permute-start.13 = (bf16[24,256,256]{2,1,0:T(8,128)(2,1)}, bf16[24,256,256]{2,1,0:T(8,128)(2,1)}, u32[]{:S(2)}, u32[]{:S(2)}) collective-permute-start(bf16[24,256,256]{2,1,0:T(8,128)(2,1)} %pad_maximum_fusion.5), channel_id=1, source_target_pairs={{0,8},{4,12},{8,0},{12,4},{16,24},{20,28},{24,16},{28,20},{1,9},{5... | collective-permute-start | bytes 9437192 | tf_op jit(solution)/shard_map/ppermute | solution.py:65
  128.5 70.5 %collective-permute-start.12 = (bf16[24,256,256]{2,1,0:T(8,128)(2,1)}, bf16[24,256,256]{2,1,0:T(8,128)(2,1)}, u32[]{:S(2)}, u32[]{:S(2)}) collective-permute-start(bf16[24,256,256]{2,1,0:T(8,128)(2,1)} %pad_maximum_fusion.4), channel_id=1, source_target_pairs={{0,16},{4,20},{8,24},{12,28},{16,0},{20,4},{24,8},{28,12},{1,17},{... | collective-permute-start | bytes 9437192 | tf_op jit(solution)/shard_map/ppermute | solution.py:65
  206.5 43.1 %collective-permute-start.16 = (bf16[48,256,256]{2,1,0:T(8,128)(2,1)}, bf16[48,256,256]{2,1,0:T(8,128)(2,1)}, u32[]{:S(2)}, u32[]{:S(2)}) collective-permute-start(bf16[48,256,256]{2,1,0:T(8,128)(2,1)} %constant_dynamic-update-slice_fusion.5.refs_11_.refs_13_.refs_15_.refs_17_.refs_27_.refs_29_.refs_31_.refs_, ...), channel_id=1, source_target_pairs={{0,4},{4,0},{8,12},{12,8},{16,20},{20,16},{24,28},{28,24},{1,5},{5... | collective-permute-start | bytes 18874376 | tf_op jit(solution)/shard_map/ppermute | solution.py:65
  220.4 71.6 %collective-permute-start.19 = (bf16[24,256,256]{2,1,0:T(8,128)(2,1)}, bf16[24,256,256]{2,1,0:T(8,128)(2,1)}, u32[]{:S(2)}, u32[]{:S(2)}) collective-permute-start(bf16[24,256,256]{2,1,0:T(8,128)(2,1)} %constant_dynamic-update-slice_fusion.10.refs_5_.refs_7_.refs_21_.refs_23_.refs_37_.refs_39_), channel_id=1, source_target_pairs={{0,16},{4,20},{8,24},{12,28},{16,0},{20,4},{24,8},{28,12},{1,17},{... | collective-permute-start | bytes 9437192 | tf_op jit(solution)/shard_map/ppermute | solution.py:65
  222.6 69.9 %collective-permute-start.20 = (bf16[24,256,256]{2,1,0:T(8,128)(2,1)S(1)}, bf16[24,256,256]{2,1,0:T(8,128)(2,1)}, u32[]{:S(2)}, u32[]{:S(2)}) collective-permute-start(bf16[24,256,256]{2,1,0:T(8,128)(2,1)S(1)} %constant_dynamic-update-slice_fusion.12.refs_13_.refs_17_.refs_29_.refs_33_.refs_45_.refs_49_), channel_id=1, source_target_pairs={{0,8},{4,12},{8,0},{12,4},{16,24},{20,28},{24,16},{28,20},{1,9},{5... | collective-permute-start | bytes 9437192 | tf_op jit(solution)/shard_map/ppermute | solution.py:65
  249.6 42.4 %collective-permute-start.17 = (bf16[256,2048]{1,0:T(8,128)(2,1)}, bf16[256,2048]{1,0:T(8,128)(2,1)S(1)}, u32[]{:S(2)}, u32[]{:S(2)}) collective-permute-start(bf16[256,2048]{1,0:T(8,128)(2,1)} %copy-done.11), channel_id=1, source_target_pairs={{0,1},{1,2},{2,3},{3,0},{4,5},{5,6},{6,7},{7,4},{8,9},{9,10},{10,1... | collective-permute-start | bytes 3145736 | tf_op jit(solution)/shard_map/ppermute | solution.py:108
  251.0 74.2 %collective-permute-start.22 = (bf16[24,256,256]{2,1,0:T(8,128)(2,1)}, bf16[24,256,256]{2,1,0:T(8,128)(2,1)}, u32[]{:S(2)}, u32[]{:S(2)}) collective-permute-start(bf16[24,256,256]{2,1,0:T(8,128)(2,1)} %constant_dynamic-update-slice_fusion.10.refs_5_.refs_7_.refs_21_.refs_23_.refs_37_.refs_39_), channel_id=1, source_target_pairs={{0,4},{4,0},{8,12},{12,8},{16,20},{20,16},{24,28},{28,24},{1,5},{5... | collective-permute-start | bytes 9437192 | tf_op jit(solution)/shard_map/ppermute | solution.py:65
  278.0 48.4 %collective-permute-start.24 = (bf16[24,256,256]{2,1,0:T(8,128)(2,1)S(1)}, bf16[24,256,256]{2,1,0:T(8,128)(2,1)}, u32[]{:S(2)}, u32[]{:S(2)}) collective-permute-start(bf16[24,256,256]{2,1,0:T(8,128)(2,1)S(1)} %constant_dynamic-update-slice_fusion.12.refs_13_.refs_17_.refs_29_.refs_33_.refs_45_.refs_49_), channel_id=1, source_target_pairs={{0,4},{4,0},{8,12},{12,8},{16,20},{20,16},{24,28},{28,24},{1,5},{5... | collective-permute-start | bytes 9437192 | tf_op jit(solution)/shard_map/ppermute | solution.py:65
  322.4 41.4 %collective-permute-start.26 = (bf16[256,2048]{1,0:T(8,128)(2,1)}, bf16[256,2048]{1,0:T(8,128)(2,1)}, u32[]{:S(2)}, u32[]{:S(2)}) collective-permute-start(bf16[256,2048]{1,0:T(8,128)(2,1)} %collective-permute-done.21.refs_0_.refs_2_), channel_id=1, source_target_pairs={{0,1},{1,2},{2,3},{3,0},{4,5},{5,6},{6,7},{7,4},{8,9},{9,10},{10,1... | collective-permute-start | bytes 3145736 | tf_op jit(solution)/shard_map/ppermute | solution.py:108
  325.1 45.9 %collective-permute-start.27 = (bf16[256,2048]{1,0:T(8,128)(2,1)}, bf16[256,2048]{1,0:T(8,128)(2,1)S(1)}, u32[]{:S(2)}, u32[]{:S(2)}) collective-permute-start(bf16[256,2048]{1,0:T(8,128)(2,1)} %collective-permute-done.18.refs_1_.refs_2_), channel_id=1, source_target_pairs={{0,1},{1,2},{2,3},{3,0},{4,5},{5,6},{6,7},{7,4},{8,9},{9,10},{10,1... | collective-permute-start | bytes 3145736 | tf_op jit(solution)/shard_map/ppermute | solution.py:108
  621.1 48.8 %collective-permute-start.49 = (bf16[8,2,256,256]{3,2,0,1:T(8,128)(2,1)}, bf16[8,2,256,256]{3,2,0,1:T(8,128)(2,1)}, u32[]{:S(2)}, u32[]{:S(2)}) collective-permute-start(bf16[8,2,256,256]{3,2,0,1:T(8,128)(2,1)} %copy.167), channel_id=1, source_target_pairs={{0,8},{4,12},{8,0},{12,4},{16,24},{20,28},{24,16},{28,20},{1,9},{5... | collective-permute-start | bytes 6291464 | tf_op jit(solution)/shard_map/ppermute | solution.py:65
  622.4 48.9 %collective-permute-start.50 = (bf16[8,2,256,256]{3,2,1,0:T(8,128)(2,1)}, bf16[8,2,256,256]{3,2,1,0:T(8,128)(2,1)}, u32[]{:S(2)}, u32[]{:S(2)}) collective-permute-start(bf16[8,2,256,256]{3,2,1,0:T(8,128)(2,1)} %get-tuple-element.389), channel_id=1, source_target_pairs={{0,16},{4,20},{8,24},{12,28},{16,0},{20,4},{24,8},{28,12},{1,17},{... | collective-permute-start | bytes 6291464 | tf_op jit(solution)/shard_map/ppermute | solution.py:65
  666.0 56.8 %collective-permute-start.52 = (bf16[8,2,256,256]{3,2,0,1:T(8,128)(2,1)S(1)}, bf16[8,2,256,256]{3,2,0,1:T(8,128)(2,1)}, u32[]{:S(2)}, u32[]{:S(2)}) collective-permute-start(bf16[8,2,256,256]{3,2,0,1:T(8,128)(2,1)S(1)} %copy.168), channel_id=1, source_target_pairs={{0,8},{4,12},{8,0},{12,4},{16,24},{20,28},{24,16},{28,20},{1,9},{5... | collective-permute-start | bytes 6291464 | tf_op jit(solution)/shard_map/ppermute | solution.py:65
  667.5 55.4 %collective-permute-start.53 = (bf16[8,2,256,256]{3,2,1,0:T(8,128)(2,1)}, bf16[8,2,256,256]{3,2,1,0:T(8,128)(2,1)}, u32[]{:S(2)}, u32[]{:S(2)}) collective-permute-start(bf16[8,2,256,256]{3,2,1,0:T(8,128)(2,1)} %get-tuple-element.398), channel_id=1, source_target_pairs={{0,16},{4,20},{8,24},{12,28},{16,0},{20,4},{24,8},{28,12},{1,17},{... | collective-permute-start | bytes 6291464 | tf_op jit(solution)/shard_map/ppermute | solution.py:65
  744.4 48.8 %collective-permute-start.58 = (bf16[16,256,256]{2,1,0:T(8,128)(2,1)}, bf16[16,256,256]{2,1,0:T(8,128)(2,1)}, u32[]{:S(2)}, u32[]{:S(2)}) collective-permute-start(bf16[16,256,256]{2,1,0:T(8,128)(2,1)} %fusion.19), channel_id=1, source_target_pairs={{0,8},{4,12},{8,0},{12,4},{16,24},{20,28},{24,16},{28,20},{1,9},{5... | collective-permute-start | bytes 6291464 | tf_op jit(solution)/shard_map/ppermute | solution.py:65
  750.6 48.8 %collective-permute-start.57 = (bf16[16,256,256]{2,1,0:T(8,128)(2,1)}, bf16[16,256,256]{2,1,0:T(8,128)(2,1)}, u32[]{:S(2)}, u32[]{:S(2)}) collective-permute-start(bf16[16,256,256]{2,1,0:T(8,128)(2,1)} %fusion.20), channel_id=1, source_target_pairs={{0,16},{4,20},{8,24},{12,28},{16,0},{20,4},{24,8},{28,12},{1,17},{... | collective-permute-start | bytes 6291464 | tf_op jit(solution)/shard_map/ppermute | solution.py:65
  767.5 47.5 %collective-permute-start.60 = (bf16[2,2,256,512]{3,2,1,0:T(8,128)(2,1)}, bf16[2,2,256,512]{3,2,1,0:T(8,128)(2,1)S(1)}, u32[]{:S(2)}, u32[]{:S(2)}) collective-permute-start(bf16[2,2,256,512]{3,2,1,0:T(8,128)(2,1)} %get-tuple-element.416), channel_id=1, source_target_pairs={{0,8},{4,12},{8,0},{12,4},{16,24},{20,28},{24,16},{28,20},{1,9},{5... | collective-permute-start | bytes 3145736 | tf_op jit(solution)/shard_map/ppermute | solution.py:65
  768.9 51.9 %collective-permute-start.61 = (bf16[2,2,256,512]{3,2,1,0:T(8,128)(2,1)S(1)}, bf16[2,2,256,512]{3,2,1,0:T(8,128)(2,1)S(1)}, u32[]{:S(2)}, u32[]{:S(2)}) collective-permute-start(bf16[2,2,256,512]{3,2,1,0:T(8,128)(2,1)S(1)} %copy-done.90), channel_id=1, source_target_pairs={{0,16},{4,20},{8,24},{12,28},{16,0},{20,4},{24,8},{28,12},{1,17},{... | collective-permute-start | bytes 3145736 | tf_op jit(solution)/shard_map/ppermute | solution.py:65
  (137 other events, 2295.6 us)
Sparse Core Ops, SparseCore 0:
  10.5 82.9 all-gather.1
  496.9 90.6 reduce-scatter.1
